TPU v7x, 256 devices: a whole 4x4x8 slice. The times are simulated.
256 devices in a mesh: seq: 16 (over z, core), head: 16 (over x, y).
Axes of the slice: x: 4, y: 4, z: 8, core: 2. Of those that a mesh axis runs over, the one named last changes fastest.
Arguments:
- features: bfloat16 [65536, 8192], P(('seq', 'head')), may hold values from -6 to 6
- step_size: float32 [65536, 128], P(('seq', 'head')), may hold values from 0.01 to 0.08
- log_decay: float32 [65536, 128], P(('seq', 'head')), may hold values from -0.6 to 0
- inject: bfloat16 [65536, 1024], P(('seq', 'head')), may hold values from -1.5 to 1.5
- readout: bfloat16 [65536, 1024], P(('seq', 'head')), may hold values from -1.5 to 1.5
- skip_gain: float32 [128], replicated, may hold values from 0.5 to 1.5
Outputs:
- mixer_out: bfloat16 [65536, 8192], P(('seq', 'head'))
All inputs are finite; a program needn't handle non-finite values.
Results may differ from a plain program's by a relative error of at most 0.02.
Values may be sent and summed in bfloat16 or wider, within the bound.
No kernel may reach another device: no remote copies, remote signals or barrier semaphores. Data moves between devices by JAX's collectives and lax.ppermute only.
A program may use at most 128 MiB of HBM per device.

v0:
```python
import jax
import jax.numpy as jnp
from jax import lax
from jax.sharding import PartitionSpec as P

HEAD_DIM = 64
STATE = 128
GROUPS = 8
SPAN = 512


def entering_2(x, axis, join, neutral):
    place = lax.axis_index(axis)
    gathered = jax.tree.map(
        lambda a, kind: lax.all_gather(a.astype(kind), axis), x, (jnp.bfloat16, jnp.bfloat16)
    )
    state = jax.tree.map(lambda a, e: jnp.zeros_like(a) + jnp.asarray(e, a.dtype), x, neutral)

    def one(step, state):
        return join(
            state,
            jax.tree.map(
                lambda a, own: lax.dynamic_index_in_dim(a, step, 0, False).astype(own.dtype),
                gathered,
                x,
            ),
        )

    return lax.fori_loop(0, place, one, state)


def shards(features, step_size, log_decay, inject, readout, skip_gain):
    head_ways = lax.axis_size("head")
    head_index = lax.axis_index("head")
    heads_all = step_size.shape[1]
    local_heads = heads_all // head_ways
    group_heads = heads_all // GROUPS
    local_groups = max(1, local_heads // group_heads)
    per_group = local_heads // local_groups
    regrouped = lax.all_to_all(features, "head", split_axis=1, concat_axis=0, tiled=True)
    steps_local, decay_local = (
        lax.all_to_all(
            step_size.astype(jnp.bfloat16), "head", split_axis=1, concat_axis=0, tiled=True
        ).astype(step_size.dtype),
        lax.all_to_all(
            log_decay.astype(jnp.bfloat16), "head", split_axis=1, concat_axis=0, tiled=True
        ).astype(log_decay.dtype),
    )
    inject_all, readout_all = (
        lax.all_gather(inject, "head", axis=0, tiled=True),
        lax.all_gather(readout, "head", axis=0, tiled=True),
    )
    first_col = head_index * local_heads // group_heads * STATE
    inject_mine = lax.dynamic_slice_in_dim(inject_all, first_col, local_groups * STATE, 1)
    readout_mine = lax.dynamic_slice_in_dim(readout_all, first_col, local_groups * STATE, 1)
    seq_rows = regrouped.shape[0]
    spans = seq_rows // SPAN
    drive = (
        regrouped.reshape(seq_rows, local_heads, HEAD_DIM).astype(jnp.float32)
        * steps_local[:, :, None]
    ).astype(jnp.bfloat16)
    drive_q = drive.reshape(spans, SPAN, local_groups, per_group, HEAD_DIM)
    cum_q = jnp.cumsum(decay_local.reshape(spans, SPAN, local_heads), axis=1)
    inject_q = inject_mine.reshape(spans, SPAN, local_groups, STATE)
    readout_q = readout_mine.reshape(spans, SPAN, local_groups, STATE)
    row_ids = lax.broadcasted_iota(jnp.int32, (SPAN, SPAN), 0)
    col_ids = lax.broadcasted_iota(jnp.int32, (SPAN, SPAN), 1)
    lower_mask = row_ids >= col_ids

    def span_terms(pieces):
        read_c, inject_c, drive_c, cum_c = pieces
        intersection = jnp.einsum(
            "ign,jgn->gij", read_c, inject_c, preferred_element_type=jnp.float32
        )
        cum_heads = cum_c.T
        log_gap = cum_heads[:, :, None] - cum_heads[:, None, :]
        decays = jnp.where(lower_mask, jnp.exp(jnp.where(lower_mask, log_gap, 0.0)), 0.0)
        weights = (
            decays.reshape(local_groups, per_group, SPAN, SPAN) * intersection[:, None]
        ).astype(jnp.bfloat16)
        inner_out = jnp.einsum(
            "ghij,jghp->ighp", weights, drive_c, preferred_element_type=jnp.float32
        )
        tail_decay = jnp.exp(cum_heads[:, -1:] - cum_heads)
        scaled = (
            drive_c.astype(jnp.float32)
            * tail_decay.T.reshape(SPAN, local_groups, per_group)[..., None]
        ).astype(jnp.bfloat16)
        summary = jnp.einsum("jghp,jgn->ghpn", scaled, inject_c, preferred_element_type=jnp.float32)
        return (inner_out, summary.reshape(local_heads, HEAD_DIM, STATE))

    inner_out, summary = lax.map(span_terms, (readout_q, inject_q, drive_q, cum_q))
    totals = cum_q[:, -1, :]

    def advance(carried, pieces):
        block_total, summary_c = pieces
        updated = carried * jnp.exp(block_total)[:, None, None] + summary_c
        return (updated, carried)

    zero_state = jnp.zeros((local_heads, HEAD_DIM, STATE), jnp.float32)
    end_state, entering = lax.scan(advance, zero_state, (totals, summary))
    dev_total = jnp.sum(totals, axis=0)

    def combine(earlier, following):
        return (
            earlier[0] + following[0],
            earlier[1] * jnp.exp(following[0])[:, None, None] + following[1],
        )

    identity = (jnp.zeros((local_heads,), jnp.float32), zero_state)
    scanned = entering_2((dev_total, end_state), "seq", combine, identity)
    incoming = scanned[1]
    before = jnp.cumsum(totals, axis=0) - totals
    states = entering + jnp.exp(before)[:, :, None, None] * incoming[None]
    held = states.astype(jnp.bfloat16).reshape(spans, local_groups, per_group, HEAD_DIM, STATE)
    outer_out = jnp.einsum("cign,cghpn->cighp", readout_q, held, preferred_element_type=jnp.float32)
    outer_out = outer_out * jnp.exp(cum_q).reshape(spans, SPAN, local_groups, per_group)[..., None]
    skip_local = lax.dynamic_slice_in_dim(skip_gain, head_index * local_heads, local_heads)
    plain = regrouped.reshape(spans, SPAN, local_groups, per_group, HEAD_DIM).astype(jnp.float32)
    total_out = (
        inner_out + outer_out + skip_local.reshape(local_groups, per_group)[:, :, None] * plain
    )
    mixed_rows = total_out.astype(jnp.bfloat16).reshape(seq_rows, local_heads * HEAD_DIM)
    return lax.all_to_all(mixed_rows, "head", split_axis=0, concat_axis=1, tiled=True)


def solution(mesh):
    placed = (
        P(("seq", "head"), None),
        P(("seq", "head"), None),
        P(("seq", "head"), None),
        P(("seq", "head"), None),
        P(("seq", "head"), None),
        P(),
    )
    return jax.shard_map(
        shards, mesh=mesh, in_specs=placed, out_specs=P(("seq", "head"), None), check_vma=False
    )
```

profile of v0, /device:TPU:225, one launch (start us, length us, event | category | flops | bytes accessed | tf_op | source)
XLA Modules:
  0.0 422.0 jit_solution(15952692852257553255)
XLA Ops:
  9.6 6.8 %all-to-all-start.2 = ((bf16[256,16,8]{0,2,1:T(8,128)(2,1)}), bf16[256,16,8]{0,2,1:T(8,128)(2,1)S(1)}, u32[]{:S(2)}, u32[]{:S(2)}) async-start(bf16[256,16,8]{0,2,1:T(8,128)(2,1)} %bitcast.102), calls=%async_computation.2 | async-start | bytes 131072 | tf_op jit(solution)/shard_map/all_to_all | solution.py:45
  18.0 4.9 %all-to-all-done.2 = bf16[256,16,8]{0,2,1:T(8,128)(2,1)S(1)} async-done(((bf16[256,16,8]{0,2,1:T(8,128)(2,1)}), bf16[256,16,8]{0,2,1:T(8,128)(2,1)S(1)}, u32[]{:S(2)}, u32[]{:S(2)}) %all-to-all-start.2) | async-done | bytes 65568 | tf_op jit(solution)/shard_map/all_to_all | solution.py:45
  26.4 6.4 %copy.78 = bf16[256,8192]{0,1:T(8,128)(2,1)} copy(bf16[256,8192]{1,0:T(8,128)(2,1)} %param.12) | data formatting | bytes 8388608 | tf_op args[0]
  33.2 6.3 %all-to-all-start = ((bf16[256,16,512]{0,2,1:T(8,128)(2,1)}), bf16[256,16,512]{0,2,1:T(8,128)(2,1)}, u32[]{:S(2)}, u32[]{:S(2)}) async-start(bf16[256,16,512]{0,2,1:T(8,128)(2,1)} %bitcast.134), calls=%async_computation | async-start | bytes 8388608 | tf_op jit(solution)/shard_map/all_to_all | solution.py:40
  39.6 9.0 %reduce-window.6 = f32[8,8,4,128]{3,1,2,0:T(8,128)S(1)} reduce-window(f32[8,8,4,128]{3,1,2,0:T(8,128)S(1)} %bitcast.139, f32[]{:T(128)} %constant.75.clone.1), window={size=1x1x1x128 pad=0_0x0_0x0_0x127_0}, to_apply=%region_0.1 | reduce-window | flops 4161536 | bytes 262148 | tf_op jit(solution)/shard_map/reduce-window
  49.6 65.2 %all-to-all-done = bf16[256,16,512]{0,2,1:T(8,128)(2,1)} async-done(((bf16[256,16,512]{0,2,1:T(8,128)(2,1)}), bf16[256,16,512]{0,2,1:T(8,128)(2,1)}, u32[]{:S(2)}, u32[]{:S(2)}) %all-to-all-start) | async-done | bytes 4194336 | tf_op jit(solution)/shard_map/all_to_all | solution.py:40
  117.9 8.1 %copy.79 = f32[16,256,512]{1,0,2:T(8,128)} copy(f32[16,256,512]{1,2,0:T(8,128)S(1)} %convert_bitcast_fusion) | data formatting | bytes 16777216 | tf_op jit(solution)/shard_map/convert_element_type | solution.py:59
  125.9 9.8 %reshape.178 = f32[8,512,1,8,64]{1,0,4,3,2:T(8,128)} reshape(f32[16,256,512]{1,0,2:T(8,128)} %copy.79) | data formatting | bytes 16777216 | tf_op jit(solution)/shard_map/convert_element_type | solution.py:59
  135.7 5.1 %multiply_convert_fusion.7 = bf16[8,512,1,8,64]{1,0,4,3,2:T(8,128)(2,1)S(1)} fusion(f32[8,512,1,8,64]{1,0,4,3,2:T(8,128)} %reshape.178, f32[8,512,8]{1,0,2:T(8,128)S(1)} %copy.81), kind=kLoop, calls=%fused_computation.43 | loop fusion | flops 4194304 | bytes 12713984 | tf_op jit(solution)/shard_map/convert_element_type | solution.py:61
  145.6 54.1 %all-gather.8.cloned.1.call-done = bf16[4096,1024]{1,0:T(8,128)(2,1)} async-done(((bf16[256,1024]{1,0:T(8,128)(2,1)}), bf16[4096,1024]{1,0:T(8,128)(2,1)}) %all-gather.8.cloned.1.call-update) | async-done | bytes 8388624 | tf_op jit(solution)/shard_map/all_gather | solution.py:50
  202.6 59.0 %while.40 = (s32[]{:T(128)}, f32[8,512,1,8,64]{1,4,3,2,0:T(8,128)}, f32[8,8,64,128]{3,2,1,0:T(8,128)}, bf16[8,512,1,8,64]{1,4,3,2,0:T(8,128)(2,1)}, f32[8,512,8]...) while((s32[]{:T(128)}, f32[8,512,1,8,64]{1,4,3,2,0:T(8,128)}, ...), condition=%wide.region_3.4_spmd.clone.clone, body=%wide.region_2.3_spmd.clone.clone.sunk | while | flops 414191616 | bytes 5492413 | solution.py:92
  203.0 4.7 %fusion.52 = f32[8,512,1,8,64]{1,4,3,2,0:T(8,128)} fusion(f32[8,512,1,8,64]{1,4,3,2,0:T(8,128)} %get-tuple-element.377, s32[]{:T(128)} %get-tuple-element.376, f32[512,512]{1,0:T(8,128)S(1)} %fusion.51, f32[8,512]{1,0:T(8,128)S(1)} %dynamic-slice_bitcast_fusion.2, pred[512,512]{1,0:T(8,128)(4,1)S(1)} %iota_compare_fusion.2, ...), kind=kOutput, calls=%fused_computation.12.clone.1 | convolution fusion | flops 278921216 | bytes 2917376 | tf_op jit(solution)/shard_map/while/body/eval_jaxpr/ghij,jghp->ighp/dot_general | solution.py:81
  217.7 4.7 %fusion.52 = f32[8,512,1,8,64]{1,4,3,2,0:T(8,128)} fusion(f32[8,512,1,8,64]{1,4,3,2,0:T(8,128)} %get-tuple-element.377, s32[]{:T(128)} %get-tuple-element.376, f32[512,512]{1,0:T(8,128)S(1)} %fusion.51, f32[8,512]{1,0:T(8,128)S(1)} %dynamic-slice_bitcast_fusion.2, pred[512,512]{1,0:T(8,128)(4,1)S(1)} %iota_compare_fusion.2, ...), kind=kOutput, calls=%fused_computation.12.clone.1 | convolution fusion | flops 278921216 | bytes 2917376 | tf_op jit(solution)/shard_map/while/body/eval_jaxpr/ghij,jghp->ighp/dot_general | solution.py:81
  225.1 4.7 %fusion.52 = f32[8,512,1,8,64]{1,4,3,2,0:T(8,128)} fusion(f32[8,512,1,8,64]{1,4,3,2,0:T(8,128)} %get-tuple-element.377, s32[]{:T(128)} %get-tuple-element.376, f32[512,512]{1,0:T(8,128)S(1)} %fusion.51, f32[8,512]{1,0:T(8,128)S(1)} %dynamic-slice_bitcast_fusion.2, pred[512,512]{1,0:T(8,128)(4,1)S(1)} %iota_compare_fusion.2, ...), kind=kOutput, calls=%fused_computation.12.clone.1 | convolution fusion | flops 278921216 | bytes 2917376 | tf_op jit(solution)/shard_map/while/body/eval_jaxpr/ghij,jghp->ighp/dot_general | solution.py:81
  232.5 4.7 %fusion.52 = f32[8,512,1,8,64]{1,4,3,2,0:T(8,128)} fusion(f32[8,512,1,8,64]{1,4,3,2,0:T(8,128)} %get-tuple-element.377, s32[]{:T(128)} %get-tuple-element.376, f32[512,512]{1,0:T(8,128)S(1)} %fusion.51, f32[8,512]{1,0:T(8,128)S(1)} %dynamic-slice_bitcast_fusion.2, pred[512,512]{1,0:T(8,128)(4,1)S(1)} %iota_compare_fusion.2, ...), kind=kOutput, calls=%fused_computation.12.clone.1 | convolution fusion | flops 278921216 | bytes 2917376 | tf_op jit(solution)/shard_map/while/body/eval_jaxpr/ghij,jghp->ighp/dot_general | solution.py:81
  247.2 4.7 %fusion.52 = f32[8,512,1,8,64]{1,4,3,2,0:T(8,128)} fusion(f32[8,512,1,8,64]{1,4,3,2,0:T(8,128)} %get-tuple-element.377, s32[]{:T(128)} %get-tuple-element.376, f32[512,512]{1,0:T(8,128)S(1)} %fusion.51, f32[8,512]{1,0:T(8,128)S(1)} %dynamic-slice_bitcast_fusion.2, pred[512,512]{1,0:T(8,128)(4,1)S(1)} %iota_compare_fusion.2, ...), kind=kOutput, calls=%fused_computation.12.clone.1 | convolution fusion | flops 278921216 | bytes 2917376 | tf_op jit(solution)/shard_map/while/body/eval_jaxpr/ghij,jghp->ighp/dot_general | solution.py:81
  261.9 8.9 %while.41 = (s32[]{:T(128)}, f32[8,64,128]{2,1,0:T(8,128)S(1)}, f32[8,8,64,128]{3,2,1,0:T(8,128)S(1)}, f32[8,8]{1,0:T(8,128)S(1)}, f32[8,8,64,128]{3,2,1,0:T(8,128)}, /*index=5*/s32[]{:T(128)}, s32[]{:T(128)}) while((s32[]{:T(128)}, f32[8,64,128]{2,1,0:T(8,128)S(1)}, f32[8,8,64,128]{3,2,1,0:T(8,128)S(1)}, f32[8,8]{1,0:T(8,128)S(1)}, ...), condition=%wide.region_5.6_spmd.clone, body=%wide.region_4.5_spmd.clone.sunk | while | flops 262147 | bytes 1310916 | solution.py:101
  273.2 23.8 %all-reduce = bf16[128]{0:T(256)(128)(2,1)S(1)} all-reduce(bf16[128]{0:T(256)(128)(2,1)S(1)} %dynamic-update-slice), channel_id=2, replica_groups=mesh['seq'=16,'head'=16] {'seq'}, use_global_device_ids=true, to_apply=%add | all-reduce | flops 128 | bytes 512
  297.1 12.5 %all-gather.10.cloned.1.call-done = bf16[128,64,128]{2,1,0:T(8,128)(2,1)} async-done(((bf16[8,64,128]{2,1,0:T(8,128)(2,1)}), bf16[128,64,128]{2,1,0:T(8,128)(2,1)}) %all-gather.10.cloned.1.call-update) | async-done | bytes 2097168 | tf_op jit(solution)/shard_map/all_gather | solution.py:15
  309.6 16.0 %while.39 = (s32[]{:T(128)}, f32[8,64,128]{2,1,0:T(8,128)S(1)}, s32[]{:T(128)}, bf16[16,8]{1,0:T(8,128)(2,1)S(1)}, bf16[16,8,64,128]{3,2,1,0:T(8,128)(2,1)}, /*index=5*/s32[]{:T(128)}, s32[]{:T(128)}, s32[]{:T(128)}) while((s32[]{:T(128)}, f32[8,64,128]{2,1,0:T(8,128)S(1)}, s32[]{:T(128)}, bf16[16,8]{1,0:T(8,128)(2,1)S(1)}, ...), condition=%wide.region_9.10_spmd, body=%wide.region_8.9_spmd.sunk | while | flops 196621 | bytes 655567 | solution.py:29
  325.6 10.9 %fusion.29 = bf16[8,512,1,8,64]{1,4,3,0,2:T(8,128)(2,1)S(1)} fusion(f32[8,512,1,8,64]{1,4,3,2,0:T(8,128)} %get-tuple-element.123, f32[8,512,1,8,64]{1,0,4,3,2:T(8,128)} %reshape.178, f32[8]{0:T(128)S(1)} %dynamic_slice.44, f32[8,512,8]{1,2,0:T(8,128)S(1)} %get-tuple-element.260, bf16[8,512,128,1]{2,1,3,0:T(8,128)(2,1)S(1)} %bitcast.137, ...), kind=kOutput, calls=%fused_computation.40 | convolution fusion | flops 548929536 | bytes 24510752 | tf_op jit(solution)/shard_map/cign,cghpn->cighp/dot_general | solution.py:116
  341.0 7.1 %all_to_all.50 = bf16[16,256,512]{1,0,2:T(8,128)(2,1)} reshape(bf16[8,512,1,8,64]{1,0,4,3,2:T(8,128)(2,1)} %copy.89) | data formatting | bytes 8388608 | tf_op jit(solution)/shard_map/all_to_all | solution.py:124
  351.8 57.4 %all_to_all.58 = bf16[16,256,512]{1,2,0:T(8,128)(2,1)} all-to-all(bf16[16,256,512]{1,2,0:T(8,128)(2,1)S(1)} %copy.90), channel_id=1, replica_groups=mesh['seq'=16,'head'=16] {'head'}, dimensions={0} | all-to-all | bytes 8388608 | tf_op jit(solution)/shard_map/all_to_all | solution.py:124
  409.2 6.3 %copy.91 = bf16[256,8192]{1,0:T(8,128)(2,1)} copy(bf16[256,8192]{0,1:T(8,128)(2,1)} %bitcast.135) | data formatting | bytes 8388608 | tf_op jit(solution)/shard_map/all_to_all | solution.py:124
  (149 shorter events, 90.3 us)
Async XLA Ops:
  6.5 137.8 %all-gather.6.cloned.1.call-start = ((), (), s32[]{:S(2)}) async-start(), calls=%async_computation.4 | async-start | bytes 8912896 | tf_op jit(solution)/shard_map/all_gather | solution.py:51
  7.3 192.4 %all-gather.8.cloned.1.call-start = ((), (), s32[]{:S(2)}) async-start(), calls=%async_computation.5 | async-start | bytes 8912896 | tf_op jit(solution)/shard_map/all_gather | solution.py:50
  9.6 13.3 %all-to-all-start.2 = ((bf16[256,16,8]{0,2,1:T(8,128)(2,1)}), bf16[256,16,8]{0,2,1:T(8,128)(2,1)S(1)}, u32[]{:S(2)}, u32[]{:S(2)}) async-start(bf16[256,16,8]{0,2,1:T(8,128)(2,1)} %bitcast.102), calls=%async_computation.2 | async-start | bytes 131072 | tf_op jit(solution)/shard_map/all_to_all | solution.py:45
  22.9 10.3 %all-to-all-start.1 = ((bf16[256,16,8]{0,2,1:T(8,128)(2,1)}), bf16[256,16,8]{0,2,1:T(8,128)(2,1)S(1)}, u32[]{:S(2)}, u32[]{:S(2)}) async-start(bf16[256,16,8]{0,2,1:T(8,128)(2,1)} %bitcast.103), calls=%async_computation.1 | async-start | bytes 131072 | tf_op jit(solution)/shard_map/all_to_all | solution.py:42
  33.2 81.6 %all-to-all-start = ((bf16[256,16,512]{0,2,1:T(8,128)(2,1)}), bf16[256,16,512]{0,2,1:T(8,128)(2,1)}, u32[]{:S(2)}, u32[]{:S(2)}) async-start(bf16[256,16,512]{0,2,1:T(8,128)(2,1)} %bitcast.134), calls=%async_computation | async-start | bytes 8388608 | tf_op jit(solution)/shard_map/all_to_all | solution.py:40
  39.5 270.1 %all-gather.10.cloned.1.call-start = ((), (), s32[]{:S(2)}) async-start(), calls=%async_computation.6 | async-start | bytes 2228224 | tf_op jit(solution)/shard_map/all_gather | solution.py:15
  261.6 9.9 %copy-start.1 = (u32[256]{0:T(256)S(1)}, u32[256]{0:T(256)}, u32[]{:S(2)}) copy-start(u32[256]{0:T(256)} %constant.87) | copy-start | bytes 3076
  261.6 11.1 %copy-start = (f32[128]{0:T(128)S(1)}, f32[128]{0:T(128)}, u32[]{:S(2)}) copy-start(f32[128]{0:T(128)} %param.17) | copy-start | bytes 1540
Sparse Core Ops, SparseCore 0:
  9.8 115.7 all-gather.5
  128.0 71.6 all-gather.7
  271.6 37.8 all-gather.9
where the time goes:
time: 424 us; the launch traced here: 422 us
  waiting for transfers between devices  138 us (33%)
  blocking collectives  81.1 us (19%)
  matrix products  66.9 us (16%)
  local copies, waits for them, and re-layouts  60.3 us (14%)
  other arithmetic  43.7 us (10%)
  starting transfers between devices  16.6 us (4%)
  between operations  14 us (3%)
    all_to_all x1, waiting for transfers between devices, shards(): lax.all_to_all(features, 'head', split_axis=1, concat_axis=0, tiled=True)  65.2 us
    all_to_all x1, blocking collectives, shards(): lax.all_to_all(mixed_rows, 'head', split_axis=0, concat_axis=1, tiled=True)  57.4 us
    all_gather x1, waiting for transfers between devices, shards(): lax.all_gather(inject, 'head', axis=0, tiled=True)  54.1 us
    dot_general x8, matrix products, span_terms(): jnp.einsum('ghij,jghp->ighp', weights, drive_c, preferred_element_type=jn...  37.3 us
    unnamed x1, blocking collectives  23.8 us
    convert_element_type x2, local copies, waits for them, and re-layouts, shards(): regrouped.reshape(seq_rows, local_heads, HEAD_DIM).astype(jnp.float32)  17.9 us
    all_to_all x3, local copies, waits for them, and re-layouts, shards(): lax.all_to_all(mixed_rows, 'head', split_axis=0, concat_axis=1, tiled=True)  17.1 us
    dot_general x8, matrix products, span_terms(): jnp.einsum('jghp,jgn->ghpn', scaled, inject_c, preferred_element_type=jnp...  16.4 us
  transfers between devices with their start and end apart: 6, of which 5 were waited for; matrix products, arithmetic and copies ran while one was open for 12% of the time, Pallas kernels for 0%

commit v1 on v0

v1 whole, which is shorter than its diff:
```python
import functools

import jax
import jax.numpy as jnp
from jax import lax
from jax.experimental import pallas as pl
from jax.experimental.pallas import tpu as pltpu
from jax.sharding import PartitionSpec as P

HEADS = 128
HEAD_DIM = 64
STATE = 128
GROUPS = 8
TOK = 256
HALF = 128
LANES = 128
OWNERS = 64
STEP = 4
OWN_HEADS = HEADS // OWNERS
COLS = OWN_HEADS * HEAD_DIM
GROUP_COLS = HEADS // GROUPS * HEAD_DIM
GROUP_OWNERS = OWNERS // GROUPS
ROWS = STATE + 8
VMEM_LIMIT = 61 * 1024 * 1024
OUT_VMEM_LIMIT = 50 * 1024 * 1024
HELD_VMEM_LIMIT = 40 * 1024 * 1024
SMALL_VMEM_LIMIT = 24 * 1024 * 1024
WIDE = 512
LOCAL_PARTS = 2
PART_GROUPS = GROUPS // LOCAL_PARTS
PART_COLS = PART_GROUPS * GROUP_COLS

f32 = jnp.float32
bf16 = jnp.bfloat16


def dot(a, b):
    return jnp.dot(a, b, preferred_element_type=f32)


def dot_exact(a, b):
    return jnp.dot(a, b, preferred_element_type=f32, precision=lax.Precision.HIGHEST)


def iota(shape, axis):
    return lax.broadcasted_iota(jnp.int32, shape, axis)


def spread(scale, first_col, cols):
    place = iota((scale.shape[0], LANES), 1) >> 6
    first_head = first_col // HEAD_DIM
    return jnp.concatenate(
        [
            jnp.take_along_axis(
                scale, place + (first_head + 2 * k), axis=1, mode="promise_in_bounds"
            )
            for k in range(cols // LANES)
        ],
        axis=1,
    )


def copies(*triples):
    made = [pltpu.make_async_copy(*t) for t in triples]
    for c in made:
        c.start()
    return made


def state_kernel(
    x_hbm, step_hbm, decay_hbm, inject_hbm, out_hbm,
    x_buf, step_buf, decay_buf, inject_buf, out_buf, sem, in_sem, out_sem,
):
    decay_in, step_in, inject_in = copies(
        (decay_hbm, decay_buf, sem.at[0]),
        (step_hbm, step_buf, sem.at[1]),
        (inject_hbm, inject_buf, sem.at[2]),
    )
    x_in = copies(
        *[
            (x_hbm.at[:, pl.ds(g * GROUP_COLS, GROUP_COLS)], x_buf.at[g], in_sem.at[g])
            for g in range(GROUPS)
        ]
    )
    later = jnp.where(iota((TOK, TOK), 1) > iota((TOK, TOK), 0), 1.0, 0.0).astype(f32)
    decay_in.wait()
    decay = decay_buf[...]
    tail = dot_exact(later, decay)
    whole = jnp.broadcast_to(jnp.exp(tail[0:1] + decay[0:1]), (8, HEADS))
    high = whole.astype(bf16).astype(f32)
    row = iota((8, HEADS), 0)
    extra = jnp.where(row == 0, high, jnp.where(row == 1, whole - high, 0.0))
    step_in.wait()
    scale = step_buf[...] * jnp.exp(tail)
    inject_in.wait()
    sent = []
    for g in range(GROUPS):
        at = g * GROUP_COLS
        weight = spread(scale, at, GROUP_COLS)
        below = spread(extra, at, GROUP_COLS).astype(bf16)
        x_in[g].wait()
        v = (x_buf[g].astype(f32) * weight).astype(bf16)
        s = lax.dot_general(
            inject_buf[:, g * STATE : (g + 1) * STATE],
            v,
            (((0,), (0,)), ((), ())),
            preferred_element_type=f32,
        ).astype(bf16)
        first = g * GROUP_OWNERS
        for k in range(GROUP_OWNERS):
            cols = slice(k * COLS, (k + 1) * COLS)
            out_buf[first + k, :STATE, :] = s[:, cols]
            out_buf[first + k, STATE:, :] = below[:, cols]
        span = pl.ds(first, GROUP_OWNERS)
        sent += copies((out_buf.at[span], out_hbm.at[span], out_sem.at[g]))
    for c in sent:
        c.wait()


def states_of(x, step, decay, inject):
    hbm = pl.BlockSpec(memory_space=pltpu.HBM)
    return pl.pallas_call(
        state_kernel,
        out_shape=jax.ShapeDtypeStruct((OWNERS, ROWS, COLS), bf16),
        in_specs=[hbm] * 4,
        out_specs=hbm,
        scratch_shapes=[
            pltpu.VMEM((GROUPS, TOK, GROUP_COLS), bf16),
            pltpu.VMEM((TOK, HEADS), f32),
            pltpu.VMEM((TOK, HEADS), f32),
            pltpu.VMEM((TOK, GROUPS * STATE), bf16),
            pltpu.VMEM((OWNERS, ROWS, COLS), bf16),
            pltpu.SemaphoreType.DMA((3,)),
            pltpu.SemaphoreType.DMA((GROUPS,)),
            pltpu.SemaphoreType.DMA((GROUPS,)),
        ],
        compiler_params=pltpu.CompilerParams(vmem_limit_bytes=VMEM_LIMIT),
        cost_estimate=pl.CostEstimate(
            flops=2_000_000_000, bytes_accessed=8_000_000, transcendentals=32768
        ),
        name="states",
    )(x, step, decay, inject)


def decay_row(block):
    return block[STATE : STATE + 1].astype(f32) + block[STATE + 1 : STATE + 2].astype(f32)


def pack_rows(decay):
    row = iota((8, COLS), 0)
    high = decay.astype(bf16).astype(f32)
    return jnp.where(row == 0, high, jnp.where(row == 1, decay - high, 0.0)).astype(bf16)


def total_kernel(in_ref, out_ref):
    state = in_ref[0, :STATE, :].astype(f32)
    decay = decay_row(in_ref[0])
    for i in range(1, OWNERS):
        d = decay_row(in_ref[i])
        state = state * d + in_ref[i, :STATE, :].astype(f32)
        decay = decay * d
    out_ref[:STATE, :] = state.astype(bf16)
    out_ref[STATE:, :] = pack_rows(decay)


def held_kernel(one_ref, two_ref, three_ref, in_ref, out_hbm, out_buf, sem):
    state = three_ref[:STATE, :].astype(f32)
    for ref in (two_ref, one_ref):
        state = ref[:STATE, :].astype(f32) + decay_row(ref[...]) * state
    sent = []
    for i in range(OWNERS):
        out_buf[i] = state.astype(bf16)
        if (i + 1) % GROUPS == 0:
            span = pl.ds(i + 1 - GROUPS, GROUPS)
            sent += copies((out_buf.at[span], out_hbm.at[span], sem.at[i // GROUPS]))
        if i + 1 < OWNERS:
            state = state * decay_row(in_ref[i]) + in_ref[i, :STATE, :].astype(f32)
    for c in sent:
        c.wait()


def total_of(arrived):
    return pl.pallas_call(
        total_kernel,
        out_shape=jax.ShapeDtypeStruct((ROWS, COLS), bf16),
        compiler_params=pltpu.CompilerParams(vmem_limit_bytes=SMALL_VMEM_LIMIT),
        cost_estimate=pl.CostEstimate(flops=4_000_000, bytes_accessed=2_000_000, transcendentals=0),
        name="total",
    )(arrived)


def held_of(earlier, arrived):
    vmem = pl.BlockSpec(memory_space=pltpu.VMEM)
    return pl.pallas_call(
        held_kernel,
        out_shape=jax.ShapeDtypeStruct((OWNERS, STATE, COLS), bf16),
        in_specs=[vmem] * 4,
        out_specs=pl.BlockSpec(memory_space=pltpu.HBM),
        scratch_shapes=[
            pltpu.VMEM((OWNERS, STATE, COLS), bf16),
            pltpu.SemaphoreType.DMA((OWNERS // GROUPS,)),
        ],
        compiler_params=pltpu.CompilerParams(vmem_limit_bytes=HELD_VMEM_LIMIT),
        cost_estimate=pl.CostEstimate(flops=4_000_000, bytes_accessed=4_000_000, transcendentals=0),
        name="held",
    )(*earlier, arrived)


def local_kernel(
    part, x_hbm, step_hbm, decay_hbm, inject_hbm, readout_hbm, gain_ref, *rest
):
    (
        out_hbm, x_buf, step_buf, decay_buf, inject_buf, readout_buf, out_buf,
        sem, in_sem, out_sem,
    ) = rest[-10:]
    decay_in, step_in, inject_in, readout_in = copies(
        (decay_hbm, decay_buf, sem.at[0]),
        (step_hbm, step_buf, sem.at[1]),
        (inject_hbm, inject_buf, sem.at[2]),
        (readout_hbm, readout_buf, sem.at[3]),
    )
    x_in = copies(
        *[
            (
                x_hbm.at[:, pl.ds(part * PART_COLS + n * GROUP_COLS, GROUP_COLS)],
                x_buf.at[n],
                in_sem.at[n],
            )
            for n in range(PART_GROUPS)
        ]
    )
    lower = iota((HALF, HALF), 0) >= iota((HALF, HALF), 1)
    lower_f = jnp.where(lower, 1.0, 0.0).astype(f32)
    decay_in.wait()
    cum_a = dot_exact(lower_f, decay_buf[:HALF])
    cum_b = dot_exact(lower_f, decay_buf[HALF:])
    mid = HALF // 2 - 1
    mid_b = cum_b[mid : mid + 1]
    gap_a = cum_a - cum_a[mid : mid + 1]
    gap_b = cum_b - mid_b
    onward = jnp.exp(mid_b + gap_a[HALF - 1 : HALF])
    few = iota((8, HEADS), 0)
    rows = jnp.where(few == 0, onward, gain_ref[...])
    step_in.wait()
    into_a = step_buf[:HALF] * jnp.exp(-gap_a)
    into_b = step_buf[HALF:] * jnp.exp(-gap_b)
    from_a = jnp.exp(gap_a)
    from_b = jnp.exp(gap_b)
    zero = jnp.zeros((HALF, HALF), f32)
    inject_in.wait()
    readout_in.wait()

    def pair(r, i):
        return lax.dot_general(r, i, (((1,), (1,)), ((), ())), preferred_element_type=f32)

    sent = []
    for n in range(PART_GROUPS):
        g = part * PART_GROUPS + n
        state_cols = slice(g * STATE, (g + 1) * STATE)
        inj_a = inject_buf[:HALF, state_cols]
        inj_b = inject_buf[HALF:, state_cols]
        read_a = readout_buf[:HALF, state_cols]
        read_b = readout_buf[HALF:, state_cols]
        near_a = jnp.where(lower, pair(read_a, inj_a), zero).astype(bf16)
        near_b = jnp.concatenate(
            [
                pair(read_b, inj_a).astype(bf16),
                jnp.where(lower, pair(read_b, inj_b), zero).astype(bf16),
            ],
            axis=1,
        )
        x_in[n].wait()
        for k in range(GROUP_COLS // WIDE):
            cols = slice(k * WIDE, (k + 1) * WIDE)
            at = g * GROUP_COLS + k * WIDE
            row = spread(rows, at, WIDE)
            gain = row[1:2]
            x_a = x_buf[n, :HALF, cols].astype(f32)
            x_b = x_buf[n, HALF:, cols].astype(f32)
            v_a = x_a * spread(into_a, at, WIDE)
            v_b = (x_b * spread(into_b, at, WIDE)).astype(bf16)
            res_a = dot(near_a, v_a.astype(bf16))
            res_b = dot(near_b, jnp.concatenate([(v_a * row[0:1]).astype(bf16), v_b], axis=0))
            out_a = res_a * spread(from_a, at, WIDE) + gain * x_a
            out_b = res_b * spread(from_b, at, WIDE) + gain * x_b
            out_buf[n, :HALF, cols] = out_a.astype(bf16)
            out_buf[n, HALF:, cols] = out_b.astype(bf16)
        sent += copies(
            (out_buf.at[n], out_hbm.at[:, pl.ds(g * GROUP_COLS, GROUP_COLS)], out_sem.at[n])
        )
    for c in sent:
        c.wait()


def local_of(part, so_far, x, step, decay, inject, readout, gain):
    hbm = pl.BlockSpec(memory_space=pltpu.HBM)
    vmem = pl.BlockSpec(memory_space=pltpu.VMEM)
    return pl.pallas_call(
        functools.partial(local_kernel, part),
        out_shape=jax.ShapeDtypeStruct(x.shape, bf16),
        in_specs=[hbm] * 5 + [vmem] + [hbm] * len(so_far),
        input_output_aliases={6: 0} if so_far else {},
        out_specs=hbm,
        scratch_shapes=[
            pltpu.VMEM((PART_GROUPS, TOK, GROUP_COLS), bf16),
            pltpu.VMEM((TOK, HEADS), f32),
            pltpu.VMEM((TOK, HEADS), f32),
            pltpu.VMEM((TOK, GROUPS * STATE), bf16),
            pltpu.VMEM((TOK, GROUPS * STATE), bf16),
            pltpu.VMEM((PART_GROUPS, TOK, GROUP_COLS), bf16),
            pltpu.SemaphoreType.DMA((4,)),
            pltpu.SemaphoreType.DMA((PART_GROUPS,)),
            pltpu.SemaphoreType.DMA((PART_GROUPS,)),
        ],
        compiler_params=pltpu.CompilerParams(vmem_limit_bytes=VMEM_LIMIT),
        cost_estimate=pl.CostEstimate(
            flops=2_000_000_000, bytes_accessed=6_000_000, transcendentals=65536
        ),
        name=f"local{part}",
    )(x, step, decay, inject, readout, gain, *so_far)


def out_kernel(
    decay_hbm, readout_hbm, held_ref, local_hbm, out_hbm,
    decay_buf, readout_buf, local_buf, out_buf, sem, local_sem, out_sem,
):
    decay_in, readout_in = copies(
        (decay_hbm, decay_buf, sem.at[0]), (readout_hbm, readout_buf, sem.at[1])
    )
    local_in = copies(
        *[
            (local_hbm.at[:, pl.ds(g * GROUP_COLS, GROUP_COLS)], local_buf.at[g], local_sem.at[g])
            for g in range(GROUPS)
        ]
    )
    lower = jnp.where(iota((TOK, TOK), 0) >= iota((TOK, TOK), 1), 1.0, 0.0).astype(f32)
    decay_in.wait()
    lead = jnp.exp(dot_exact(lower, decay_buf[...]))
    readout_in.wait()
    sent = []
    for g in range(GROUPS):
        readout = readout_buf[:, g * STATE : (g + 1) * STATE]
        local_in[g].wait()
        for k in range(GROUP_COLS // WIDE):
            cols = slice(k * WIDE, (k + 1) * WIDE)
            at = g * GROUP_COLS + k * WIDE
            first = at // COLS
            held = jnp.concatenate(
                [held_ref[first + i] for i in range(WIDE // COLS)], axis=1
            )
            out = dot(readout, held) * spread(lead, at, WIDE) + local_buf[g, :, cols].astype(f32)
            out_buf[g, :, cols] = out.astype(bf16)
        sent += copies(
            (out_buf.at[g], out_hbm.at[:, pl.ds(g * GROUP_COLS, GROUP_COLS)], out_sem.at[g])
        )
    for c in sent:
        c.wait()


def outputs_of(decay, readout, held, local):
    hbm = pl.BlockSpec(memory_space=pltpu.HBM)
    vmem = pl.BlockSpec(memory_space=pltpu.VMEM)
    return pl.pallas_call(
        out_kernel,
        out_shape=jax.ShapeDtypeStruct((TOK, HEADS * HEAD_DIM), bf16),
        in_specs=[hbm, hbm, vmem, hbm],
        out_specs=hbm,
        scratch_shapes=[
            pltpu.VMEM((TOK, HEADS), f32),
            pltpu.VMEM((TOK, GROUPS * STATE), bf16),
            pltpu.VMEM((GROUPS, TOK, GROUP_COLS), bf16),
            pltpu.VMEM((GROUPS, TOK, GROUP_COLS), bf16),
            pltpu.SemaphoreType.DMA((2,)),
            pltpu.SemaphoreType.DMA((GROUPS,)),
            pltpu.SemaphoreType.DMA((GROUPS,)),
        ],
        compiler_params=pltpu.CompilerParams(vmem_limit_bytes=OUT_VMEM_LIMIT),
        cost_estimate=pl.CostEstimate(
            flops=2_000_000_000, bytes_accessed=12_000_000, transcendentals=32768
        ),
        name="outputs",
    )(decay, readout, held, local)


def later_by(v, shift, ways):
    return lax.ppermute(v, "seq", [(i, i + shift) for i in range(ways - shift)])


def exchange(v, devices):
    return lax.all_to_all(
        v,
        ("seq", "head"),
        split_axis=0,
        concat_axis=0,
        tiled=True,
        axis_index_groups=[
            list(range(first, first + OWNERS)) for first in range(0, devices, OWNERS)
        ],
    )


def shards(features, step_size, log_decay, inject, readout, skip_gain):
    ways = lax.axis_size("seq")
    devices = ways * lax.axis_size("head")
    args = (features, step_size, log_decay, inject, readout, skip_gain[None, :])
    arrived = exchange(states_of(features, step_size, log_decay, inject), devices)
    local = local_of(0, (), *args)
    arrived, local = lax.optimization_barrier((arrived, local))
    total = total_of(arrived)
    earlier = [later_by(total, k * STEP, ways) for k in (1, 2, 3)]
    held = held_of(earlier, arrived)
    held = exchange(held, devices)
    local = local_of(1, (local,), *args)
    return outputs_of(log_decay, readout, held, local)


def solution(mesh):
    rows = P(("seq", "head"), None)
    return jax.shard_map(
        shards,
        mesh=mesh,
        in_specs=(rows, rows, rows, rows, rows, P()),
        out_specs=rows,
        check_vma=False,
    )
```

time: 424 us -> 102 us (0.24)
  the two profiles are of different devices: /device:TPU:225 before, /device:TPU:1 now
where the time goes in v1:
time: 102 us
  waiting for transfers between devices  43.8 us (43%)
  starting transfers between devices  29.5 us (29%)
  Pallas kernels  27.1 us (27%)
  local copies, waits for them, and re-layouts  1.33 us (1%)
    all_to_all x2, waiting for transfers between devices, exchange(): lax.all_to_all(v, ('seq', 'head'), split_axis=0, concat_axis=0, tiled=Tru...  42.4 us
    all_to_all x2, starting transfers between devices, exchange(): lax.all_to_all(v, ('seq', 'head'), split_axis=0, concat_axis=0, tiled=Tru...  17.2 us
    pallas_call x2, Pallas kernels, local_of(): pl.pallas_call(functools.partial(local_kernel, part), out_shape=jax.Shape...  13.4 us
    ppermute x3, starting transfers between devices, later_by(): return lax.ppermute(v, 'seq', [(i, i + shift) for i in range(ways - shift)])  12.3 us
    pallas_call x1, Pallas kernels, states_of(): pl.pallas_call(state_kernel, out_shape=jax.ShapeDtypeStruct((OWNERS, ROWS...  6.94 us
    pallas_call x1, Pallas kernels, outputs_of(): pl.pallas_call(out_kernel, out_shape=jax.ShapeDtypeStruct((TOK, HEADS * H...  5.44 us
  transfers between devices with their start and end apart: 5, of which 3 were waited for; matrix products, arithmetic and copies ran while one was open for 0% of the time, Pallas kernels for 13%

profile of v1, /device:TPU:1, one launch (start us, length us, event | category | flops | bytes accessed | tf_op | source)
XLA Modules:
  0.0 102.1 jit_solution(11080262300280503253)
XLA Ops:
  0.0 6.9 %states.1 = bf16[64,136,128]{2,1,0:T(8,128)(2,1)} custom-call(bf16[256,8192]{1,0:T(8,128)(2,1)} %x_hbm.5, f32[256,128]{1,0:T(8,128)} %step_hbm.5, f32[256,128]{1,0:T(8,128)} %decay_hbm.7, bf16[256,1024]{1,0:T(8,128)(2,1)} %inject_hbm.5), custom_call_target="tpu_custom_call" | custom-call | flops 2000000000 | bytes 8000000 | tf_op jit(solution)/shard_map/states/pallas_call | solution.py:122
  6.9 10.4 %all-to-all-start = ((bf16[64,136,128]{2,1,0:T(8,128)(2,1)}), bf16[64,136,128]{2,1,0:T(8,128)(2,1)S(1)}, u32[]{:S(2)}, u32[]{:S(2)}) async-start(bf16[64,136,128]{2,1,0:T(8,128)(2,1)} %states.1), calls=%async_computation | async-start | bytes 4456448 | tf_op jit(solution)/shard_map/all_to_all | solution.py:390
  17.3 6.7 %local0.1.rest_0_ = bf16[256,8192]{1,0:T(8,128)(2,1)} custom-call(bf16[256,8192]{1,0:T(8,128)(2,1)} %x_hbm.5, f32[256,128]{1,0:T(8,128)} %step_hbm.5, f32[256,128]{1,0:T(8,128)} %decay_hbm.7, bf16[256,1024]{1,0:T(8,128)(2,1)} %inject_hbm.5, bf16[256,1024]{1,0:T(8,128)(2,1)} %readout_hbm.5, f32[1,128]{1,0:T(1,128)} %bitcast.1), custom_call_target="tpu_custom_call" | custom-call | flops 2000000000 | bytes 6000000 | tf_op jit(solution)/shard_map/local0/pallas_call | solution.py:298
  24.0 22.0 %all-to-all-done.in_ref = bf16[64,136,128]{2,1,0:T(8,128)(2,1)S(1)} async-done(((bf16[64,136,128]{2,1,0:T(8,128)(2,1)}), bf16[64,136,128]{2,1,0:T(8,128)(2,1)S(1)}, u32[]{:S(2)}, u32[]{:S(2)}) %all-to-all-start) | async-done | bytes 2228256 | tf_op jit(solution)/shard_map/all_to_all | solution.py:390
  46.0 0.5 total.1
  46.5 4.9 %collective-permute-start = (bf16[136,128]{1,0:T(8,128)(2,1)S(1)}, bf16[136,128]{1,0:T(8,128)(2,1)S(1)}, u32[]{:S(2)}, u32[]{:S(2)}) collective-permute-start(bf16[136,128]{1,0:T(8,128)(2,1)S(1)} %total.1), channel_id=1, source_target_pairs={{0,64},{16,80},{32,96},{48,112},{64,128},{80,144},{96,160},{112,17... | collective-permute-start | bytes 104456 | tf_op jit(solution)/shard_map/ppermute | solution.py:386
  51.4 6.1 %collective-permute-start.1 = (bf16[136,128]{1,0:T(8,128)(2,1)S(1)}, bf16[136,128]{1,0:T(8,128)(2,1)S(1)}, u32[]{:S(2)}, u32[]{:S(2)}) collective-permute-start(bf16[136,128]{1,0:T(8,128)(2,1)S(1)} %total.1), channel_id=1, source_target_pairs={{0,128},{16,144},{32,160},{48,176},{64,192},{80,208},{96,224},{112... | collective-permute-start | bytes 104456 | tf_op jit(solution)/shard_map/ppermute | solution.py:386
  57.6 1.3 %collective-permute-start.2 = (bf16[136,128]{1,0:T(8,128)(2,1)S(1)}, bf16[136,128]{1,0:T(8,128)(2,1)S(1)}, u32[]{:S(2)}, u32[]{:S(2)}) collective-permute-start(bf16[136,128]{1,0:T(8,128)(2,1)S(1)} %total.1), channel_id=1, source_target_pairs={{0,192},{16,208},{32,224},{48,240},{1,193},{17,209},{33,225},{49,2... | collective-permute-start | bytes 104456 | tf_op jit(solution)/shard_map/ppermute | solution.py:386
  58.9 0.0 collective-permute-done.one_ref
  58.9 0.0 collective-permute-done.1.two_ref
  58.9 1.4 %collective-permute-done.2.three_ref = bf16[136,128]{1,0:T(8,128)(2,1)S(1)} collective-permute-done((bf16[136,128]{1,0:T(8,128)(2,1)S(1)}, bf16[136,128]{1,0:T(8,128)(2,1)S(1)}, u32[]{:S(2)}, u32[]{:S(2)}) %collective-permute-start.2) | collective-permute-done | bytes 34848 | tf_op jit(solution)/shard_map/ppermute | solution.py:386
  60.3 0.8 held.1
  61.1 0.0 copy-start
  61.1 1.3 %copy-done = bf16[64,128,128]{2,1,0:T(8,128)(2,1)} copy-done((bf16[64,128,128]{2,1,0:T(8,128)(2,1)}, bf16[64,128,128]{2,1,0:T(8,128)(2,1)S(1)}, u32[]{:S(2)}) %copy-start) | copy-done | bytes 2097176
  62.4 6.9 %all-to-all-start.1 = ((bf16[64,128,128]{2,1,0:T(8,128)(2,1)}), bf16[64,128,128]{2,1,0:T(8,128)(2,1)S(1)}, u32[]{:S(2)}, u32[]{:S(2)}) async-start(bf16[64,128,128]{2,1,0:T(8,128)(2,1)} %copy-done), calls=%async_computation.1 | async-start | bytes 4194304 | tf_op jit(solution)/shard_map/all_to_all | solution.py:390
  69.3 0.0 copy-start.1
  69.3 0.0 copy-start.2
  69.3 6.7 %local1.1.local_hbm = bf16[256,8192]{1,0:T(8,128)(2,1)} custom-call(bf16[256,8192]{1,0:T(8,128)(2,1)} %x_hbm.5, f32[256,128]{1,0:T(8,128)} %step_hbm.5, f32[256,128]{1,0:T(8,128)} %decay_hbm.7, bf16[256,1024]{1,0:T(8,128)(2,1)} %inject_hbm.5, bf16[256,1024]{1,0:T(8,128)(2,1)} %readout_hbm.5, f32[1,128]{1,0:T(1,128)} %bitcast.2, ...), custom_call_target="tpu_custom_call", output_to_operand_aliasing={{}: (6, {})} | custom-call | flops 2000000000 | bytes 6000000 | tf_op jit(solution)/shard_map/local1/pallas_call | solution.py:298
  76.0 20.4 %all-to-all-done.1.held_ref = bf16[64,128,128]{2,1,0:T(8,128)(2,1)S(1)} async-done(((bf16[64,128,128]{2,1,0:T(8,128)(2,1)}), bf16[64,128,128]{2,1,0:T(8,128)(2,1)S(1)}, u32[]{:S(2)}, u32[]{:S(2)}) %all-to-all-start.1) | async-done | bytes 2097184 | tf_op jit(solution)/shard_map/all_to_all | solution.py:390
  96.5 0.0 copy-done.1
  96.5 0.0 copy-done.2
  96.5 5.4 %outputs.1 = bf16[256,8192]{1,0:T(8,128)(2,1)} custom-call(f32[256,128]{1,0:T(8,128)S(1)} %copy-done.2, bf16[256,1024]{1,0:T(8,128)(2,1)S(1)} %copy-done.1, bf16[64,128,128]{2,1,0:T(8,128)(2,1)S(1)} %all-to-all-done.1.held_ref, bf16[256,8192]{1,0:T(8,128)(2,1)} %local1.1.local_hbm), custom_call_target="tpu_custom_call" | custom-call | flops 2000000000 | bytes 12000000 | tf_op jit(solution)/shard_map/outputs/pallas_call | solution.py:363
Async XLA Ops:
  6.9 39.1 %all-to-all-start = ((bf16[64,136,128]{2,1,0:T(8,128)(2,1)}), bf16[64,136,128]{2,1,0:T(8,128)(2,1)S(1)}, u32[]{:S(2)}, u32[]{:S(2)}) async-start(bf16[64,136,128]{2,1,0:T(8,128)(2,1)} %states.1), calls=%async_computation | async-start | bytes 4456448 | tf_op jit(solution)/shard_map/all_to_all | solution.py:390
  46.5 12.3 %collective-permute-start = (bf16[136,128]{1,0:T(8,128)(2,1)S(1)}, bf16[136,128]{1,0:T(8,128)(2,1)S(1)}, u32[]{:S(2)}, u32[]{:S(2)}) collective-permute-start(bf16[136,128]{1,0:T(8,128)(2,1)S(1)} %total.1), channel_id=1, source_target_pairs={{0,64},{16,80},{32,96},{48,112},{64,128},{80,144},{96,160},{112,17... | collective-permute-start | bytes 104456 | tf_op jit(solution)/shard_map/ppermute | solution.py:386
  51.4 7.4 %collective-permute-start.1 = (bf16[136,128]{1,0:T(8,128)(2,1)S(1)}, bf16[136,128]{1,0:T(8,128)(2,1)S(1)}, u32[]{:S(2)}, u32[]{:S(2)}) collective-permute-start(bf16[136,128]{1,0:T(8,128)(2,1)S(1)} %total.1), channel_id=1, source_target_pairs={{0,128},{16,144},{32,160},{48,176},{64,192},{80,208},{96,224},{112... | collective-permute-start | bytes 104456 | tf_op jit(solution)/shard_map/ppermute | solution.py:386
  57.6 2.7 %collective-permute-start.2 = (bf16[136,128]{1,0:T(8,128)(2,1)S(1)}, bf16[136,128]{1,0:T(8,128)(2,1)S(1)}, u32[]{:S(2)}, u32[]{:S(2)}) collective-permute-start(bf16[136,128]{1,0:T(8,128)(2,1)S(1)} %total.1), channel_id=1, source_target_pairs={{0,192},{16,208},{32,224},{48,240},{1,193},{17,209},{33,225},{49,2... | collective-permute-start | bytes 104456 | tf_op jit(solution)/shard_map/ppermute | solution.py:386
  61.1 1.3 %copy-start = (bf16[64,128,128]{2,1,0:T(8,128)(2,1)}, bf16[64,128,128]{2,1,0:T(8,128)(2,1)S(1)}, u32[]{:S(2)}) copy-start(bf16[64,128,128]{2,1,0:T(8,128)(2,1)S(1)} %held.1) | copy-start | bytes 6291460
  62.4 34.1 %all-to-all-start.1 = ((bf16[64,128,128]{2,1,0:T(8,128)(2,1)}), bf16[64,128,128]{2,1,0:T(8,128)(2,1)S(1)}, u32[]{:S(2)}, u32[]{:S(2)}) async-start(bf16[64,128,128]{2,1,0:T(8,128)(2,1)} %copy-done), calls=%async_computation.1 | async-start | bytes 4194304 | tf_op jit(solution)/shard_map/all_to_all | solution.py:390
  69.3 27.2 %copy-start.1 = (bf16[256,1024]{1,0:T(8,128)(2,1)S(1)}, bf16[256,1024]{1,0:T(8,128)(2,1)}, u32[]{:S(2)}) copy-start(bf16[256,1024]{1,0:T(8,128)(2,1)} %readout_hbm.5) | copy-start | bytes 1572868
  69.3 27.2 %copy-start.2 = (f32[256,128]{1,0:T(8,128)S(1)}, f32[256,128]{1,0:T(8,128)}, u32[]{:S(2)}) copy-start(f32[256,128]{1,0:T(8,128)} %decay_hbm.7) | copy-start | bytes 393220

commit v2 on v1

v2 whole, which is shorter than its diff:
```python
import functools

import jax
import jax.numpy as jnp
from jax import lax
from jax.experimental import pallas as pl
from jax.experimental.pallas import tpu as pltpu
from jax.sharding import PartitionSpec as P

HEADS = 128
HEAD_DIM = 64
STATE = 128
GROUPS = 8
GROUP_HEADS = HEADS // GROUPS
TOK = 256
HALF = 128
LANES = 128
PARTS = 2
PART_GROUPS = GROUPS // PARTS
GROUP_COLS = GROUP_HEADS * HEAD_DIM
PART_COLS = PART_GROUPS * GROUP_COLS
OWNERS = HEADS // PARTS
STEP = 4
ROWS = STATE // 2
EXTRA = 8
WIDE = 512
VMEM_LIMIT = 61 * 1024 * 1024
OUT_VMEM_LIMIT = 50 * 1024 * 1024
HELD_VMEM_LIMIT = 40 * 1024 * 1024
SMALL_VMEM_LIMIT = 24 * 1024 * 1024

f32 = jnp.float32
bf16 = jnp.bfloat16


def dot(a, b):
    return jnp.dot(a, b, preferred_element_type=f32)


def dot_exact(a, b):
    return jnp.dot(a, b, preferred_element_type=f32, precision=lax.Precision.HIGHEST)


def iota(shape, axis):
    return lax.broadcasted_iota(jnp.int32, shape, axis)


def spread(scale, first_col, cols):
    place = iota((scale.shape[0], LANES), 1) >> 6
    first_head = first_col // HEAD_DIM
    return jnp.concatenate(
        [
            jnp.take_along_axis(
                scale, place + (first_head + 2 * k), axis=1, mode="promise_in_bounds"
            )
            for k in range(cols // LANES)
        ],
        axis=1,
    )


def copies(*triples):
    made = [pltpu.make_async_copy(*t) for t in triples]
    for c in made:
        c.start()
    return made


def swap_matrix():
    row = iota((2 * LANES, 2 * LANES), 0)
    quarter = row >> 6
    goal = jnp.where(quarter == 1, 2, jnp.where(quarter == 2, 1, quarter))
    hit = iota((2 * LANES, 2 * LANES), 1) == goal * HEAD_DIM + (row & (HEAD_DIM - 1))
    return jnp.where(hit, 1.0, 0.0).astype(bf16)


def state_kernel(
    part, x_hbm, step_hbm, decay_hbm, inject_hbm, out_hbm,
    x_buf, step_buf, decay_buf, inject_buf, out_buf, sem, in_sem, out_sem,
):
    decay_in, step_in, inject_in = copies(
        (decay_hbm, decay_buf, sem.at[0]),
        (step_hbm, step_buf, sem.at[1]),
        (inject_hbm.at[:, pl.ds(part * PART_GROUPS * STATE, PART_GROUPS * STATE)], inject_buf, sem.at[2]),
    )
    x_in = copies(
        *[
            (
                x_hbm.at[:, pl.ds(part * PART_COLS + n * GROUP_COLS, GROUP_COLS)],
                x_buf.at[n],
                in_sem.at[n],
            )
            for n in range(PART_GROUPS)
        ]
    )
    swap = swap_matrix()
    later = jnp.where(iota((TOK, TOK), 1) > iota((TOK, TOK), 0), 1.0, 0.0).astype(f32)
    decay_in.wait()
    decay = decay_buf[...]
    tail = dot_exact(later, decay)
    if part == 0:
        whole = jnp.broadcast_to(jnp.exp(tail[0:1] + decay[0:1]), (EXTRA, HEADS))
        other = jnp.concatenate([whole[:, OWNERS:], whole[:, :OWNERS]], axis=1)
        row = iota((EXTRA, HEADS), 0)
        value = jnp.where(row < 2, whole, jnp.where(row < 4, other, 0.0))
        high = value.astype(bf16).astype(f32)
        extra = jnp.where((row & 1) == 0, high, value - high)
    step_in.wait()
    scale = step_buf[...] * jnp.exp(tail)
    inject_in.wait()
    sent = []
    for n in range(PART_GROUPS):
        g = part * PART_GROUPS + n
        weight = spread(scale, g * GROUP_COLS, GROUP_COLS)
        x_in[n].wait()
        v = (x_buf[n].astype(f32) * weight).astype(bf16)
        s = lax.dot_general(
            inject_buf[:, n * STATE : (n + 1) * STATE],
            v,
            (((0,), (0,)), ((), ())),
            preferred_element_type=f32,
        ).astype(bf16)
        pairs = jnp.concatenate(
            [
                jnp.concatenate([s[:ROWS, k * LANES : (k + 1) * LANES], s[ROWS:, k * LANES : (k + 1) * LANES]], axis=1)
                for k in range(GROUP_COLS // LANES)
            ],
            axis=0,
        )
        blocks = dot(pairs, swap).astype(bf16)
        first = n * GROUP_HEADS
        for k in range(GROUP_HEADS):
            top = k // 2 * ROWS
            left = k % 2 * LANES
            out_buf[first + k, :ROWS, :] = blocks[top : top + ROWS, left : left + LANES]
            if part == 0:
                place = jnp.full((EXTRA, LANES), first + k, jnp.int32)
                out_buf[first + k, ROWS:, :] = jnp.take_along_axis(
                    extra, place, axis=1, mode="promise_in_bounds"
                ).astype(bf16)
        span = pl.ds(first, GROUP_HEADS)
        sent += copies((out_buf.at[span], out_hbm.at[span], out_sem.at[n]))
    for c in sent:
        c.wait()


def states_of(part, x, step, decay, inject):
    hbm = pl.BlockSpec(memory_space=pltpu.HBM)
    shape = (OWNERS, ROWS + (EXTRA if part == 0 else 0), LANES)
    return pl.pallas_call(
        functools.partial(state_kernel, part),
        out_shape=jax.ShapeDtypeStruct(shape, bf16),
        in_specs=[hbm] * 4,
        out_specs=hbm,
        scratch_shapes=[
            pltpu.VMEM((PART_GROUPS, TOK, GROUP_COLS), bf16),
            pltpu.VMEM((TOK, HEADS), f32),
            pltpu.VMEM((TOK, HEADS), f32),
            pltpu.VMEM((TOK, PART_GROUPS * STATE), bf16),
            pltpu.VMEM(shape, bf16),
            pltpu.SemaphoreType.DMA((3,)),
            pltpu.SemaphoreType.DMA((PART_GROUPS,)),
            pltpu.SemaphoreType.DMA((PART_GROUPS,)),
        ],
        compiler_params=pltpu.CompilerParams(vmem_limit_bytes=VMEM_LIMIT),
        cost_estimate=pl.CostEstimate(
            flops=1_000_000_000, bytes_accessed=4_000_000, transcendentals=32768
        ),
        name=f"states{part}",
    )(x, step, decay, inject)


def two_rows(block, at):
    return block[at : at + 1].astype(f32) + block[at + 1 : at + 2].astype(f32)


def total_kernel(part, in_ref, decay_ref, out_ref):
    state = jnp.zeros((ROWS, LANES), f32)
    decay = jnp.ones((1, LANES), f32)
    for i in range(OWNERS):
        d = two_rows(decay_ref[i, ROWS:, :], 2 * part)
        state = state * d + in_ref[i, :ROWS, :].astype(f32)
        decay = decay * d
    out_ref[:ROWS, :] = state.astype(bf16)
    row = iota((EXTRA, LANES), 0)
    high = decay.astype(bf16).astype(f32)
    rows = jnp.where(row == 0, high, jnp.where(row == 1, decay - high, 0.0))
    out_ref[ROWS:, :] = rows.astype(bf16)


def held_kernel(part, one_ref, two_ref, three_ref, in_ref, decay_ref, out_hbm, out_buf, sem):
    state = three_ref[:ROWS, :].astype(f32)
    for ref in (two_ref, one_ref):
        state = ref[:ROWS, :].astype(f32) + two_rows(ref[ROWS:, :], 0) * state
    sent = []
    for i in range(OWNERS):
        out_buf[i] = state.astype(bf16)
        if (i + 1) % GROUP_HEADS == 0:
            span = pl.ds(i + 1 - GROUP_HEADS, GROUP_HEADS)
            sent += copies((out_buf.at[span], out_hbm.at[span], sem.at[i // GROUP_HEADS]))
        if i + 1 < OWNERS:
            d = two_rows(decay_ref[i, ROWS:, :], 2 * part)
            state = state * d + in_ref[i, :ROWS, :].astype(f32)
    for c in sent:
        c.wait()


def total_of(part, arrived, decays):
    return pl.pallas_call(
        functools.partial(total_kernel, part),
        out_shape=jax.ShapeDtypeStruct((ROWS + EXTRA, LANES), bf16),
        compiler_params=pltpu.CompilerParams(vmem_limit_bytes=SMALL_VMEM_LIMIT),
        cost_estimate=pl.CostEstimate(flops=2_000_000, bytes_accessed=1_000_000, transcendentals=0),
        name=f"total{part}",
    )(arrived, decays)


def held_of(part, earlier, arrived, decays):
    vmem = pl.BlockSpec(memory_space=pltpu.VMEM)
    return pl.pallas_call(
        functools.partial(held_kernel, part),
        out_shape=jax.ShapeDtypeStruct((OWNERS, ROWS, LANES), bf16),
        in_specs=[vmem] * 5,
        out_specs=pl.BlockSpec(memory_space=pltpu.HBM),
        scratch_shapes=[
            pltpu.VMEM((OWNERS, ROWS, LANES), bf16),
            pltpu.SemaphoreType.DMA((OWNERS // GROUP_HEADS,)),
        ],
        compiler_params=pltpu.CompilerParams(vmem_limit_bytes=HELD_VMEM_LIMIT),
        cost_estimate=pl.CostEstimate(flops=2_000_000, bytes_accessed=2_000_000, transcendentals=0),
        name=f"held{part}",
    )(*earlier, arrived, decays)


def local_kernel(
    part, x_hbm, step_hbm, decay_hbm, inject_hbm, readout_hbm, gain_ref, out_hbm,
    x_buf, step_buf, decay_buf, inject_buf, readout_buf, out_buf, sem, in_sem, out_sem,
):
    decay_in, step_in, inject_in, readout_in = copies(
        (decay_hbm, decay_buf, sem.at[0]),
        (step_hbm, step_buf, sem.at[1]),
        (inject_hbm, inject_buf, sem.at[2]),
        (readout_hbm, readout_buf, sem.at[3]),
    )
    x_in = copies(
        *[
            (
                x_hbm.at[:, pl.ds(part * PART_COLS + n * GROUP_COLS, GROUP_COLS)],
                x_buf.at[n],
                in_sem.at[n],
            )
            for n in range(PART_GROUPS)
        ]
    )
    lower = iota((HALF, HALF), 0) >= iota((HALF, HALF), 1)
    lower_f = jnp.where(lower, 1.0, 0.0).astype(f32)
    decay_in.wait()
    cum_a = dot_exact(lower_f, decay_buf[:HALF])
    cum_b = dot_exact(lower_f, decay_buf[HALF:])
    mid = HALF // 2 - 1
    mid_b = cum_b[mid : mid + 1]
    gap_a = cum_a - cum_a[mid : mid + 1]
    gap_b = cum_b - mid_b
    onward = jnp.exp(mid_b + gap_a[HALF - 1 : HALF])
    few = iota((8, HEADS), 0)
    rows = jnp.where(few == 0, onward, gain_ref[...])
    step_in.wait()
    into_a = step_buf[:HALF] * jnp.exp(-gap_a)
    into_b = step_buf[HALF:] * jnp.exp(-gap_b)
    from_a = jnp.exp(gap_a)
    from_b = jnp.exp(gap_b)
    zero = jnp.zeros((HALF, HALF), f32)
    inject_in.wait()
    readout_in.wait()

    def pair(r, i):
        return lax.dot_general(r, i, (((1,), (1,)), ((), ())), preferred_element_type=f32)

    sent = []
    for n in range(PART_GROUPS):
        g = part * PART_GROUPS + n
        state_cols = slice(g * STATE, (g + 1) * STATE)
        inj_a = inject_buf[:HALF, state_cols]
        inj_b = inject_buf[HALF:, state_cols]
        read_a = readout_buf[:HALF, state_cols]
        read_b = readout_buf[HALF:, state_cols]
        near_a = jnp.where(lower, pair(read_a, inj_a), zero).astype(bf16)
        near_b = jnp.concatenate(
            [
                pair(read_b, inj_a).astype(bf16),
                jnp.where(lower, pair(read_b, inj_b), zero).astype(bf16),
            ],
            axis=1,
        )
        x_in[n].wait()
        for k in range(GROUP_COLS // WIDE):
            cols = slice(k * WIDE, (k + 1) * WIDE)
            at = g * GROUP_COLS + k * WIDE
            row = spread(rows, at, WIDE)
            gain = row[1:2]
            x_a = x_buf[n, :HALF, cols].astype(f32)
            x_b = x_buf[n, HALF:, cols].astype(f32)
            v_a = x_a * spread(into_a, at, WIDE)
            v_b = (x_b * spread(into_b, at, WIDE)).astype(bf16)
            res_a = dot(near_a, v_a.astype(bf16))
            res_b = dot(near_b, jnp.concatenate([(v_a * row[0:1]).astype(bf16), v_b], axis=0))
            out_a = res_a * spread(from_a, at, WIDE) + gain * x_a
            out_b = res_b * spread(from_b, at, WIDE) + gain * x_b
            out_buf[n, :HALF, cols] = out_a.astype(bf16)
            out_buf[n, HALF:, cols] = out_b.astype(bf16)
        sent += copies(
            (out_buf.at[n], out_hbm.at[:, pl.ds(g * GROUP_COLS, GROUP_COLS)], out_sem.at[n])
        )
    for c in sent:
        c.wait()


def local_of(part, x, step, decay, inject, readout, gain):
    hbm = pl.BlockSpec(memory_space=pltpu.HBM)
    vmem = pl.BlockSpec(memory_space=pltpu.VMEM)
    return pl.pallas_call(
        functools.partial(local_kernel, part),
        out_shape=jax.ShapeDtypeStruct(x.shape, bf16),
        in_specs=[hbm] * 5 + [vmem],
        out_specs=hbm,
        scratch_shapes=[
            pltpu.VMEM((PART_GROUPS, TOK, GROUP_COLS), bf16),
            pltpu.VMEM((TOK, HEADS), f32),
            pltpu.VMEM((TOK, HEADS), f32),
            pltpu.VMEM((TOK, GROUPS * STATE), bf16),
            pltpu.VMEM((TOK, GROUPS * STATE), bf16),
            pltpu.VMEM((PART_GROUPS, TOK, GROUP_COLS), bf16),
            pltpu.SemaphoreType.DMA((4,)),
            pltpu.SemaphoreType.DMA((PART_GROUPS,)),
            pltpu.SemaphoreType.DMA((PART_GROUPS,)),
        ],
        compiler_params=pltpu.CompilerParams(vmem_limit_bytes=VMEM_LIMIT),
        cost_estimate=pl.CostEstimate(
            flops=2_000_000_000, bytes_accessed=6_000_000, transcendentals=65536
        ),
        name=f"local{part}",
    )(x, step, decay, inject, readout, gain)


def out_kernel(part, decay_hbm, readout_hbm, held_ref, local_hbm, *rest):
    out_hbm, decay_buf, readout_buf, local_buf, out_buf, sem, local_sem, out_sem = rest[-8:]
    decay_in, readout_in = copies(
        (decay_hbm, decay_buf, sem.at[0]),
        (
            readout_hbm.at[:, pl.ds(part * PART_GROUPS * STATE, PART_GROUPS * STATE)],
            readout_buf,
            sem.at[1],
        ),
    )
    local_in = copies(
        *[
            (
                local_hbm.at[:, pl.ds(part * PART_COLS + n * GROUP_COLS, GROUP_COLS)],
                local_buf.at[n],
                local_sem.at[n],
            )
            for n in range(PART_GROUPS)
        ]
    )
    swap = swap_matrix()
    lower = jnp.where(iota((TOK, TOK), 0) >= iota((TOK, TOK), 1), 1.0, 0.0).astype(f32)
    decay_in.wait()
    lead = jnp.exp(dot_exact(lower, decay_buf[...]))
    readout_in.wait()
    sent = []
    for n in range(PART_GROUPS):
        g = part * PART_GROUPS + n
        first = n * GROUP_HEADS
        blocks = jnp.concatenate(
            [
                jnp.concatenate([held_ref[first + k], held_ref[first + k + 1]], axis=1)
                for k in range(0, GROUP_HEADS, 2)
            ],
            axis=0,
        )
        pairs = dot(blocks, swap).astype(bf16)
        readout = readout_buf[:, n * STATE : (n + 1) * STATE]
        local_in[n].wait()
        for k in range(GROUP_COLS // WIDE):
            cols = slice(k * WIDE, (k + 1) * WIDE)
            tiles = range(k * WIDE // LANES, (k + 1) * WIDE // LANES)
            held = jnp.concatenate(
                [
                    jnp.concatenate([pairs[i * ROWS : (i + 1) * ROWS, side] for i in tiles], axis=1)
                    for side in (slice(0, LANES), slice(LANES, 2 * LANES))
                ],
                axis=0,
            )
            far = dot(readout, held) * spread(lead, g * GROUP_COLS + k * WIDE, WIDE)
            out_buf[n, :, cols] = (far + local_buf[n, :, cols].astype(f32)).astype(bf16)
        sent += copies(
            (out_buf.at[n], out_hbm.at[:, pl.ds(g * GROUP_COLS, GROUP_COLS)], out_sem.at[n])
        )
    for c in sent:
        c.wait()


def outputs_of(part, so_far, decay, readout, held, local):
    hbm = pl.BlockSpec(memory_space=pltpu.HBM)
    vmem = pl.BlockSpec(memory_space=pltpu.VMEM)
    return pl.pallas_call(
        functools.partial(out_kernel, part),
        out_shape=jax.ShapeDtypeStruct((TOK, HEADS * HEAD_DIM), bf16),
        in_specs=[hbm, hbm, vmem, hbm] + [hbm] * len(so_far),
        out_specs=hbm,
        input_output_aliases={4: 0} if so_far else {},
        scratch_shapes=[
            pltpu.VMEM((TOK, HEADS), f32),
            pltpu.VMEM((TOK, PART_GROUPS * STATE), bf16),
            pltpu.VMEM((PART_GROUPS, TOK, GROUP_COLS), bf16),
            pltpu.VMEM((PART_GROUPS, TOK, GROUP_COLS), bf16),
            pltpu.SemaphoreType.DMA((2,)),
            pltpu.SemaphoreType.DMA((PART_GROUPS,)),
            pltpu.SemaphoreType.DMA((PART_GROUPS,)),
        ],
        compiler_params=pltpu.CompilerParams(vmem_limit_bytes=OUT_VMEM_LIMIT),
        cost_estimate=pl.CostEstimate(
            flops=1_000_000_000, bytes_accessed=6_000_000, transcendentals=32768
        ),
        name=f"outputs{part}",
    )(decay, readout, held, local, *so_far)


def later_by(v, shift, ways):
    return lax.ppermute(v, "seq", [(i, i + shift) for i in range(ways - shift)])


def exchange(v, devices):
    return lax.all_to_all(
        v,
        ("seq", "head"),
        split_axis=0,
        concat_axis=0,
        tiled=True,
        axis_index_groups=[
            list(range(first, first + OWNERS)) for first in range(0, devices, OWNERS)
        ],
    )


def shards(features, step_size, log_decay, inject, readout, skip_gain):
    ways = lax.axis_size("seq")
    devices = ways * lax.axis_size("head")
    args = (features, step_size, log_decay, inject, readout, skip_gain[None, :])

    def hold(part, arrived, decays):
        total = total_of(part, arrived, decays)
        earlier = [later_by(total, k * STEP, ways) for k in (1, 2, 3)]
        return held_of(part, earlier, arrived, decays)

    arrived_0 = exchange(states_of(0, features, step_size, log_decay, inject), devices)
    states_1 = states_of(1, features, step_size, log_decay, inject)
    local_0 = local_of(0, *args)
    arrived_0, states_1, local_0 = lax.optimization_barrier((arrived_0, states_1, local_0))
    arrived_1 = exchange(states_1, devices)
    held_0 = hold(0, arrived_0, arrived_0)
    arrived_1, held_0 = lax.optimization_barrier((arrived_1, held_0))
    back_0 = exchange(held_0, devices)
    held_1 = hold(1, arrived_1, arrived_0)
    back_0, held_1, args = lax.optimization_barrier((back_0, held_1, args))
    back_1 = exchange(held_1, devices)
    local_1 = local_of(1, *args)
    out = outputs_of(0, (), log_decay, readout, back_0, local_0)
    return outputs_of(1, (out,), log_decay, readout, back_1, local_1)


def solution(mesh):
    rows = P(("seq", "head"), None)
    return jax.shard_map(
        shards,
        mesh=mesh,
        in_specs=(rows, rows, rows, rows, rows, P()),
        out_specs=rows,
        check_vma=False,
    )
```

time: 102 us -> 109 us (1.069)
  starting transfers between devices: 29.5 us -> 55.4 us
  waiting for transfers between devices: 43.8 us -> 18.6 us
  Pallas kernels: 27.1 us -> 33.2 us
    all_to_all x2 -> x4, waiting for transfers between devices: 42.4 us -> 16.9 us  [exchange(): lax.all_to_all(v, ('seq', 'head'), split_axis=0, concat_axis=0, tiled=Tru...]
    all_to_all x2 -> x4, starting transfers between devices: 17.2 us -> 31.4 us  [exchange(): lax.all_to_all(v, ('seq', 'head'), split_axis=0, concat_axis=0, tiled=Tru...]
    ppermute x3 -> x6, starting transfers between devices: 12.3 us -> 24 us  [later_by(): return lax.ppermute(v, 'seq', [(i, i + shift) for i in range(ways - shift)])]
    pallas_call x4 -> x8, Pallas kernels: 13.7 us -> 19.8 us  [the longest x2 9.06 us: states_of(): pl.pallas_call(functools.partial(state_kernel, part), out_shape=jax.Shape...]
  transfers between devices with their start and end apart: 5 -> 10, of which waited for: 3 -> 6; matrix products, arithmetic and copies ran while one was open for 0% -> 0% of each run, Pallas kernels for 13% -> 23%
where the time goes in v2:
time: 109 us
  starting transfers between devices  55.4 us (51%)
  Pallas kernels  33.2 us (30%)
  waiting for transfers between devices  18.6 us (17%)
    all_to_all x4, starting transfers between devices, exchange(): lax.all_to_all(v, ('seq', 'head'), split_axis=0, concat_axis=0, tiled=Tru...  31.4 us
    ppermute x6, starting transfers between devices, later_by(): return lax.ppermute(v, 'seq', [(i, i + shift) for i in range(ways - shift)])  24 us
    all_to_all x4, waiting for transfers between devices, exchange(): lax.all_to_all(v, ('seq', 'head'), split_axis=0, concat_axis=0, tiled=Tru...  16.9 us
    pallas_call x2, Pallas kernels, local_of(): pl.pallas_call(functools.partial(local_kernel, part), out_shape=jax.Shape...  13.4 us
    pallas_call x2, Pallas kernels, states_of(): pl.pallas_call(functools.partial(state_kernel, part), out_shape=jax.Shape...  9.06 us
    pallas_call x2, Pallas kernels, outputs_of(): pl.pallas_call(functools.partial(out_kernel, part), out_shape=jax.ShapeDt...  8.61 us
  transfers between devices with their start and end apart: 10, of which 6 were waited for; matrix products, arithmetic and copies ran while one was open for 0% of the time, Pallas kernels for 23%

profile of v2, /device:TPU:1, one launch (start us, length us, event | category | flops | bytes accessed | tf_op | source)
XLA Modules:
  0.0 108.6 jit_solution(5925989954949671396)
XLA Ops:
  0.0 4.5 %states0.1 = bf16[64,72,128]{2,1,0:T(8,128)(2,1)} custom-call(bf16[256,8192]{1,0:T(8,128)(2,1)} %x_hbm.6, f32[256,128]{1,0:T(8,128)} %step_hbm.6, f32[256,128]{1,0:T(8,128)} %decay_hbm.10, bf16[256,1024]{1,0:T(8,128)(2,1)} %inject_hbm.6), custom_call_target="tpu_custom_call" | custom-call | flops 1000000000 | bytes 4000000 | tf_op jit(solution)/shard_map/states0/pallas_call | solution.py:150
  4.5 10.4 %all-to-all-start = ((bf16[64,72,128]{2,1,0:T(8,128)(2,1)}), bf16[64,72,128]{2,1,0:T(8,128)(2,1)S(1)}, u32[]{:S(2)}, u32[]{:S(2)}) async-start(bf16[64,72,128]{2,1,0:T(8,128)(2,1)} %states0.1), calls=%async_computation | async-start | bytes 2359296 | tf_op jit(solution)/shard_map/all_to_all | solution.py:434
  14.9 4.5 %states1.1 = bf16[64,64,128]{2,1,0:T(8,128)(2,1)} custom-call(bf16[256,8192]{1,0:T(8,128)(2,1)} %x_hbm.6, f32[256,128]{1,0:T(8,128)} %step_hbm.6, f32[256,128]{1,0:T(8,128)} %decay_hbm.10, bf16[256,1024]{1,0:T(8,128)(2,1)} %inject_hbm.6), custom_call_target="tpu_custom_call" | custom-call | flops 1000000000 | bytes 4000000 | tf_op jit(solution)/shard_map/states1/pallas_call | solution.py:150
  19.4 6.7 %local0.1.local_hbm = bf16[256,8192]{1,0:T(8,128)(2,1)} custom-call(bf16[256,8192]{1,0:T(8,128)(2,1)} %x_hbm.6, f32[256,128]{1,0:T(8,128)} %step_hbm.6, f32[256,128]{1,0:T(8,128)} %decay_hbm.10, bf16[256,1024]{1,0:T(8,128)(2,1)} %inject_hbm.6, bf16[256,1024]{1,0:T(8,128)(2,1)} %readout_hbm.6, f32[1,128]{1,0:T(1,128)} %bitcast.1), custom_call_target="tpu_custom_call" | custom-call | flops 2000000000 | bytes 6000000 | tf_op jit(solution)/shard_map/local0/pallas_call | solution.py:321
  26.1 7.0 %all-to-all-done.in_ref.decay_ref = bf16[64,72,128]{2,1,0:T(8,128)(2,1)S(1)} async-done(((bf16[64,72,128]{2,1,0:T(8,128)(2,1)}), bf16[64,72,128]{2,1,0:T(8,128)(2,1)S(1)}, u32[]{:S(2)}, u32[]{:S(2)}) %all-to-all-start) | async-done | bytes 1179680 | tf_op jit(solution)/shard_map/all_to_all | solution.py:434
  33.1 5.6 %all-to-all-start.1 = ((bf16[64,64,128]{2,1,0:T(8,128)(2,1)}), bf16[64,64,128]{2,1,0:T(8,128)(2,1)S(1)}, u32[]{:S(2)}, u32[]{:S(2)}) async-start(bf16[64,64,128]{2,1,0:T(8,128)(2,1)} %states1.1), calls=%async_computation.1 | async-start | bytes 2097152 | tf_op jit(solution)/shard_map/all_to_all | solution.py:434
  39.1 7.0 %collective-permute-start.2 = (bf16[72,128]{1,0:T(8,128)(2,1)S(1)}, bf16[72,128]{1,0:T(8,128)(2,1)S(1)}, u32[]{:S(2)}, u32[]{:S(2)}) collective-permute-start(bf16[72,128]{1,0:T(8,128)(2,1)S(1)} %total0.1), channel_id=1, source_target_pairs={{0,192},{16,208},{32,224},{48,240},{1,193},{17,209},{33,225},{49,2... | collective-permute-start | bytes 55304 | tf_op jit(solution)/shard_map/ppermute | solution.py:430
  46.1 1.6 %collective-permute-start.1 = (bf16[72,128]{1,0:T(8,128)(2,1)S(1)}, bf16[72,128]{1,0:T(8,128)(2,1)S(1)}, u32[]{:S(2)}, u32[]{:S(2)}) collective-permute-start(bf16[72,128]{1,0:T(8,128)(2,1)S(1)} %total0.1), channel_id=1, source_target_pairs={{0,128},{16,144},{32,160},{48,176},{64,192},{80,208},{96,224},{112... | collective-permute-start | bytes 55304 | tf_op jit(solution)/shard_map/ppermute | solution.py:430
  47.6 3.7 %collective-permute-start = (bf16[72,128]{1,0:T(8,128)(2,1)S(1)}, bf16[72,128]{1,0:T(8,128)(2,1)S(1)}, u32[]{:S(2)}, u32[]{:S(2)}) collective-permute-start(bf16[72,128]{1,0:T(8,128)(2,1)S(1)} %total0.1), channel_id=1, source_target_pairs={{0,64},{16,80},{32,96},{48,112},{64,128},{80,144},{96,160},{112,17... | collective-permute-start | bytes 55304 | tf_op jit(solution)/shard_map/ppermute | solution.py:430
  51.4 0.8 collective-permute-done.one_ref
  52.3 1.1 held0.1
  53.3 2.3 %all-to-all-done.1.in_ref = bf16[64,64,128]{2,1,0:T(8,128)(2,1)S(1)} async-done(((bf16[64,64,128]{2,1,0:T(8,128)(2,1)}), bf16[64,64,128]{2,1,0:T(8,128)(2,1)S(1)}, u32[]{:S(2)}, u32[]{:S(2)}) %all-to-all-start.1) | async-done | bytes 1048608 | tf_op jit(solution)/shard_map/all_to_all | solution.py:434
  55.6 8.0 %all-to-all-start.2 = ((bf16[64,64,128]{2,1,0:T(8,128)(2,1)}), bf16[64,64,128]{2,1,0:T(8,128)(2,1)}, u32[]{:S(2)}, u32[]{:S(2)}) async-start(bf16[64,64,128]{2,1,0:T(8,128)(2,1)} %held0.1), calls=%async_computation.2 | async-start | bytes 2097152 | tf_op jit(solution)/shard_map/all_to_all | solution.py:434
  63.9 6.4 %collective-permute-start.5 = (bf16[72,128]{1,0:T(8,128)(2,1)S(1)}, bf16[72,128]{1,0:T(8,128)(2,1)S(1)}, u32[]{:S(2)}, u32[]{:S(2)}) collective-permute-start(bf16[72,128]{1,0:T(8,128)(2,1)S(1)} %total1.1), channel_id=1, source_target_pairs={{0,192},{16,208},{32,224},{48,240},{1,193},{17,209},{33,225},{49,2... | collective-permute-start | bytes 55304 | tf_op jit(solution)/shard_map/ppermute | solution.py:430
  70.3 1.3 %collective-permute-start.4 = (bf16[72,128]{1,0:T(8,128)(2,1)S(1)}, bf16[72,128]{1,0:T(8,128)(2,1)S(1)}, u32[]{:S(2)}, u32[]{:S(2)}) collective-permute-start(bf16[72,128]{1,0:T(8,128)(2,1)S(1)} %total1.1), channel_id=1, source_target_pairs={{0,128},{16,144},{32,160},{48,176},{64,192},{80,208},{96,224},{112... | collective-permute-start | bytes 55304 | tf_op jit(solution)/shard_map/ppermute | solution.py:430
  71.6 4.0 %collective-permute-start.3 = (bf16[72,128]{1,0:T(8,128)(2,1)S(1)}, bf16[72,128]{1,0:T(8,128)(2,1)S(1)}, u32[]{:S(2)}, u32[]{:S(2)}) collective-permute-start(bf16[72,128]{1,0:T(8,128)(2,1)S(1)} %total1.1), channel_id=1, source_target_pairs={{0,64},{16,80},{32,96},{48,112},{64,128},{80,144},{96,160},{112,17... | collective-permute-start | bytes 55304 | tf_op jit(solution)/shard_map/ppermute | solution.py:430
  75.6 0.8 collective-permute-done.3.one_ref
  76.9 1.0 copy-done.4
  77.8 2.5 %all-to-all-done.2.held_ref = bf16[64,64,128]{2,1,0:T(8,128)(2,1)} async-done(((bf16[64,64,128]{2,1,0:T(8,128)(2,1)}), bf16[64,64,128]{2,1,0:T(8,128)(2,1)}, u32[]{:S(2)}, u32[]{:S(2)}) %all-to-all-start.2) | async-done | bytes 1048608 | tf_op jit(solution)/shard_map/all_to_all | solution.py:434
  80.3 7.5 %all-to-all-start.3 = ((bf16[64,64,128]{2,1,0:T(8,128)(2,1)}), bf16[64,64,128]{2,1,0:T(8,128)(2,1)S(1)}, u32[]{:S(2)}, u32[]{:S(2)}) async-start(bf16[64,64,128]{2,1,0:T(8,128)(2,1)} %copy-done.4), calls=%async_computation.3 | async-start | bytes 2097152 | tf_op jit(solution)/shard_map/all_to_all | solution.py:434
  87.8 4.9 %outputs0.1.rest_0_ = bf16[256,8192]{1,0:T(8,128)(2,1)} custom-call(f32[256,128]{1,0:T(8,128)S(1)} %copy-done.2, bf16[256,1024]{1,0:T(8,128)(2,1)S(1)} %copy-done, bf16[64,64,128]{2,1,0:T(8,128)(2,1)} %all-to-all-done.2.held_ref, bf16[256,8192]{1,0:T(8,128)(2,1)} %local0.1.local_hbm), custom_call_target="tpu_custom_call" | custom-call | flops 1000000000 | bytes 6000000 | tf_op jit(solution)/shard_map/outputs0/pallas_call | solution.py:406
  92.7 6.7 %local1.1.local_hbm = bf16[256,8192]{1,0:T(8,128)(2,1)} custom-call(bf16[256,8192]{1,0:T(8,128)(2,1)} %x_hbm.6, f32[256,128]{1,0:T(8,128)} %step_hbm.6, f32[256,128]{1,0:T(8,128)} %decay_hbm.10, bf16[256,1024]{1,0:T(8,128)(2,1)} %inject_hbm.6, bf16[256,1024]{1,0:T(8,128)(2,1)} %readout_hbm.6, f32[1,128]{1,0:T(1,128)} %bitcast.2), custom_call_target="tpu_custom_call" | custom-call | flops 2000000000 | bytes 6000000 | tf_op jit(solution)/shard_map/local1/pallas_call | solution.py:321
  99.5 5.2 %all-to-all-done.3.held_ref = bf16[64,64,128]{2,1,0:T(8,128)(2,1)S(1)} async-done(((bf16[64,64,128]{2,1,0:T(8,128)(2,1)}), bf16[64,64,128]{2,1,0:T(8,128)(2,1)S(1)}, u32[]{:S(2)}, u32[]{:S(2)}) %all-to-all-start.3) | async-done | bytes 1048608 | tf_op jit(solution)/shard_map/all_to_all | solution.py:434
  104.7 3.7 %outputs1.1 = bf16[256,8192]{1,0:T(8,128)(2,1)} custom-call(f32[256,128]{1,0:T(8,128)S(1)} %copy-done.3, bf16[256,1024]{1,0:T(8,128)(2,1)S(1)} %copy-done.1, bf16[64,64,128]{2,1,0:T(8,128)(2,1)S(1)} %all-to-all-done.3.held_ref, bf16[256,8192]{1,0:T(8,128)(2,1)} %local1.1.local_hbm, bf16[256,8192]{1,0:T(8,128)(2,1)} %outputs0.1.rest_0_), custom_call_target="tpu_custom_call", output_to_operand_aliasing={{}: (4, {})} | custom-call | flops 1000000000 | bytes 6000000 | tf_op jit(solution)/shard_map/outputs1/pallas_call | solution.py:406
  (16 shorter events, 1.1 us)
Async XLA Ops:
  4.5 28.5 %all-to-all-start = ((bf16[64,72,128]{2,1,0:T(8,128)(2,1)}), bf16[64,72,128]{2,1,0:T(8,128)(2,1)S(1)}, u32[]{:S(2)}, u32[]{:S(2)}) async-start(bf16[64,72,128]{2,1,0:T(8,128)(2,1)} %states0.1), calls=%async_computation | async-start | bytes 2359296 | tf_op jit(solution)/shard_map/all_to_all | solution.py:434
  33.1 22.5 %all-to-all-start.1 = ((bf16[64,64,128]{2,1,0:T(8,128)(2,1)}), bf16[64,64,128]{2,1,0:T(8,128)(2,1)S(1)}, u32[]{:S(2)}, u32[]{:S(2)}) async-start(bf16[64,64,128]{2,1,0:T(8,128)(2,1)} %states1.1), calls=%async_computation.1 | async-start | bytes 2097152 | tf_op jit(solution)/shard_map/all_to_all | solution.py:434
  39.1 12.3 %collective-permute-start.2 = (bf16[72,128]{1,0:T(8,128)(2,1)S(1)}, bf16[72,128]{1,0:T(8,128)(2,1)S(1)}, u32[]{:S(2)}, u32[]{:S(2)}) collective-permute-start(bf16[72,128]{1,0:T(8,128)(2,1)S(1)} %total0.1), channel_id=1, source_target_pairs={{0,192},{16,208},{32,224},{48,240},{1,193},{17,209},{33,225},{49,2... | collective-permute-start | bytes 55304 | tf_op jit(solution)/shard_map/ppermute | solution.py:430
  46.1 5.3 %collective-permute-start.1 = (bf16[72,128]{1,0:T(8,128)(2,1)S(1)}, bf16[72,128]{1,0:T(8,128)(2,1)S(1)}, u32[]{:S(2)}, u32[]{:S(2)}) collective-permute-start(bf16[72,128]{1,0:T(8,128)(2,1)S(1)} %total0.1), channel_id=1, source_target_pairs={{0,128},{16,144},{32,160},{48,176},{64,192},{80,208},{96,224},{112... | collective-permute-start | bytes 55304 | tf_op jit(solution)/shard_map/ppermute | solution.py:430
  47.6 4.6 %collective-permute-start = (bf16[72,128]{1,0:T(8,128)(2,1)S(1)}, bf16[72,128]{1,0:T(8,128)(2,1)S(1)}, u32[]{:S(2)}, u32[]{:S(2)}) collective-permute-start(bf16[72,128]{1,0:T(8,128)(2,1)S(1)} %total0.1), channel_id=1, source_target_pairs={{0,64},{16,80},{32,96},{48,112},{64,128},{80,144},{96,160},{112,17... | collective-permute-start | bytes 55304 | tf_op jit(solution)/shard_map/ppermute | solution.py:430
  55.6 24.7 %all-to-all-start.2 = ((bf16[64,64,128]{2,1,0:T(8,128)(2,1)}), bf16[64,64,128]{2,1,0:T(8,128)(2,1)}, u32[]{:S(2)}, u32[]{:S(2)}) async-start(bf16[64,64,128]{2,1,0:T(8,128)(2,1)} %held0.1), calls=%async_computation.2 | async-start | bytes 2097152 | tf_op jit(solution)/shard_map/all_to_all | solution.py:434
  63.5 24.3 %copy-start = (bf16[256,1024]{1,0:T(8,128)(2,1)S(1)}, bf16[256,1024]{1,0:T(8,128)(2,1)}, u32[]{:S(2)}) copy-start(bf16[256,1024]{1,0:T(8,128)(2,1)} %readout_hbm.6) | copy-start | bytes 1572868
  63.6 24.3 %copy-start.2 = (f32[256,128]{1,0:T(8,128)S(1)}, f32[256,128]{1,0:T(8,128)}, u32[]{:S(2)}) copy-start(f32[256,128]{1,0:T(8,128)} %decay_hbm.10) | copy-start | bytes 393220
  63.9 11.7 %collective-permute-start.5 = (bf16[72,128]{1,0:T(8,128)(2,1)S(1)}, bf16[72,128]{1,0:T(8,128)(2,1)S(1)}, u32[]{:S(2)}, u32[]{:S(2)}) collective-permute-start(bf16[72,128]{1,0:T(8,128)(2,1)S(1)} %total1.1), channel_id=1, source_target_pairs={{0,192},{16,208},{32,224},{48,240},{1,193},{17,209},{33,225},{49,2... | collective-permute-start | bytes 55304 | tf_op jit(solution)/shard_map/ppermute | solution.py:430
  70.3 5.3 %collective-permute-start.4 = (bf16[72,128]{1,0:T(8,128)(2,1)S(1)}, bf16[72,128]{1,0:T(8,128)(2,1)S(1)}, u32[]{:S(2)}, u32[]{:S(2)}) collective-permute-start(bf16[72,128]{1,0:T(8,128)(2,1)S(1)} %total1.1), channel_id=1, source_target_pairs={{0,128},{16,144},{32,160},{48,176},{64,192},{80,208},{96,224},{112... | collective-permute-start | bytes 55304 | tf_op jit(solution)/shard_map/ppermute | solution.py:430
  71.6 4.9 %collective-permute-start.3 = (bf16[72,128]{1,0:T(8,128)(2,1)S(1)}, bf16[72,128]{1,0:T(8,128)(2,1)S(1)}, u32[]{:S(2)}, u32[]{:S(2)}) collective-permute-start(bf16[72,128]{1,0:T(8,128)(2,1)S(1)} %total1.1), channel_id=1, source_target_pairs={{0,64},{16,80},{32,96},{48,112},{64,128},{80,144},{96,160},{112,17... | collective-permute-start | bytes 55304 | tf_op jit(solution)/shard_map/ppermute | solution.py:430
  76.8 1.0 copy-start.4
  80.3 24.4 %all-to-all-start.3 = ((bf16[64,64,128]{2,1,0:T(8,128)(2,1)}), bf16[64,64,128]{2,1,0:T(8,128)(2,1)S(1)}, u32[]{:S(2)}, u32[]{:S(2)}) async-start(bf16[64,64,128]{2,1,0:T(8,128)(2,1)} %copy-done.4), calls=%async_computation.3 | async-start | bytes 2097152 | tf_op jit(solution)/shard_map/all_to_all | solution.py:434
  92.7 12.0 %copy-start.1 = (bf16[256,1024]{1,0:T(8,128)(2,1)S(1)}, bf16[256,1024]{1,0:T(8,128)(2,1)}, u32[]{:S(2)}) copy-start(bf16[256,1024]{1,0:T(8,128)(2,1)} %readout_hbm.6) | copy-start | bytes 1572868
  92.7 12.0 %copy-start.3 = (f32[256,128]{1,0:T(8,128)S(1)}, f32[256,128]{1,0:T(8,128)}, u32[]{:S(2)}) copy-start(f32[256,128]{1,0:T(8,128)} %decay_hbm.10) | copy-start | bytes 393220

commit v3 on v1

--- a/solution.py
+++ b/solution.py
@@ -16,6 +16,8 @@
 LANES = 128
 OWNERS = 64
 STEP = 4
+SPANS = 4
+PIECES = 4
 OWN_HEADS = HEADS // OWNERS
 COLS = OWN_HEADS * HEAD_DIM
 GROUP_COLS = HEADS // GROUPS * HEAD_DIM
@@ -23,9 +25,10 @@
 ROWS = STATE + 8
 VMEM_LIMIT = 61 * 1024 * 1024
 OUT_VMEM_LIMIT = 50 * 1024 * 1024
-HELD_VMEM_LIMIT = 40 * 1024 * 1024
+HELD_VMEM_LIMIT = 52 * 1024 * 1024
 SMALL_VMEM_LIMIT = 24 * 1024 * 1024
 WIDE = 512
+NARROW = 256
 LOCAL_PARTS = 2
 PART_GROUPS = GROUPS // LOCAL_PARTS
 PART_COLS = PART_GROUPS * GROUP_COLS
@@ -38,8 +41,13 @@
     return jnp.dot(a, b, preferred_element_type=f32)
 
 
-def dot_exact(a, b):
-    return jnp.dot(a, b, preferred_element_type=f32, precision=lax.Precision.HIGHEST)
+def sums(mask, v):
+    high = v.astype(bf16)
+    rest = v - high.astype(f32)
+    middle = rest.astype(bf16)
+    low = (rest - middle.astype(f32)).astype(bf16)
+    p = dot(mask.astype(bf16), jnp.concatenate([high, middle, low], axis=1))
+    return p[:, :HEADS] + p[:, HEADS : 2 * HEADS] + p[:, 2 * HEADS :]
 
 
 def iota(shape, axis):
@@ -69,7 +77,7 @@
 
 def state_kernel(
     x_hbm, step_hbm, decay_hbm, inject_hbm, out_hbm,
-    x_buf, step_buf, decay_buf, inject_buf, out_buf, sem, in_sem, out_sem,
+    x_buf, step_buf, decay_buf, inject_buf, turned_buf, v_buf, out_buf, sem, in_sem, out_sem,
 ):
     decay_in, step_in, inject_in = copies(
         (decay_hbm, decay_buf, sem.at[0]),
@@ -85,7 +93,7 @@
     later = jnp.where(iota((TOK, TOK), 1) > iota((TOK, TOK), 0), 1.0, 0.0).astype(f32)
     decay_in.wait()
     decay = decay_buf[...]
-    tail = dot_exact(later, decay)
+    tail = sums(later, decay)
     whole = jnp.broadcast_to(jnp.exp(tail[0:1] + decay[0:1]), (8, HEADS))
     high = whole.astype(bf16).astype(f32)
     row = iota((8, HEADS), 0)
@@ -93,26 +101,31 @@
     step_in.wait()
     scale = step_buf[...] * jnp.exp(tail)
     inject_in.wait()
+    for g in range(GROUPS):
+        turned_buf[g] = inject_buf[:, g * STATE : (g + 1) * STATE].T
     sent = []
-    for g in range(GROUPS):
-        at = g * GROUP_COLS
-        weight = spread(scale, at, GROUP_COLS)
-        below = spread(extra, at, GROUP_COLS).astype(bf16)
-        x_in[g].wait()
-        v = (x_buf[g].astype(f32) * weight).astype(bf16)
-        s = lax.dot_general(
-            inject_buf[:, g * STATE : (g + 1) * STATE],
-            v,
-            (((0,), (0,)), ((), ())),
-            preferred_element_type=f32,
-        ).astype(bf16)
-        first = g * GROUP_OWNERS
-        for k in range(GROUP_OWNERS):
-            cols = slice(k * COLS, (k + 1) * COLS)
-            out_buf[first + k, :STATE, :] = s[:, cols]
-            out_buf[first + k, STATE:, :] = below[:, cols]
-        span = pl.ds(first, GROUP_OWNERS)
-        sent += copies((out_buf.at[span], out_hbm.at[span], out_sem.at[g]))
+    for g in range(GROUPS + 1):
+        if g < GROUPS:
+            if g % 2 == 0:
+                x_in[g].wait()
+                x_in[g + 1].wait()
+        first = (g - 1) * GROUP_OWNERS
+        for w in range(GROUP_COLS // NARROW):
+            part = slice(w * NARROW, (w + 1) * NARROW)
+            if g < GROUPS:
+                weight = spread(scale, g * GROUP_COLS + w * NARROW, NARROW)
+                v_buf[g % 2, :, part] = (x_buf[g, :, part].astype(f32) * weight).astype(bf16)
+            if g > 0:
+                s = dot(turned_buf[g - 1], v_buf[(g - 1) % 2, :, part]).astype(bf16)
+                below = spread(extra, (g - 1) * GROUP_COLS + w * NARROW, NARROW).astype(bf16)
+                for k in range(NARROW // COLS):
+                    cols = slice(k * COLS, (k + 1) * COLS)
+                    owner = first + w * (NARROW // COLS) + k
+                    out_buf[owner, :STATE, :] = s[:, cols]
+                    out_buf[owner, STATE:, :] = below[:, cols]
+        if g > 0:
+            span = pl.ds(first, GROUP_OWNERS)
+            sent += copies((out_buf.at[span], out_hbm.at[span], out_sem.at[g - 1]))
     for c in sent:
         c.wait()
 
@@ -129,6 +142,8 @@
             pltpu.VMEM((TOK, HEADS), f32),
             pltpu.VMEM((TOK, HEADS), f32),
             pltpu.VMEM((TOK, GROUPS * STATE), bf16),
+            pltpu.VMEM((GROUPS, STATE, TOK), bf16),
+            pltpu.VMEM((2, TOK, GROUP_COLS), bf16),
             pltpu.VMEM((OWNERS, ROWS, COLS), bf16),
             pltpu.SemaphoreType.DMA((3,)),
             pltpu.SemaphoreType.DMA((GROUPS,)),
@@ -152,67 +167,83 @@
     return jnp.where(row == 0, high, jnp.where(row == 1, decay - high, 0.0)).astype(bf16)
 
 
-def total_kernel(in_ref, out_ref):
+def total_kernel(place_ref, in_ref, out_ref):
     state = in_ref[0, :STATE, :].astype(f32)
     decay = decay_row(in_ref[0])
     for i in range(1, OWNERS):
         d = decay_row(in_ref[i])
         state = state * d + in_ref[i, :STATE, :].astype(f32)
         decay = decay * d
-    out_ref[:STATE, :] = state.astype(bf16)
-    out_ref[STATE:, :] = pack_rows(decay)
-
-
-def held_kernel(one_ref, two_ref, three_ref, in_ref, out_hbm, out_buf, sem):
-    state = three_ref[:STATE, :].astype(f32)
-    for ref in (two_ref, one_ref):
-        state = ref[:STATE, :].astype(f32) + decay_row(ref[...]) * state
+    rows = pack_rows(decay).astype(f32)
+    same = jnp.where(iota((8, COLS), 0) == 0, 1.0, 0.0)
+    for k in range(SPANS):
+        later = place_ref[0] < k
+        out_ref[k, :STATE, :] = jnp.where(later, state, 0.0).astype(bf16)
+        out_ref[k, STATE:, :] = jnp.where(later, rows, same).astype(bf16)
+
+
+def held_kernel(earlier_ref, in_hbm, out_hbm, in_buf, out_buf, in_sem, out_sem):
+    size = OWNERS // PIECES
+    spans = [pl.ds(i * size, size) for i in range(PIECES)]
+    arrive = copies(*[(in_hbm.at[p], in_buf.at[p], in_sem.at[i]) for i, p in enumerate(spans)])
+    state = jnp.zeros((STATE, COLS), f32)
+    for k in range(SPANS - 1):
+        state = earlier_ref[k, :STATE, :].astype(f32) + decay_row(earlier_ref[k]) * state
     sent = []
     for i in range(OWNERS):
+        if i % size == 0:
+            arrive[i // size].wait()
         out_buf[i] = state.astype(bf16)
-        if (i + 1) % GROUPS == 0:
-            span = pl.ds(i + 1 - GROUPS, GROUPS)
-            sent += copies((out_buf.at[span], out_hbm.at[span], sem.at[i // GROUPS]))
+        if (i + 1) % size == 0:
+            p = spans[i // size]
+            sent += copies((out_buf.at[p], out_hbm.at[p], out_sem.at[i // size]))
         if i + 1 < OWNERS:
-            state = state * decay_row(in_ref[i]) + in_ref[i, :STATE, :].astype(f32)
+            state = state * decay_row(in_buf[i]) + in_buf[i, :STATE, :].astype(f32)
     for c in sent:
         c.wait()
 
 
-def total_of(arrived):
+def total_of(place, arrived):
     return pl.pallas_call(
         total_kernel,
-        out_shape=jax.ShapeDtypeStruct((ROWS, COLS), bf16),
+        out_shape=jax.ShapeDtypeStruct((SPANS, ROWS, COLS), bf16),
+        in_specs=[
+            pl.BlockSpec(memory_space=pltpu.SMEM),
+            pl.BlockSpec(memory_space=pltpu.VMEM),
+        ],
         compiler_params=pltpu.CompilerParams(vmem_limit_bytes=SMALL_VMEM_LIMIT),
         cost_estimate=pl.CostEstimate(flops=4_000_000, bytes_accessed=2_000_000, transcendentals=0),
         name="total",
-    )(arrived)
+    )(place, arrived)
 
 
 def held_of(earlier, arrived):
-    vmem = pl.BlockSpec(memory_space=pltpu.VMEM)
+    hbm = pl.BlockSpec(memory_space=pltpu.HBM)
     return pl.pallas_call(
         held_kernel,
         out_shape=jax.ShapeDtypeStruct((OWNERS, STATE, COLS), bf16),
-        in_specs=[vmem] * 4,
-        out_specs=pl.BlockSpec(memory_space=pltpu.HBM),
+        in_specs=[pl.BlockSpec(memory_space=pltpu.VMEM), hbm],
+        out_specs=hbm,
         scratch_shapes=[
+            pltpu.VMEM((OWNERS, ROWS, COLS), bf16),
             pltpu.VMEM((OWNERS, STATE, COLS), bf16),
-            pltpu.SemaphoreType.DMA((OWNERS // GROUPS,)),
+            pltpu.SemaphoreType.DMA((PIECES,)),
+            pltpu.SemaphoreType.DMA((PIECES,)),
         ],
         compiler_params=pltpu.CompilerParams(vmem_limit_bytes=HELD_VMEM_LIMIT),
         cost_estimate=pl.CostEstimate(flops=4_000_000, bytes_accessed=4_000_000, transcendentals=0),
         name="held",
-    )(*earlier, arrived)
+    )(earlier, arrived)
 
 
 def local_kernel(
     part, x_hbm, step_hbm, decay_hbm, inject_hbm, readout_hbm, gain_ref, *rest
 ):
-    (
-        out_hbm, x_buf, step_buf, decay_buf, inject_buf, readout_buf, out_buf,
-        sem, in_sem, out_sem,
-    ) = rest[-10:]
+    if part == 0:
+        out_hbm, lead_ref = rest[:2]
+    else:
+        out_hbm = rest[1]
+    x_buf, step_buf, decay_buf, inject_buf, readout_buf, out_buf, sem, in_sem, out_sem = rest[2:]
     decay_in, step_in, inject_in, readout_in = copies(
         (decay_hbm, decay_buf, sem.at[0]),
         (step_hbm, step_buf, sem.at[1]),
@@ -232,8 +263,11 @@
     lower = iota((HALF, HALF), 0) >= iota((HALF, HALF), 1)
     lower_f = jnp.where(lower, 1.0, 0.0).astype(f32)
     decay_in.wait()
-    cum_a = dot_exact(lower_f, decay_buf[:HALF])
-    cum_b = dot_exact(lower_f, decay_buf[HALF:])
+    cum_a = sums(lower_f, decay_buf[:HALF])
+    cum_b = sums(lower_f, decay_buf[HALF:])
+    if part == 0:
+        lead_ref[:HALF] = jnp.exp(cum_a)
+        lead_ref[HALF:] = jnp.exp(cum_b + cum_a[HALF - 1 : HALF])
     mid = HALF // 2 - 1
     mid_b = cum_b[mid : mid + 1]
     gap_a = cum_a - cum_a[mid : mid + 1]
@@ -297,10 +331,11 @@
     vmem = pl.BlockSpec(memory_space=pltpu.VMEM)
     return pl.pallas_call(
         functools.partial(local_kernel, part),
-        out_shape=jax.ShapeDtypeStruct(x.shape, bf16),
+        out_shape=[jax.ShapeDtypeStruct(x.shape, bf16)]
+        + ([] if so_far else [jax.ShapeDtypeStruct((TOK, HEADS), f32)]),
         in_specs=[hbm] * 5 + [vmem] + [hbm] * len(so_far),
         input_output_aliases={6: 0} if so_far else {},
-        out_specs=hbm,
+        out_specs=[hbm] if so_far else [hbm, vmem],
         scratch_shapes=[
             pltpu.VMEM((PART_GROUPS, TOK, GROUP_COLS), bf16),
             pltpu.VMEM((TOK, HEADS), f32),
@@ -321,69 +356,66 @@
 
 
 def out_kernel(
-    decay_hbm, readout_hbm, held_ref, local_hbm, out_hbm,
-    decay_buf, readout_buf, local_buf, out_buf, sem, local_sem, out_sem,
+    lead_ref, readout_ref, held_ref, local_hbm, out_hbm, far_buf, local_buf, out_buf, local_sem, out_sem
 ):
-    decay_in, readout_in = copies(
-        (decay_hbm, decay_buf, sem.at[0]), (readout_hbm, readout_buf, sem.at[1])
-    )
     local_in = copies(
         *[
             (local_hbm.at[:, pl.ds(g * GROUP_COLS, GROUP_COLS)], local_buf.at[g], local_sem.at[g])
             for g in range(GROUPS)
         ]
     )
-    lower = jnp.where(iota((TOK, TOK), 0) >= iota((TOK, TOK), 1), 1.0, 0.0).astype(f32)
-    decay_in.wait()
-    lead = jnp.exp(dot_exact(lower, decay_buf[...]))
-    readout_in.wait()
     sent = []
-    for g in range(GROUPS):
-        readout = readout_buf[:, g * STATE : (g + 1) * STATE]
-        local_in[g].wait()
-        for k in range(GROUP_COLS // WIDE):
-            cols = slice(k * WIDE, (k + 1) * WIDE)
-            at = g * GROUP_COLS + k * WIDE
-            first = at // COLS
+    for g in range(GROUPS + 1):
+        if g > 0:
+            local_in[g - 1].wait()
+        if g < GROUPS:
             held = jnp.concatenate(
-                [held_ref[first + i] for i in range(WIDE // COLS)], axis=1
+                [held_ref[g * GROUP_OWNERS + i] for i in range(GROUP_OWNERS)], axis=1
             )
-            out = dot(readout, held) * spread(lead, at, WIDE) + local_buf[g, :, cols].astype(f32)
-            out_buf[g, :, cols] = out.astype(bf16)
-        sent += copies(
-            (out_buf.at[g], out_hbm.at[:, pl.ds(g * GROUP_COLS, GROUP_COLS)], out_sem.at[g])
-        )
+            far_buf[g % 2] = dot(readout_ref[:, g * STATE : (g + 1) * STATE], held)
+        if g > 0:
+            at = (g - 1) * GROUP_COLS
+            far = far_buf[(g - 1) % 2] * spread(lead_ref[...], at, GROUP_COLS)
+            out_buf[g - 1] = (far + local_buf[g - 1].astype(f32)).astype(bf16)
+            sent += copies(
+                (out_buf.at[g - 1], out_hbm.at[:, pl.ds(at, GROUP_COLS)], out_sem.at[g - 1])
+            )
     for c in sent:
         c.wait()
 
 
-def outputs_of(decay, readout, held, local):
+def outputs_of(lead, readout, held, local):
     hbm = pl.BlockSpec(memory_space=pltpu.HBM)
     vmem = pl.BlockSpec(memory_space=pltpu.VMEM)
     return pl.pallas_call(
         out_kernel,
         out_shape=jax.ShapeDtypeStruct((TOK, HEADS * HEAD_DIM), bf16),
-        in_specs=[hbm, hbm, vmem, hbm],
+        in_specs=[vmem, vmem, vmem, hbm],
         out_specs=hbm,
         scratch_shapes=[
-            pltpu.VMEM((TOK, HEADS), f32),
-            pltpu.VMEM((TOK, GROUPS * STATE), bf16),
+            pltpu.VMEM((2, TOK, GROUP_COLS), f32),
             pltpu.VMEM((GROUPS, TOK, GROUP_COLS), bf16),
             pltpu.VMEM((GROUPS, TOK, GROUP_COLS), bf16),
-            pltpu.SemaphoreType.DMA((2,)),
             pltpu.SemaphoreType.DMA((GROUPS,)),
             pltpu.SemaphoreType.DMA((GROUPS,)),
         ],
         compiler_params=pltpu.CompilerParams(vmem_limit_bytes=OUT_VMEM_LIMIT),
         cost_estimate=pl.CostEstimate(
-            flops=2_000_000_000, bytes_accessed=12_000_000, transcendentals=32768
+            flops=2_000_000_000, bytes_accessed=12_000_000, transcendentals=0
         ),
         name="outputs",
-    )(decay, readout, held, local)
-
-
-def later_by(v, shift, ways):
-    return lax.ppermute(v, "seq", [(i, i + shift) for i in range(ways - shift)])
+    )(lead, readout, held, local)
+
+
+def across(v, ways):
+    return lax.all_to_all(
+        v,
+        "seq",
+        split_axis=0,
+        concat_axis=0,
+        tiled=True,
+        axis_index_groups=[list(range(i, ways, STEP)) for i in range(STEP)],
+    )
 
 
 def exchange(v, devices):
@@ -404,14 +436,14 @@
     devices = ways * lax.axis_size("head")
     args = (features, step_size, log_decay, inject, readout, skip_gain[None, :])
     arrived = exchange(states_of(features, step_size, log_decay, inject), devices)
-    local = local_of(0, (), *args)
-    arrived, local = lax.optimization_barrier((arrived, local))
-    total = total_of(arrived)
-    earlier = [later_by(total, k * STEP, ways) for k in (1, 2, 3)]
+    local, lead = local_of(0, (), *args)
+    arrived, local, lead = lax.optimization_barrier((arrived, local, lead))
+    place = (lax.axis_index("seq") // STEP).astype(jnp.int32)[None]
+    earlier = across(total_of(place, arrived), ways)
     held = held_of(earlier, arrived)
     held = exchange(held, devices)
-    local = local_of(1, (local,), *args)
-    return outputs_of(log_decay, readout, held, local)
+    (local,) = local_of(1, (local,), *args)
+    return outputs_of(lead, readout, held, local)
 
 
 def solution(mesh):

time: 102 us -> 104 us (1.020)
  blocking collectives: 0 us -> 14.8 us
  starting transfers between devices: 29.5 us -> 18 us
  waiting for transfers between devices: 43.8 us -> 41.8 us
  Pallas kernels: 27.1 us -> 28.7 us
  local copies, waits for them, and re-layouts: 1.33 us -> 0.01 us
    all_to_all x0 -> x1, blocking collectives: none -> 14.8 us  [across(): lax.all_to_all(v, 'seq', split_axis=0, concat_axis=0, tiled=True, axis_in...]
    ppermute x3 -> x0, starting transfers between devices: 12.3 us -> none  [later_by(): return lax.ppermute(v, 'seq', [(i, i + shift) for i in range(ways - shift)])]
    pallas_call x1, Pallas kernels: 0.79 us -> 2.6 us  [held_of(): pl.pallas_call(held_kernel, out_shape=jax.ShapeDtypeStruct((OWNERS, STATE...]
    ppermute x3 -> x0, waiting for transfers between devices: 1.39 us -> none  [later_by(): return lax.ppermute(v, 'seq', [(i, i + shift) for i in range(ways - shift)])]
    unnamed x6, local copies, waits for them, and re-layouts: 1.33 us -> 0.01 us
  transfers between devices with their start and end apart: 5 -> 2, of which waited for: 3 -> 2; matrix products, arithmetic and copies ran while one was open for 0% -> 0% of each run, Pallas kernels for 13% -> 14%
where the time goes in v3:
time: 104 us
  waiting for transfers between devices  41.8 us (40%)
  Pallas kernels  28.7 us (28%)
  starting transfers between devices  18 us (17%)
  blocking collectives  14.8 us (14%)
    all_to_all x2, waiting for transfers between devices, exchange(): lax.all_to_all(v, ('seq', 'head'), split_axis=0, concat_axis=0, tiled=Tru...  41.8 us
    all_to_all x2, starting transfers between devices, exchange(): lax.all_to_all(v, ('seq', 'head'), split_axis=0, concat_axis=0, tiled=Tru...  18 us
    all_to_all x1, blocking collectives, across(): lax.all_to_all(v, 'seq', split_axis=0, concat_axis=0, tiled=True, axis_in...  14.8 us
    pallas_call x2, Pallas kernels, local_of(): pl.pallas_call(functools.partial(local_kernel, part), out_shape=[jax.Shap...  14 us
    pallas_call x1, Pallas kernels, states_of(): pl.pallas_call(state_kernel, out_shape=jax.ShapeDtypeStruct((OWNERS, ROWS...  6.46 us
    pallas_call x1, Pallas kernels, outputs_of(): pl.pallas_call(out_kernel, out_shape=jax.ShapeDtypeStruct((TOK, HEADS * H...  5.12 us
    pallas_call x1, Pallas kernels, held_of(): pl.pallas_call(held_kernel, out_shape=jax.ShapeDtypeStruct((OWNERS, STATE...  2.6 us
  transfers between devices with their start and end apart: 2, of which 2 were waited for; matrix products, arithmetic and copies ran while one was open for 0% of the time, Pallas kernels for 14%

profile of v3, /device:TPU:1, one launch (start us, length us, event | category | flops | bytes accessed | tf_op | source)
XLA Modules:
  0.0 103.6 jit_solution(16821428190973908754)
XLA Ops:
  0.0 6.5 %states.1 = bf16[64,136,128]{2,1,0:T(8,128)(2,1)} custom-call(bf16[256,8192]{1,0:T(8,128)(2,1)} %x_hbm.5, f32[256,128]{1,0:T(8,128)} %step_hbm.5, f32[256,128]{1,0:T(8,128)} %decay_hbm.5, bf16[256,1024]{1,0:T(8,128)(2,1)} %inject_hbm.5), custom_call_target="tpu_custom_call" | custom-call | flops 2000000000 | bytes 8000000 | tf_op jit(solution)/shard_map/states/pallas_call | solution.py:135
  6.5 10.4 %all-to-all-start = ((bf16[64,136,128]{2,1,0:T(8,128)(2,1)}), bf16[64,136,128]{2,1,0:T(8,128)(2,1)S(1)}, u32[]{:S(2)}, u32[]{:S(2)}) async-start(bf16[64,136,128]{2,1,0:T(8,128)(2,1)} %states.1), calls=%async_computation | async-start | bytes 4456448 | tf_op jit(solution)/shard_map/all_to_all | solution.py:422
  16.8 7.3 %local0.1 = (bf16[256,8192]{1,0:T(8,128)(2,1)}, f32[256,128]{1,0:T(8,128)}) custom-call(bf16[256,8192]{1,0:T(8,128)(2,1)} %x_hbm.5, f32[256,128]{1,0:T(8,128)} %step_hbm.5, f32[256,128]{1,0:T(8,128)} %decay_hbm.5, bf16[256,1024]{1,0:T(8,128)(2,1)} %inject_hbm.5, bf16[256,1024]{1,0:T(8,128)(2,1)} %readout_ref.1, f32[1,128]{1,0:T(1,128)} %bitcast.2), custom_call_target="tpu_custom_call" | custom-call | flops 2000000000 | bytes 6000000 | tf_op jit(solution)/shard_map/local0/pallas_call | solution.py:332
  24.2 21.3 %all-to-all-done.in_ref.in_hbm = bf16[64,136,128]{2,1,0:T(8,128)(2,1)S(1)} async-done(((bf16[64,136,128]{2,1,0:T(8,128)(2,1)}), bf16[64,136,128]{2,1,0:T(8,128)(2,1)S(1)}, u32[]{:S(2)}, u32[]{:S(2)}) %all-to-all-start) | async-done | bytes 2228256 | tf_op jit(solution)/shard_map/all_to_all | solution.py:422
  45.5 0.0 copy-start
  45.5 0.5 total.1
  46.1 14.8 %all_to_all.15.earlier_ref = bf16[4,136,128]{2,1,0:T(8,128)(2,1)S(1)} all-to-all(bf16[4,136,128]{2,1,0:T(8,128)(2,1)S(1)} %total.1), channel_id=1, replica_groups={{0,64,128,192},{16,80,144,208},{32,96,160,224},{48,112,176,240},{1,65,1..., dimensions={0} | all-to-all | bytes 278528 | tf_op jit(solution)/shard_map/all_to_all | solution.py:411
  60.9 0.0 copy-done
  60.9 2.6 %held.1 = bf16[64,128,128]{2,1,0:T(8,128)(2,1)} custom-call(bf16[4,136,128]{2,1,0:T(8,128)(2,1)S(1)} %all_to_all.15.earlier_ref, bf16[64,136,128]{2,1,0:T(8,128)(2,1)} %copy-done), custom_call_target="tpu_custom_call" | custom-call | flops 4000000 | bytes 4000000 | tf_op jit(solution)/shard_map/held/pallas_call | solution.py:222
  63.5 7.6 %all-to-all-start.2 = ((bf16[64,128,128]{2,1,0:T(8,128)(2,1)}), bf16[64,128,128]{2,1,0:T(8,128)(2,1)S(1)}, u32[]{:S(2)}, u32[]{:S(2)}) async-start(bf16[64,128,128]{2,1,0:T(8,128)(2,1)} %held.1), calls=%async_computation.2 | async-start | bytes 4194304 | tf_op jit(solution)/shard_map/all_to_all | solution.py:422
  71.1 0.0 copy-start.1
  71.1 0.0 copy-start.2
  71.1 6.7 %local1.1.local_hbm = bf16[256,8192]{1,0:T(8,128)(2,1)} custom-call(bf16[256,8192]{1,0:T(8,128)(2,1)} %x_hbm.5, f32[256,128]{1,0:T(8,128)} %step_hbm.5, f32[256,128]{1,0:T(8,128)} %decay_hbm.5, bf16[256,1024]{1,0:T(8,128)(2,1)} %inject_hbm.5, bf16[256,1024]{1,0:T(8,128)(2,1)} %readout_ref.1, f32[1,128]{1,0:T(1,128)} %bitcast.3, ...), custom_call_target="tpu_custom_call", output_to_operand_aliasing={{}: (6, {})} | custom-call | flops 2000000000 | bytes 6000000 | tf_op jit(solution)/shard_map/local1/pallas_call | solution.py:332
  77.8 20.5 %all-to-all-done.2.held_ref = bf16[64,128,128]{2,1,0:T(8,128)(2,1)S(1)} async-done(((bf16[64,128,128]{2,1,0:T(8,128)(2,1)}), bf16[64,128,128]{2,1,0:T(8,128)(2,1)S(1)}, u32[]{:S(2)}, u32[]{:S(2)}) %all-to-all-start.2) | async-done | bytes 2097184 | tf_op jit(solution)/shard_map/all_to_all | solution.py:422
  98.3 0.0 copy-done.1
  98.3 0.0 copy-done.2
  98.3 5.1 %outputs.1 = bf16[256,8192]{1,0:T(8,128)(2,1)} custom-call(f32[256,128]{1,0:T(8,128)S(1)} %copy-done.2, bf16[256,1024]{1,0:T(8,128)(2,1)S(1)} %copy-done.1, bf16[64,128,128]{2,1,0:T(8,128)(2,1)S(1)} %all-to-all-done.2.held_ref, bf16[256,8192]{1,0:T(8,128)(2,1)} %local1.1.local_hbm), custom_call_target="tpu_custom_call" | custom-call | flops 2000000000 | bytes 12000000 | tf_op jit(solution)/shard_map/outputs/pallas_call | solution.py:390
Async XLA Ops:
  6.5 39.1 %all-to-all-start = ((bf16[64,136,128]{2,1,0:T(8,128)(2,1)}), bf16[64,136,128]{2,1,0:T(8,128)(2,1)S(1)}, u32[]{:S(2)}, u32[]{:S(2)}) async-start(bf16[64,136,128]{2,1,0:T(8,128)(2,1)} %states.1), calls=%async_computation | async-start | bytes 4456448 | tf_op jit(solution)/shard_map/all_to_all | solution.py:422
  45.5 15.3 %copy-start = (bf16[64,136,128]{2,1,0:T(8,128)(2,1)}, bf16[64,136,128]{2,1,0:T(8,128)(2,1)S(1)}, u32[]{:S(2)}) copy-start(bf16[64,136,128]{2,1,0:T(8,128)(2,1)S(1)} %all-to-all-done.in_ref.in_hbm) | copy-start | bytes 6684676
  63.5 34.9 %all-to-all-start.2 = ((bf16[64,128,128]{2,1,0:T(8,128)(2,1)}), bf16[64,128,128]{2,1,0:T(8,128)(2,1)S(1)}, u32[]{:S(2)}, u32[]{:S(2)}) async-start(bf16[64,128,128]{2,1,0:T(8,128)(2,1)} %held.1), calls=%async_computation.2 | async-start | bytes 4194304 | tf_op jit(solution)/shard_map/all_to_all | solution.py:422
  71.1 27.2 %copy-start.1 = (bf16[256,1024]{1,0:T(8,128)(2,1)S(1)}, bf16[256,1024]{1,0:T(8,128)(2,1)}, u32[]{:S(2)}) copy-start(bf16[256,1024]{1,0:T(8,128)(2,1)} %readout_ref.1) | copy-start | bytes 1572868
  71.1 27.2 %copy-start.2 = (f32[256,128]{1,0:T(8,128)S(1)}, f32[256,128]{1,0:T(8,128)}, u32[]{:S(2)}) copy-start(f32[256,128]{1,0:T(8,128)} %get-tuple-element.12.lead_ref) | copy-start | bytes 393220

commit v4 on v3

--- a/solution.py
+++ b/solution.py
@@ -16,7 +16,6 @@
 LANES = 128
 OWNERS = 64
 STEP = 4
-SPANS = 4
 PIECES = 4
 OWN_HEADS = HEADS // OWNERS
 COLS = OWN_HEADS * HEAD_DIM
@@ -25,7 +24,7 @@
 ROWS = STATE + 8
 VMEM_LIMIT = 61 * 1024 * 1024
 OUT_VMEM_LIMIT = 50 * 1024 * 1024
-HELD_VMEM_LIMIT = 52 * 1024 * 1024
+HELD_VMEM_LIMIT = 40 * 1024 * 1024
 SMALL_VMEM_LIMIT = 24 * 1024 * 1024
 WIDE = 512
 NARROW = 256
@@ -167,73 +166,82 @@
     return jnp.where(row == 0, high, jnp.where(row == 1, decay - high, 0.0)).astype(bf16)
 
 
-def total_kernel(place_ref, in_ref, out_ref):
+def total_kernel(in_ref, out_ref):
     state = in_ref[0, :STATE, :].astype(f32)
     decay = decay_row(in_ref[0])
     for i in range(1, OWNERS):
         d = decay_row(in_ref[i])
         state = state * d + in_ref[i, :STATE, :].astype(f32)
         decay = decay * d
-    rows = pack_rows(decay).astype(f32)
-    same = jnp.where(iota((8, COLS), 0) == 0, 1.0, 0.0)
-    for k in range(SPANS):
-        later = place_ref[0] < k
-        out_ref[k, :STATE, :] = jnp.where(later, state, 0.0).astype(bf16)
-        out_ref[k, STATE:, :] = jnp.where(later, rows, same).astype(bf16)
-
-
-def held_kernel(earlier_ref, in_hbm, out_hbm, in_buf, out_buf, in_sem, out_sem):
+    out_ref[:STATE, :] = state.astype(bf16)
+    out_ref[STATE:, :] = pack_rows(decay)
+
+
+def join_kernel(place_ref, own_ref, other_ref, pair_ref):
+    second = place_ref[0] % 2 == 1
+    own, other = own_ref[...].astype(f32), other_ref[...].astype(f32)
+    late = jnp.where(second, own, other)
+    early = jnp.where(second, other, own)
+    late_decay, early_decay = decay_row(late), decay_row(early)
+    pair_ref[:STATE, :] = (late[:STATE] + late_decay * early[:STATE]).astype(bf16)
+    pair_ref[STATE:, :] = pack_rows(late_decay * early_decay)
+
+
+def held_kernel(place_ref, other_ref, pair_ref, in_ref, out_hbm, out_buf, sem):
+    place = place_ref[0]
+    state = jnp.where(place >= 2, pair_ref[:STATE, :].astype(f32), 0.0)
+    other = other_ref[...].astype(f32)
+    state = jnp.where(place % 2 == 1, other[:STATE] + decay_row(other) * state, state)
     size = OWNERS // PIECES
-    spans = [pl.ds(i * size, size) for i in range(PIECES)]
-    arrive = copies(*[(in_hbm.at[p], in_buf.at[p], in_sem.at[i]) for i, p in enumerate(spans)])
-    state = jnp.zeros((STATE, COLS), f32)
-    for k in range(SPANS - 1):
-        state = earlier_ref[k, :STATE, :].astype(f32) + decay_row(earlier_ref[k]) * state
     sent = []
     for i in range(OWNERS):
-        if i % size == 0:
-            arrive[i // size].wait()
         out_buf[i] = state.astype(bf16)
         if (i + 1) % size == 0:
-            p = spans[i // size]
-            sent += copies((out_buf.at[p], out_hbm.at[p], out_sem.at[i // size]))
+            span = pl.ds(i + 1 - size, size)
+            sent += copies((out_buf.at[span], out_hbm.at[span], sem.at[i // size]))
         if i + 1 < OWNERS:
-            state = state * decay_row(in_buf[i]) + in_buf[i, :STATE, :].astype(f32)
+            state = state * decay_row(in_ref[i]) + in_ref[i, :STATE, :].astype(f32)
     for c in sent:
         c.wait()
 
 
-def total_of(place, arrived):
+def total_of(arrived):
     return pl.pallas_call(
         total_kernel,
-        out_shape=jax.ShapeDtypeStruct((SPANS, ROWS, COLS), bf16),
-        in_specs=[
-            pl.BlockSpec(memory_space=pltpu.SMEM),
-            pl.BlockSpec(memory_space=pltpu.VMEM),
-        ],
+        out_shape=jax.ShapeDtypeStruct((ROWS, COLS), bf16),
         compiler_params=pltpu.CompilerParams(vmem_limit_bytes=SMALL_VMEM_LIMIT),
         cost_estimate=pl.CostEstimate(flops=4_000_000, bytes_accessed=2_000_000, transcendentals=0),
         name="total",
-    )(place, arrived)
-
-
-def held_of(earlier, arrived):
-    hbm = pl.BlockSpec(memory_space=pltpu.HBM)
+    )(arrived)
+
+
+def pair_of(place, own, other):
+    vmem = pl.BlockSpec(memory_space=pltpu.VMEM)
+    return pl.pallas_call(
+        join_kernel,
+        out_shape=jax.ShapeDtypeStruct((ROWS, COLS), bf16),
+        in_specs=[pl.BlockSpec(memory_space=pltpu.SMEM), vmem, vmem],
+        compiler_params=pltpu.CompilerParams(vmem_limit_bytes=SMALL_VMEM_LIMIT),
+        cost_estimate=pl.CostEstimate(flops=100_000, bytes_accessed=100_000, transcendentals=0),
+        name="pair",
+    )(place, own, other)
+
+
+def held_of(place, other, pair, arrived):
+    vmem = pl.BlockSpec(memory_space=pltpu.VMEM)
     return pl.pallas_call(
         held_kernel,
-        out_shape=jax.ShapeDtypeStruct((OWNERS, STATE, COLS), bf16),
-        in_specs=[pl.BlockSpec(memory_space=pltpu.VMEM), hbm],
-        out_specs=hbm,
+        out_shape=pltpu.HBM((OWNERS, STATE, COLS), bf16),
+        in_specs=[pl.BlockSpec(memory_space=pltpu.SMEM), vmem, vmem, vmem],
+        out_specs=pl.BlockSpec(memory_space=pltpu.HBM),
         scratch_shapes=[
-            pltpu.VMEM((OWNERS, ROWS, COLS), bf16),
             pltpu.VMEM((OWNERS, STATE, COLS), bf16),
-            pltpu.SemaphoreType.DMA((PIECES,)),
             pltpu.SemaphoreType.DMA((PIECES,)),
         ],
         compiler_params=pltpu.CompilerParams(vmem_limit_bytes=HELD_VMEM_LIMIT),
         cost_estimate=pl.CostEstimate(flops=4_000_000, bytes_accessed=4_000_000, transcendentals=0),
         name="held",
-    )(earlier, arrived)
+    )(place, other, pair, arrived)
 
 
 def local_kernel(
@@ -407,15 +415,8 @@
     )(lead, readout, held, local)
 
 
-def across(v, ways):
-    return lax.all_to_all(
-        v,
-        "seq",
-        split_axis=0,
-        concat_axis=0,
-        tiled=True,
-        axis_index_groups=[list(range(i, ways, STEP)) for i in range(STEP)],
-    )
+def swap_runs(v, bit, ways):
+    return lax.ppermute(v, "seq", [(i, i ^ (bit * STEP)) for i in range(ways)])
 
 
 def exchange(v, devices):
@@ -439,8 +440,10 @@
     local, lead = local_of(0, (), *args)
     arrived, local, lead = lax.optimization_barrier((arrived, local, lead))
     place = (lax.axis_index("seq") // STEP).astype(jnp.int32)[None]
-    earlier = across(total_of(place, arrived), ways)
-    held = held_of(earlier, arrived)
+    total = total_of(arrived)
+    other = swap_runs(total, 1, ways)
+    pair = swap_runs(pair_of(place, total, other), 2, ways)
+    held = held_of(place, other, pair, arrived)
     held = exchange(held, devices)
     (local,) = local_of(1, (local,), *args)
     return outputs_of(lead, readout, held, local)

time: 104 us -> 100 us (0.962)
  blocking collectives: 14.8 us -> 0 us
  starting transfers between devices: 18 us -> 27.4 us
  waiting for transfers between devices: 41.8 us -> 44.5 us
    all_to_all x1 -> x0, blocking collectives: 14.8 us -> none  [across(): lax.all_to_all(v, 'seq', split_axis=0, concat_axis=0, tiled=True, axis_in...]
    ppermute x0 -> x2, starting transfers between devices: none -> 8.55 us  [swap_runs(): return lax.ppermute(v, 'seq', [(i, i ^ bit * STEP) for i in range(ways)])]
    ppermute x0 -> x2, waiting for transfers between devices: none -> 2.66 us  [swap_runs(): return lax.ppermute(v, 'seq', [(i, i ^ bit * STEP) for i in range(ways)])]
    pallas_call x2 -> x3, Pallas kernels: 3.13 us -> 2.03 us  [the longest x1 1.48 us: held_of(): pl.pallas_call(held_kernel, out_shape=pltpu.HBM((OWNERS, STATE, COLS), bf...]
  transfers between devices with their start and end apart: 2 -> 4, of which waited for: 2 -> 4; matrix products, arithmetic and copies ran while one was open for 0% -> 0% of each run, Pallas kernels for 14% -> 14%
where the time goes in v4:
time: 100 us; the launch traced here: 99.8 us
  waiting for transfers between devices  44.5 us (44%)
  Pallas kernels  27.7 us (28%)
  starting transfers between devices  27.4 us (27%)
    all_to_all x2, waiting for transfers between devices, exchange(): lax.all_to_all(v, ('seq', 'head'), split_axis=0, concat_axis=0, tiled=Tru...  41.8 us
    all_to_all x2, starting transfers between devices, exchange(): lax.all_to_all(v, ('seq', 'head'), split_axis=0, concat_axis=0, tiled=Tru...  18.9 us
    pallas_call x2, Pallas kernels, local_of(): pl.pallas_call(functools.partial(local_kernel, part), out_shape=[jax.Shap...  14.1 us
    ppermute x2, starting transfers between devices, swap_runs(): return lax.ppermute(v, 'seq', [(i, i ^ bit * STEP) for i in range(ways)])  8.55 us
    pallas_call x1, Pallas kernels, states_of(): pl.pallas_call(state_kernel, out_shape=jax.ShapeDtypeStruct((OWNERS, ROWS...  6.46 us
    pallas_call x1, Pallas kernels, outputs_of(): pl.pallas_call(out_kernel, out_shape=jax.ShapeDtypeStruct((TOK, HEADS * H...  5.13 us
    ppermute x2, waiting for transfers between devices, swap_runs(): return lax.ppermute(v, 'seq', [(i, i ^ bit * STEP) for i in range(ways)])  2.66 us
  transfers between devices with their start and end apart: 4, of which 4 were waited for; matrix products, arithmetic and copies ran while one was open for 0% of the time, Pallas kernels for 14%

profile of v4, /device:TPU:1, one launch (start us, length us, event | category | flops | bytes accessed | tf_op | source)
XLA Modules:
  0.0 99.8 jit_solution(12520004903042955535)
XLA Ops:
  0.0 6.5 %states.1 = bf16[64,136,128]{2,1,0:T(8,128)(2,1)} custom-call(bf16[256,8192]{1,0:T(8,128)(2,1)} %x_hbm.5, f32[256,128]{1,0:T(8,128)} %step_hbm.5, f32[256,128]{1,0:T(8,128)} %decay_hbm.5, bf16[256,1024]{1,0:T(8,128)(2,1)} %inject_hbm.5), custom_call_target="tpu_custom_call" | custom-call | flops 2000000000 | bytes 8000000 | tf_op jit(solution)/shard_map/states/pallas_call | solution.py:134
  6.5 10.4 %all-to-all-start = ((bf16[64,136,128]{2,1,0:T(8,128)(2,1)}), bf16[64,136,128]{2,1,0:T(8,128)(2,1)S(1)}, u32[]{:S(2)}, u32[]{:S(2)}) async-start(bf16[64,136,128]{2,1,0:T(8,128)(2,1)} %states.1), calls=%async_computation | async-start | bytes 4456448 | tf_op jit(solution)/shard_map/all_to_all | solution.py:423
  16.8 7.3 %local0.1 = (bf16[256,8192]{1,0:T(8,128)(2,1)}, f32[256,128]{1,0:T(8,128)}) custom-call(bf16[256,8192]{1,0:T(8,128)(2,1)} %x_hbm.5, f32[256,128]{1,0:T(8,128)} %step_hbm.5, f32[256,128]{1,0:T(8,128)} %decay_hbm.5, bf16[256,1024]{1,0:T(8,128)(2,1)} %inject_hbm.5, bf16[256,1024]{1,0:T(8,128)(2,1)} %readout_ref.1, f32[1,128]{1,0:T(1,128)} %bitcast.2), custom_call_target="tpu_custom_call" | custom-call | flops 2000000000 | bytes 6000000 | tf_op jit(solution)/shard_map/local0/pallas_call | solution.py:340
  24.2 21.4 %all-to-all-done.in_ref = bf16[64,136,128]{2,1,0:T(8,128)(2,1)S(1)} async-done(((bf16[64,136,128]{2,1,0:T(8,128)(2,1)}), bf16[64,136,128]{2,1,0:T(8,128)(2,1)S(1)}, u32[]{:S(2)}, u32[]{:S(2)}) %all-to-all-start) | async-done | bytes 2228256 | tf_op jit(solution)/shard_map/all_to_all | solution.py:423
  45.5 0.5 total.1.own_ref
  46.0 3.1 %collective-permute-start = (bf16[136,128]{1,0:T(8,128)(2,1)S(1)}, bf16[136,128]{1,0:T(8,128)(2,1)S(1)}, u32[]{:S(2)}, u32[]{:S(2)}) collective-permute-start(bf16[136,128]{1,0:T(8,128)(2,1)S(1)} %total.1.own_ref), channel_id=1, source_target_pairs={{0,64},{16,80},{32,96},{48,112},{64,0},{80,16},{96,32},{112,48},{1... | collective-permute-start | bytes 104456 | tf_op jit(solution)/shard_map/ppermute | solution.py:419
  49.1 1.3 %collective-permute-done.other_ref = bf16[136,128]{1,0:T(8,128)(2,1)S(1)} collective-permute-done((bf16[136,128]{1,0:T(8,128)(2,1)S(1)}, bf16[136,128]{1,0:T(8,128)(2,1)S(1)}, u32[]{:S(2)}, u32[]{:S(2)}) %collective-permute-start) | collective-permute-done | bytes 34848 | tf_op jit(solution)/shard_map/ppermute | solution.py:419
  50.5 5.5 %collective-permute-start.1 = (bf16[136,128]{1,0:T(8,128)(2,1)S(1)}, bf16[136,128]{1,0:T(8,128)(2,1)S(1)}, u32[]{:S(2)}, u32[]{:S(2)}) collective-permute-start(bf16[136,128]{1,0:T(8,128)(2,1)S(1)} %pair.1), channel_id=1, source_target_pairs={{0,128},{16,144},{32,160},{48,176},{64,192},{80,208},{96,224},{112... | collective-permute-start | bytes 104456 | tf_op jit(solution)/shard_map/ppermute | solution.py:419
  56.0 1.3 %collective-permute-done.1.pair_ref = bf16[136,128]{1,0:T(8,128)(2,1)S(1)} collective-permute-done((bf16[136,128]{1,0:T(8,128)(2,1)S(1)}, bf16[136,128]{1,0:T(8,128)(2,1)S(1)}, u32[]{:S(2)}, u32[]{:S(2)}) %collective-permute-start.1) | collective-permute-done | bytes 34848 | tf_op jit(solution)/shard_map/ppermute | solution.py:419
  57.3 1.5 %held.1 = bf16[64,128,128]{2,1,0:T(8,128)(2,1)} custom-call(s32[1]{0:T(128)} %bitcast.1.place_ref, bf16[136,128]{1,0:T(8,128)(2,1)S(1)} %collective-permute-done.other_ref, bf16[136,128]{1,0:T(8,128)(2,1)S(1)} %collective-permute-done.1.pair_ref, bf16[64,136,128]{2,1,0:T(8,128)(2,1)S(1)} %all-to-all-done.in_ref), custom_call_target="tpu_custom_call" | custom-call | flops 4000000 | bytes 4000000 | tf_op jit(solution)/shard_map/held/pallas_call | solution.py:232
  58.8 8.5 %all-to-all-start.1 = ((bf16[64,128,128]{2,1,0:T(8,128)(2,1)}), bf16[64,128,128]{2,1,0:T(8,128)(2,1)S(1)}, u32[]{:S(2)}, u32[]{:S(2)}) async-start(bf16[64,128,128]{2,1,0:T(8,128)(2,1)} %held.1), calls=%async_computation.1 | async-start | bytes 4194304 | tf_op jit(solution)/shard_map/all_to_all | solution.py:423
  67.3 0.0 copy-start
  67.3 0.0 copy-start.1
  67.3 6.8 %local1.1.local_hbm = bf16[256,8192]{1,0:T(8,128)(2,1)} custom-call(bf16[256,8192]{1,0:T(8,128)(2,1)} %x_hbm.5, f32[256,128]{1,0:T(8,128)} %step_hbm.5, f32[256,128]{1,0:T(8,128)} %decay_hbm.5, bf16[256,1024]{1,0:T(8,128)(2,1)} %inject_hbm.5, bf16[256,1024]{1,0:T(8,128)(2,1)} %readout_ref.1, f32[1,128]{1,0:T(1,128)} %bitcast.3, ...), custom_call_target="tpu_custom_call", output_to_operand_aliasing={{}: (6, {})} | custom-call | flops 2000000000 | bytes 6000000 | tf_op jit(solution)/shard_map/local1/pallas_call | solution.py:340
  74.1 20.4 %all-to-all-done.1.held_ref = bf16[64,128,128]{2,1,0:T(8,128)(2,1)S(1)} async-done(((bf16[64,128,128]{2,1,0:T(8,128)(2,1)}), bf16[64,128,128]{2,1,0:T(8,128)(2,1)S(1)}, u32[]{:S(2)}, u32[]{:S(2)}) %all-to-all-start.1) | async-done | bytes 2097184 | tf_op jit(solution)/shard_map/all_to_all | solution.py:423
  94.5 0.0 copy-done
  94.5 0.0 copy-done.1
  94.5 5.1 %outputs.1 = bf16[256,8192]{1,0:T(8,128)(2,1)} custom-call(f32[256,128]{1,0:T(8,128)S(1)} %copy-done.1, bf16[256,1024]{1,0:T(8,128)(2,1)S(1)} %copy-done, bf16[64,128,128]{2,1,0:T(8,128)(2,1)S(1)} %all-to-all-done.1.held_ref, bf16[256,8192]{1,0:T(8,128)(2,1)} %local1.1.local_hbm), custom_call_target="tpu_custom_call" | custom-call | flops 2000000000 | bytes 12000000 | tf_op jit(solution)/shard_map/outputs/pallas_call | solution.py:398
  (1 shorter events, 0.0 us)
Async XLA Ops:
  6.5 39.1 %all-to-all-start = ((bf16[64,136,128]{2,1,0:T(8,128)(2,1)}), bf16[64,136,128]{2,1,0:T(8,128)(2,1)S(1)}, u32[]{:S(2)}, u32[]{:S(2)}) async-start(bf16[64,136,128]{2,1,0:T(8,128)(2,1)} %states.1), calls=%async_computation | async-start | bytes 4456448 | tf_op jit(solution)/shard_map/all_to_all | solution.py:423
  46.0 4.4 %collective-permute-start = (bf16[136,128]{1,0:T(8,128)(2,1)S(1)}, bf16[136,128]{1,0:T(8,128)(2,1)S(1)}, u32[]{:S(2)}, u32[]{:S(2)}) collective-permute-start(bf16[136,128]{1,0:T(8,128)(2,1)S(1)} %total.1.own_ref), channel_id=1, source_target_pairs={{0,64},{16,80},{32,96},{48,112},{64,0},{80,16},{96,32},{112,48},{1... | collective-permute-start | bytes 104456 | tf_op jit(solution)/shard_map/ppermute | solution.py:419
  50.5 6.8 %collective-permute-start.1 = (bf16[136,128]{1,0:T(8,128)(2,1)S(1)}, bf16[136,128]{1,0:T(8,128)(2,1)S(1)}, u32[]{:S(2)}, u32[]{:S(2)}) collective-permute-start(bf16[136,128]{1,0:T(8,128)(2,1)S(1)} %pair.1), channel_id=1, source_target_pairs={{0,128},{16,144},{32,160},{48,176},{64,192},{80,208},{96,224},{112... | collective-permute-start | bytes 104456 | tf_op jit(solution)/shard_map/ppermute | solution.py:419
  58.8 35.8 %all-to-all-start.1 = ((bf16[64,128,128]{2,1,0:T(8,128)(2,1)}), bf16[64,128,128]{2,1,0:T(8,128)(2,1)S(1)}, u32[]{:S(2)}, u32[]{:S(2)}) async-start(bf16[64,128,128]{2,1,0:T(8,128)(2,1)} %held.1), calls=%async_computation.1 | async-start | bytes 4194304 | tf_op jit(solution)/shard_map/all_to_all | solution.py:423
  67.3 27.2 %copy-start = (bf16[256,1024]{1,0:T(8,128)(2,1)S(1)}, bf16[256,1024]{1,0:T(8,128)(2,1)}, u32[]{:S(2)}) copy-start(bf16[256,1024]{1,0:T(8,128)(2,1)} %readout_ref.1) | copy-start | bytes 1572868
  67.3 27.2 %copy-start.1 = (f32[256,128]{1,0:T(8,128)S(1)}, f32[256,128]{1,0:T(8,128)}, u32[]{:S(2)}) copy-start(f32[256,128]{1,0:T(8,128)} %get-tuple-element.12.lead_ref) | copy-start | bytes 393220

commit v5 on v4

--- a/solution.py
+++ b/solution.py
@@ -105,15 +105,15 @@
     sent = []
     for g in range(GROUPS + 1):
         if g < GROUPS:
-            if g % 2 == 0:
-                x_in[g].wait()
-                x_in[g + 1].wait()
+            if g % 4 == 0:
+                for c in x_in[g : g + 4]:
+                    c.wait()
         first = (g - 1) * GROUP_OWNERS
         for w in range(GROUP_COLS // NARROW):
             part = slice(w * NARROW, (w + 1) * NARROW)
             if g < GROUPS:
                 weight = spread(scale, g * GROUP_COLS + w * NARROW, NARROW)
-                v_buf[g % 2, :, part] = (x_buf[g, :, part].astype(f32) * weight).astype(bf16)
+                v_buf[g % 2, :, part] = x_buf[g, :, part] * weight.astype(bf16)
             if g > 0:
                 s = dot(turned_buf[g - 1], v_buf[(g - 1) % 2, :, part]).astype(bf16)
                 below = spread(extra, (g - 1) * GROUP_COLS + w * NARROW, NARROW).astype(bf16)
@@ -374,8 +374,9 @@
     )
     sent = []
     for g in range(GROUPS + 1):
-        if g > 0:
+        if g % 2 == 1:
             local_in[g - 1].wait()
+            local_in[g].wait()
         if g < GROUPS:
             held = jnp.concatenate(
                 [held_ref[g * GROUP_OWNERS + i] for i in range(GROUP_OWNERS)], axis=1
@@ -415,8 +416,8 @@
     )(lead, readout, held, local)
 
 
-def swap_runs(v, bit, ways):
-    return lax.ppermute(v, "seq", [(i, i ^ (bit * STEP)) for i in range(ways)])
+def swap_runs(v, bits, ways):
+    return lax.ppermute(v, "seq", [(i, i ^ (bits * STEP)) for i in range(ways)])
 
 
 def exchange(v, devices):
@@ -442,7 +443,7 @@
     place = (lax.axis_index("seq") // STEP).astype(jnp.int32)[None]
     total = total_of(arrived)
     other = swap_runs(total, 1, ways)
-    pair = swap_runs(pair_of(place, total, other), 2, ways)
+    pair = swap_runs(pair_of(place, total, other), 3, ways)
     held = held_of(place, other, pair, arrived)
     held = exchange(held, devices)
     (local,) = local_of(1, (local,), *args)

time: 100 us -> 98.1 us (0.981)
  Pallas kernels: 27.7 us -> 26.1 us
    pallas_call x1, Pallas kernels: 6.46 us -> 5.15 us  [states_of(): pl.pallas_call(state_kernel, out_shape=jax.ShapeDtypeStruct((OWNERS, ROWS...]
where the time goes in v5:
time: 98.1 us; the launch traced here: 97.7 us
  waiting for transfers between devices  44.5 us (45%)
  starting transfers between devices  26.9 us (27%)
  Pallas kernels  26.1 us (27%)
    all_to_all x2, waiting for transfers between devices, exchange(): lax.all_to_all(v, ('seq', 'head'), split_axis=0, concat_axis=0, tiled=Tru...  41.8 us
    all_to_all x2, starting transfers between devices, exchange(): lax.all_to_all(v, ('seq', 'head'), split_axis=0, concat_axis=0, tiled=Tru...  19.2 us
    pallas_call x2, Pallas kernels, local_of(): pl.pallas_call(functools.partial(local_kernel, part), out_shape=[jax.Shap...  14.1 us
    ppermute x2, starting transfers between devices, swap_runs(): return lax.ppermute(v, 'seq', [(i, i ^ bits * STEP) for i in range(ways)])  7.67 us
    pallas_call x1, Pallas kernels, states_of(): pl.pallas_call(state_kernel, out_shape=jax.ShapeDtypeStruct((OWNERS, ROWS...  5.15 us
    pallas_call x1, Pallas kernels, outputs_of(): pl.pallas_call(out_kernel, out_shape=jax.ShapeDtypeStruct((TOK, HEADS * H...  4.89 us
    ppermute x2, waiting for transfers between devices, swap_runs(): return lax.ppermute(v, 'seq', [(i, i ^ bits * STEP) for i in range(ways)])  2.65 us
  transfers between devices with their start and end apart: 4, of which 4 were waited for; matrix products, arithmetic and copies ran while one was open for 0% of the time, Pallas kernels for 14%

profile of v5, /device:TPU:1, one launch (start us, length us, event | category | flops | bytes accessed | tf_op | source)
XLA Modules:
  0.0 97.7 jit_solution(11240921656051514880)
XLA Ops:
  0.0 5.2 %states.1 = bf16[64,136,128]{2,1,0:T(8,128)(2,1)} custom-call(bf16[256,8192]{1,0:T(8,128)(2,1)} %x_hbm.5, f32[256,128]{1,0:T(8,128)} %step_hbm.5, f32[256,128]{1,0:T(8,128)} %decay_hbm.5, bf16[256,1024]{1,0:T(8,128)(2,1)} %inject_hbm.5), custom_call_target="tpu_custom_call" | custom-call | flops 2000000000 | bytes 8000000 | tf_op jit(solution)/shard_map/states/pallas_call | solution.py:134
  5.2 10.4 %all-to-all-start = ((bf16[64,136,128]{2,1,0:T(8,128)(2,1)}), bf16[64,136,128]{2,1,0:T(8,128)(2,1)S(1)}, u32[]{:S(2)}, u32[]{:S(2)}) async-start(bf16[64,136,128]{2,1,0:T(8,128)(2,1)} %states.1), calls=%async_computation | async-start | bytes 4456448 | tf_op jit(solution)/shard_map/all_to_all | solution.py:424
  15.5 7.3 %local0.1 = (bf16[256,8192]{1,0:T(8,128)(2,1)}, f32[256,128]{1,0:T(8,128)}) custom-call(bf16[256,8192]{1,0:T(8,128)(2,1)} %x_hbm.5, f32[256,128]{1,0:T(8,128)} %step_hbm.5, f32[256,128]{1,0:T(8,128)} %decay_hbm.5, bf16[256,1024]{1,0:T(8,128)(2,1)} %inject_hbm.5, bf16[256,1024]{1,0:T(8,128)(2,1)} %readout_ref.1, f32[1,128]{1,0:T(1,128)} %bitcast.2), custom_call_target="tpu_custom_call" | custom-call | flops 2000000000 | bytes 6000000 | tf_op jit(solution)/shard_map/local0/pallas_call | solution.py:340
  22.8 21.4 %all-to-all-done.in_ref = bf16[64,136,128]{2,1,0:T(8,128)(2,1)S(1)} async-done(((bf16[64,136,128]{2,1,0:T(8,128)(2,1)}), bf16[64,136,128]{2,1,0:T(8,128)(2,1)S(1)}, u32[]{:S(2)}, u32[]{:S(2)}) %all-to-all-start) | async-done | bytes 2228256 | tf_op jit(solution)/shard_map/all_to_all | solution.py:424
  44.2 0.5 total.1.own_ref
  44.7 3.1 %collective-permute-start = (bf16[136,128]{1,0:T(8,128)(2,1)S(1)}, bf16[136,128]{1,0:T(8,128)(2,1)S(1)}, u32[]{:S(2)}, u32[]{:S(2)}) collective-permute-start(bf16[136,128]{1,0:T(8,128)(2,1)S(1)} %total.1.own_ref), channel_id=1, source_target_pairs={{0,64},{16,80},{32,96},{48,112},{64,0},{80,16},{96,32},{112,48},{1... | collective-permute-start | bytes 104456 | tf_op jit(solution)/shard_map/ppermute | solution.py:420
  47.8 1.3 %collective-permute-done.other_ref = bf16[136,128]{1,0:T(8,128)(2,1)S(1)} collective-permute-done((bf16[136,128]{1,0:T(8,128)(2,1)S(1)}, bf16[136,128]{1,0:T(8,128)(2,1)S(1)}, u32[]{:S(2)}, u32[]{:S(2)}) %collective-permute-start) | collective-permute-done | bytes 34848 | tf_op jit(solution)/shard_map/ppermute | solution.py:420
  49.2 4.6 %collective-permute-start.1 = (bf16[136,128]{1,0:T(8,128)(2,1)S(1)}, bf16[136,128]{1,0:T(8,128)(2,1)S(1)}, u32[]{:S(2)}, u32[]{:S(2)}) collective-permute-start(bf16[136,128]{1,0:T(8,128)(2,1)S(1)} %pair.1), channel_id=1, source_target_pairs={{0,192},{16,208},{32,224},{48,240},{64,128},{80,144},{96,160},{112... | collective-permute-start | bytes 104456 | tf_op jit(solution)/shard_map/ppermute | solution.py:420
  53.8 1.3 %collective-permute-done.1.pair_ref = bf16[136,128]{1,0:T(8,128)(2,1)S(1)} collective-permute-done((bf16[136,128]{1,0:T(8,128)(2,1)S(1)}, bf16[136,128]{1,0:T(8,128)(2,1)S(1)}, u32[]{:S(2)}, u32[]{:S(2)}) %collective-permute-start.1) | collective-permute-done | bytes 34848 | tf_op jit(solution)/shard_map/ppermute | solution.py:420
  55.1 1.5 %held.1 = bf16[64,128,128]{2,1,0:T(8,128)(2,1)} custom-call(s32[1]{0:T(128)} %bitcast.1.place_ref, bf16[136,128]{1,0:T(8,128)(2,1)S(1)} %collective-permute-done.other_ref, bf16[136,128]{1,0:T(8,128)(2,1)S(1)} %collective-permute-done.1.pair_ref, bf16[64,136,128]{2,1,0:T(8,128)(2,1)S(1)} %all-to-all-done.in_ref), custom_call_target="tpu_custom_call" | custom-call | flops 4000000 | bytes 4000000 | tf_op jit(solution)/shard_map/held/pallas_call | solution.py:232
  56.6 8.9 %all-to-all-start.1 = ((bf16[64,128,128]{2,1,0:T(8,128)(2,1)}), bf16[64,128,128]{2,1,0:T(8,128)(2,1)S(1)}, u32[]{:S(2)}, u32[]{:S(2)}) async-start(bf16[64,128,128]{2,1,0:T(8,128)(2,1)} %held.1), calls=%async_computation.1 | async-start | bytes 4194304 | tf_op jit(solution)/shard_map/all_to_all | solution.py:424
  65.5 0.0 copy-start
  65.5 0.0 copy-start.1
  65.5 6.8 %local1.1.local_hbm = bf16[256,8192]{1,0:T(8,128)(2,1)} custom-call(bf16[256,8192]{1,0:T(8,128)(2,1)} %x_hbm.5, f32[256,128]{1,0:T(8,128)} %step_hbm.5, f32[256,128]{1,0:T(8,128)} %decay_hbm.5, bf16[256,1024]{1,0:T(8,128)(2,1)} %inject_hbm.5, bf16[256,1024]{1,0:T(8,128)(2,1)} %readout_ref.1, f32[1,128]{1,0:T(1,128)} %bitcast.3, ...), custom_call_target="tpu_custom_call", output_to_operand_aliasing={{}: (6, {})} | custom-call | flops 2000000000 | bytes 6000000 | tf_op jit(solution)/shard_map/local1/pallas_call | solution.py:340
  72.2 20.4 %all-to-all-done.1.held_ref = bf16[64,128,128]{2,1,0:T(8,128)(2,1)S(1)} async-done(((bf16[64,128,128]{2,1,0:T(8,128)(2,1)}), bf16[64,128,128]{2,1,0:T(8,128)(2,1)S(1)}, u32[]{:S(2)}, u32[]{:S(2)}) %all-to-all-start.1) | async-done | bytes 2097184 | tf_op jit(solution)/shard_map/all_to_all | solution.py:424
  92.7 0.0 copy-done
  92.7 0.0 copy-done.1
  92.7 4.9 %outputs.1 = bf16[256,8192]{1,0:T(8,128)(2,1)} custom-call(f32[256,128]{1,0:T(8,128)S(1)} %copy-done.1, bf16[256,1024]{1,0:T(8,128)(2,1)S(1)} %copy-done, bf16[64,128,128]{2,1,0:T(8,128)(2,1)S(1)} %all-to-all-done.1.held_ref, bf16[256,8192]{1,0:T(8,128)(2,1)} %local1.1.local_hbm), custom_call_target="tpu_custom_call" | custom-call | flops 2000000000 | bytes 12000000 | tf_op jit(solution)/shard_map/outputs/pallas_call | solution.py:399
  (1 shorter events, 0.0 us)
Async XLA Ops:
  5.2 39.1 %all-to-all-start = ((bf16[64,136,128]{2,1,0:T(8,128)(2,1)}), bf16[64,136,128]{2,1,0:T(8,128)(2,1)S(1)}, u32[]{:S(2)}, u32[]{:S(2)}) async-start(bf16[64,136,128]{2,1,0:T(8,128)(2,1)} %states.1), calls=%async_computation | async-start | bytes 4456448 | tf_op jit(solution)/shard_map/all_to_all | solution.py:424
  44.7 4.4 %collective-permute-start = (bf16[136,128]{1,0:T(8,128)(2,1)S(1)}, bf16[136,128]{1,0:T(8,128)(2,1)S(1)}, u32[]{:S(2)}, u32[]{:S(2)}) collective-permute-start(bf16[136,128]{1,0:T(8,128)(2,1)S(1)} %total.1.own_ref), channel_id=1, source_target_pairs={{0,64},{16,80},{32,96},{48,112},{64,0},{80,16},{96,32},{112,48},{1... | collective-permute-start | bytes 104456 | tf_op jit(solution)/shard_map/ppermute | solution.py:420
  49.2 5.9 %collective-permute-start.1 = (bf16[136,128]{1,0:T(8,128)(2,1)S(1)}, bf16[136,128]{1,0:T(8,128)(2,1)S(1)}, u32[]{:S(2)}, u32[]{:S(2)}) collective-permute-start(bf16[136,128]{1,0:T(8,128)(2,1)S(1)} %pair.1), channel_id=1, source_target_pairs={{0,192},{16,208},{32,224},{48,240},{64,128},{80,144},{96,160},{112... | collective-permute-start | bytes 104456 | tf_op jit(solution)/shard_map/ppermute | solution.py:420
  56.6 36.1 %all-to-all-start.1 = ((bf16[64,128,128]{2,1,0:T(8,128)(2,1)}), bf16[64,128,128]{2,1,0:T(8,128)(2,1)S(1)}, u32[]{:S(2)}, u32[]{:S(2)}) async-start(bf16[64,128,128]{2,1,0:T(8,128)(2,1)} %held.1), calls=%async_computation.1 | async-start | bytes 4194304 | tf_op jit(solution)/shard_map/all_to_all | solution.py:424
  65.5 27.2 %copy-start = (bf16[256,1024]{1,0:T(8,128)(2,1)S(1)}, bf16[256,1024]{1,0:T(8,128)(2,1)}, u32[]{:S(2)}) copy-start(bf16[256,1024]{1,0:T(8,128)(2,1)} %readout_ref.1) | copy-start | bytes 1572868
  65.5 27.2 %copy-start.1 = (f32[256,128]{1,0:T(8,128)S(1)}, f32[256,128]{1,0:T(8,128)}, u32[]{:S(2)}) copy-start(f32[256,128]{1,0:T(8,128)} %get-tuple-element.12.lead_ref) | copy-start | bytes 393220

commit v6 on v5

--- a/solution.py
+++ b/solution.py
@@ -177,21 +177,17 @@
     out_ref[STATE:, :] = pack_rows(decay)
 
 
-def join_kernel(place_ref, own_ref, other_ref, pair_ref):
-    second = place_ref[0] % 2 == 1
-    own, other = own_ref[...].astype(f32), other_ref[...].astype(f32)
-    late = jnp.where(second, own, other)
-    early = jnp.where(second, other, own)
-    late_decay, early_decay = decay_row(late), decay_row(early)
-    pair_ref[:STATE, :] = (late[:STATE] + late_decay * early[:STATE]).astype(bf16)
-    pair_ref[STATE:, :] = pack_rows(late_decay * early_decay)
-
-
-def held_kernel(place_ref, other_ref, pair_ref, in_ref, out_hbm, out_buf, sem):
+def held_kernel(place_ref, one_ref, two_ref, three_ref, in_ref, out_hbm, out_buf, sem):
     place = place_ref[0]
-    state = jnp.where(place >= 2, pair_ref[:STATE, :].astype(f32), 0.0)
-    other = other_ref[...].astype(f32)
-    state = jnp.where(place % 2 == 1, other[:STATE] + decay_row(other) * state, state)
+    state = jnp.zeros((STATE, COLS), f32)
+    for run in range(3):
+        bits = place ^ run
+        block = jnp.where(
+            bits == 1,
+            one_ref[...].astype(f32),
+            jnp.where(bits == 2, two_ref[...].astype(f32), three_ref[...].astype(f32)),
+        )
+        state = jnp.where(run < place, block[:STATE] + decay_row(block) * state, state)
     size = OWNERS // PIECES
     sent = []
     for i in range(OWNERS):
@@ -215,24 +211,12 @@
     )(arrived)
 
 
-def pair_of(place, own, other):
-    vmem = pl.BlockSpec(memory_space=pltpu.VMEM)
-    return pl.pallas_call(
-        join_kernel,
-        out_shape=jax.ShapeDtypeStruct((ROWS, COLS), bf16),
-        in_specs=[pl.BlockSpec(memory_space=pltpu.SMEM), vmem, vmem],
-        compiler_params=pltpu.CompilerParams(vmem_limit_bytes=SMALL_VMEM_LIMIT),
-        cost_estimate=pl.CostEstimate(flops=100_000, bytes_accessed=100_000, transcendentals=0),
-        name="pair",
-    )(place, own, other)
-
-
-def held_of(place, other, pair, arrived):
+def held_of(place, others, arrived):
     vmem = pl.BlockSpec(memory_space=pltpu.VMEM)
     return pl.pallas_call(
         held_kernel,
         out_shape=pltpu.HBM((OWNERS, STATE, COLS), bf16),
-        in_specs=[pl.BlockSpec(memory_space=pltpu.SMEM), vmem, vmem, vmem],
+        in_specs=[pl.BlockSpec(memory_space=pltpu.SMEM)] + [vmem] * 4,
         out_specs=pl.BlockSpec(memory_space=pltpu.HBM),
         scratch_shapes=[
             pltpu.VMEM((OWNERS, STATE, COLS), bf16),
@@ -241,7 +225,7 @@
         compiler_params=pltpu.CompilerParams(vmem_limit_bytes=HELD_VMEM_LIMIT),
         cost_estimate=pl.CostEstimate(flops=4_000_000, bytes_accessed=4_000_000, transcendentals=0),
         name="held",
-    )(place, other, pair, arrived)
+    )(place, *others, arrived)
 
 
 def local_kernel(
@@ -442,9 +426,8 @@
     arrived, local, lead = lax.optimization_barrier((arrived, local, lead))
     place = (lax.axis_index("seq") // STEP).astype(jnp.int32)[None]
     total = total_of(arrived)
-    other = swap_runs(total, 1, ways)
-    pair = swap_runs(pair_of(place, total, other), 3, ways)
-    held = held_of(place, other, pair, arrived)
+    others = [swap_runs(total, bits, ways) for bits in (1, 2, 3)]
+    held = held_of(place, others, arrived)
     held = exchange(held, devices)
     (local,) = local_of(1, (local,), *args)
     return outputs_of(lead, readout, held, local)

time: 98.1 us -> 99.1 us (1.010)
  waiting for transfers between devices: 44.5 us -> 46.9 us
  starting transfers between devices: 26.9 us -> 25.5 us
    ppermute x2 -> x3, waiting for transfers between devices: 2.65 us -> 5.08 us  [swap_runs(): return lax.ppermute(v, 'seq', [(i, i ^ bits * STEP) for i in range(ways)])]
    all_to_all x2, starting transfers between devices: 19.2 us -> 18.1 us  [exchange(): lax.all_to_all(v, ('seq', 'head'), split_axis=0, concat_axis=0, tiled=Tru...]
    ppermute x2 -> x3, starting transfers between devices: 7.67 us -> 7.39 us  [swap_runs(): return lax.ppermute(v, 'seq', [(i, i ^ bits * STEP) for i in range(ways)])]
  transfers between devices with their start and end apart: 4 -> 5, of which waited for: 4 -> 3; matrix products, arithmetic and copies ran while one was open for 0% -> 0% of each run, Pallas kernels for 14% -> 14%
where the time goes in v6:
time: 99.1 us; the launch traced here: 98.7 us
  waiting for transfers between devices  46.9 us (47%)
  Pallas kernels  26.1 us (26%)
  starting transfers between devices  25.5 us (26%)
    all_to_all x2, waiting for transfers between devices, exchange(): lax.all_to_all(v, ('seq', 'head'), split_axis=0, concat_axis=0, tiled=Tru...  41.8 us
    all_to_all x2, starting transfers between devices, exchange(): lax.all_to_all(v, ('seq', 'head'), split_axis=0, concat_axis=0, tiled=Tru...  18.1 us
    pallas_call x2, Pallas kernels, local_of(): pl.pallas_call(functools.partial(local_kernel, part), out_shape=[jax.Shap...  14.1 us
    ppermute x3, starting transfers between devices, swap_runs(): return lax.ppermute(v, 'seq', [(i, i ^ bits * STEP) for i in range(ways)])  7.39 us
    pallas_call x1, Pallas kernels, states_of(): pl.pallas_call(state_kernel, out_shape=jax.ShapeDtypeStruct((OWNERS, ROWS...  5.15 us
    ppermute x3, waiting for transfers between devices, swap_runs(): return lax.ppermute(v, 'seq', [(i, i ^ bits * STEP) for i in range(ways)])  5.08 us
    pallas_call x1, Pallas kernels, outputs_of(): pl.pallas_call(out_kernel, out_shape=jax.ShapeDtypeStruct((TOK, HEADS * H...  4.89 us
  transfers between devices with their start and end apart: 5, of which 3 were waited for; matrix products, arithmetic and copies ran while one was open for 0% of the time, Pallas kernels for 14%

profile of v6, /device:TPU:1, one launch (start us, length us, event | category | flops | bytes accessed | tf_op | source)
XLA Modules:
  0.0 98.7 jit_solution(10536783601967168804)
XLA Ops:
  0.0 5.2 %states.1 = bf16[64,136,128]{2,1,0:T(8,128)(2,1)} custom-call(bf16[256,8192]{1,0:T(8,128)(2,1)} %x_hbm.5, f32[256,128]{1,0:T(8,128)} %step_hbm.5, f32[256,128]{1,0:T(8,128)} %decay_hbm.5, bf16[256,1024]{1,0:T(8,128)(2,1)} %inject_hbm.5), custom_call_target="tpu_custom_call" | custom-call | flops 2000000000 | bytes 8000000 | tf_op jit(solution)/shard_map/states/pallas_call | solution.py:134
  5.2 10.4 %all-to-all-start = ((bf16[64,136,128]{2,1,0:T(8,128)(2,1)}), bf16[64,136,128]{2,1,0:T(8,128)(2,1)S(1)}, u32[]{:S(2)}, u32[]{:S(2)}) async-start(bf16[64,136,128]{2,1,0:T(8,128)(2,1)} %states.1), calls=%async_computation | async-start | bytes 4456448 | tf_op jit(solution)/shard_map/all_to_all | solution.py:408
  15.5 7.3 %local0.1 = (bf16[256,8192]{1,0:T(8,128)(2,1)}, f32[256,128]{1,0:T(8,128)}) custom-call(bf16[256,8192]{1,0:T(8,128)(2,1)} %x_hbm.5, f32[256,128]{1,0:T(8,128)} %step_hbm.5, f32[256,128]{1,0:T(8,128)} %decay_hbm.5, bf16[256,1024]{1,0:T(8,128)(2,1)} %inject_hbm.5, bf16[256,1024]{1,0:T(8,128)(2,1)} %readout_ref.1, f32[1,128]{1,0:T(1,128)} %bitcast.2), custom_call_target="tpu_custom_call" | custom-call | flops 2000000000 | bytes 6000000 | tf_op jit(solution)/shard_map/local0/pallas_call | solution.py:324
  22.9 21.4 %all-to-all-done.in_ref = bf16[64,136,128]{2,1,0:T(8,128)(2,1)S(1)} async-done(((bf16[64,136,128]{2,1,0:T(8,128)(2,1)}), bf16[64,136,128]{2,1,0:T(8,128)(2,1)S(1)}, u32[]{:S(2)}, u32[]{:S(2)}) %all-to-all-start) | async-done | bytes 2228256 | tf_op jit(solution)/shard_map/all_to_all | solution.py:408
  44.2 0.5 total.1
  44.7 5.2 %collective-permute-start.2 = (bf16[136,128]{1,0:T(8,128)(2,1)S(1)}, bf16[136,128]{1,0:T(8,128)(2,1)S(1)}, u32[]{:S(2)}, u32[]{:S(2)}) collective-permute-start(bf16[136,128]{1,0:T(8,128)(2,1)S(1)} %total.1), channel_id=1, source_target_pairs={{0,192},{16,208},{32,224},{48,240},{64,128},{80,144},{96,160},{112... | collective-permute-start | bytes 104456 | tf_op jit(solution)/shard_map/ppermute | solution.py:404
  50.0 1.2 %collective-permute-start.1 = (bf16[136,128]{1,0:T(8,128)(2,1)S(1)}, bf16[136,128]{1,0:T(8,128)(2,1)S(1)}, u32[]{:S(2)}, u32[]{:S(2)}) collective-permute-start(bf16[136,128]{1,0:T(8,128)(2,1)S(1)} %total.1), channel_id=1, source_target_pairs={{0,128},{16,144},{32,160},{48,176},{64,192},{80,208},{96,224},{112... | collective-permute-start | bytes 104456 | tf_op jit(solution)/shard_map/ppermute | solution.py:404
  51.1 1.0 %collective-permute-start = (bf16[136,128]{1,0:T(8,128)(2,1)S(1)}, bf16[136,128]{1,0:T(8,128)(2,1)S(1)}, u32[]{:S(2)}, u32[]{:S(2)}) collective-permute-start(bf16[136,128]{1,0:T(8,128)(2,1)S(1)} %total.1), channel_id=1, source_target_pairs={{0,64},{16,80},{32,96},{48,112},{64,0},{80,16},{96,32},{112,48},{1... | collective-permute-start | bytes 104456 | tf_op jit(solution)/shard_map/ppermute | solution.py:404
  52.1 0.0 collective-permute-done.2.three_ref
  52.1 5.1 %collective-permute-done.1.two_ref = bf16[136,128]{1,0:T(8,128)(2,1)S(1)} collective-permute-done((bf16[136,128]{1,0:T(8,128)(2,1)S(1)}, bf16[136,128]{1,0:T(8,128)(2,1)S(1)}, u32[]{:S(2)}, u32[]{:S(2)}) %collective-permute-start.1) | collective-permute-done | bytes 34848 | tf_op jit(solution)/shard_map/ppermute | solution.py:404
  57.2 0.0 collective-permute-done.one_ref
  57.2 1.5 %held.1 = bf16[64,128,128]{2,1,0:T(8,128)(2,1)} custom-call(s32[1]{0:T(128)} %bitcast.1.place_ref, bf16[136,128]{1,0:T(8,128)(2,1)S(1)} %collective-permute-done.one_ref, bf16[136,128]{1,0:T(8,128)(2,1)S(1)} %collective-permute-done.1.two_ref, bf16[136,128]{1,0:T(8,128)(2,1)S(1)} %collective-permute-done.2.three_ref, ...), custom_call_target="tpu_custom_call" | custom-call | flops 4000000 | bytes 4000000 | tf_op jit(solution)/shard_map/held/pallas_call | solution.py:216
  58.7 7.7 %all-to-all-start.1 = ((bf16[64,128,128]{2,1,0:T(8,128)(2,1)}), bf16[64,128,128]{2,1,0:T(8,128)(2,1)S(1)}, u32[]{:S(2)}, u32[]{:S(2)}) async-start(bf16[64,128,128]{2,1,0:T(8,128)(2,1)} %held.1), calls=%async_computation.1 | async-start | bytes 4194304 | tf_op jit(solution)/shard_map/all_to_all | solution.py:408
  66.4 0.0 copy-start
  66.5 0.0 copy-start.1
  66.5 6.7 %local1.1.local_hbm = bf16[256,8192]{1,0:T(8,128)(2,1)} custom-call(bf16[256,8192]{1,0:T(8,128)(2,1)} %x_hbm.5, f32[256,128]{1,0:T(8,128)} %step_hbm.5, f32[256,128]{1,0:T(8,128)} %decay_hbm.5, bf16[256,1024]{1,0:T(8,128)(2,1)} %inject_hbm.5, bf16[256,1024]{1,0:T(8,128)(2,1)} %readout_ref.1, f32[1,128]{1,0:T(1,128)} %bitcast.3, ...), custom_call_target="tpu_custom_call", output_to_operand_aliasing={{}: (6, {})} | custom-call | flops 2000000000 | bytes 6000000 | tf_op jit(solution)/shard_map/local1/pallas_call | solution.py:324
  73.2 20.4 %all-to-all-done.1.held_ref = bf16[64,128,128]{2,1,0:T(8,128)(2,1)S(1)} async-done(((bf16[64,128,128]{2,1,0:T(8,128)(2,1)}), bf16[64,128,128]{2,1,0:T(8,128)(2,1)S(1)}, u32[]{:S(2)}, u32[]{:S(2)}) %all-to-all-start.1) | async-done | bytes 2097184 | tf_op jit(solution)/shard_map/all_to_all | solution.py:408
  93.7 0.0 copy-done
  93.7 0.0 copy-done.1
  93.7 4.9 %outputs.1 = bf16[256,8192]{1,0:T(8,128)(2,1)} custom-call(f32[256,128]{1,0:T(8,128)S(1)} %copy-done.1, bf16[256,1024]{1,0:T(8,128)(2,1)S(1)} %copy-done, bf16[64,128,128]{2,1,0:T(8,128)(2,1)S(1)} %all-to-all-done.1.held_ref, bf16[256,8192]{1,0:T(8,128)(2,1)} %local1.1.local_hbm), custom_call_target="tpu_custom_call" | custom-call | flops 2000000000 | bytes 12000000 | tf_op jit(solution)/shard_map/outputs/pallas_call | solution.py:383
Async XLA Ops:
  5.2 39.1 %all-to-all-start = ((bf16[64,136,128]{2,1,0:T(8,128)(2,1)}), bf16[64,136,128]{2,1,0:T(8,128)(2,1)S(1)}, u32[]{:S(2)}, u32[]{:S(2)}) async-start(bf16[64,136,128]{2,1,0:T(8,128)(2,1)} %states.1), calls=%async_computation | async-start | bytes 4456448 | tf_op jit(solution)/shard_map/all_to_all | solution.py:408
  44.7 7.4 %collective-permute-start.2 = (bf16[136,128]{1,0:T(8,128)(2,1)S(1)}, bf16[136,128]{1,0:T(8,128)(2,1)S(1)}, u32[]{:S(2)}, u32[]{:S(2)}) collective-permute-start(bf16[136,128]{1,0:T(8,128)(2,1)S(1)} %total.1), channel_id=1, source_target_pairs={{0,192},{16,208},{32,224},{48,240},{64,128},{80,144},{96,160},{112... | collective-permute-start | bytes 104456 | tf_op jit(solution)/shard_map/ppermute | solution.py:404
  50.0 7.3 %collective-permute-start.1 = (bf16[136,128]{1,0:T(8,128)(2,1)S(1)}, bf16[136,128]{1,0:T(8,128)(2,1)S(1)}, u32[]{:S(2)}, u32[]{:S(2)}) collective-permute-start(bf16[136,128]{1,0:T(8,128)(2,1)S(1)} %total.1), channel_id=1, source_target_pairs={{0,128},{16,144},{32,160},{48,176},{64,192},{80,208},{96,224},{112... | collective-permute-start | bytes 104456 | tf_op jit(solution)/shard_map/ppermute | solution.py:404
  51.1 6.1 %collective-permute-start = (bf16[136,128]{1,0:T(8,128)(2,1)S(1)}, bf16[136,128]{1,0:T(8,128)(2,1)S(1)}, u32[]{:S(2)}, u32[]{:S(2)}) collective-permute-start(bf16[136,128]{1,0:T(8,128)(2,1)S(1)} %total.1), channel_id=1, source_target_pairs={{0,64},{16,80},{32,96},{48,112},{64,0},{80,16},{96,32},{112,48},{1... | collective-permute-start | bytes 104456 | tf_op jit(solution)/shard_map/ppermute | solution.py:404
  58.7 34.9 %all-to-all-start.1 = ((bf16[64,128,128]{2,1,0:T(8,128)(2,1)}), bf16[64,128,128]{2,1,0:T(8,128)(2,1)S(1)}, u32[]{:S(2)}, u32[]{:S(2)}) async-start(bf16[64,128,128]{2,1,0:T(8,128)(2,1)} %held.1), calls=%async_computation.1 | async-start | bytes 4194304 | tf_op jit(solution)/shard_map/all_to_all | solution.py:408
  66.4 27.2 %copy-start = (bf16[256,1024]{1,0:T(8,128)(2,1)S(1)}, bf16[256,1024]{1,0:T(8,128)(2,1)}, u32[]{:S(2)}) copy-start(bf16[256,1024]{1,0:T(8,128)(2,1)} %readout_ref.1) | copy-start | bytes 1572868
  66.5 27.2 %copy-start.1 = (f32[256,128]{1,0:T(8,128)S(1)}, f32[256,128]{1,0:T(8,128)}, u32[]{:S(2)}) copy-start(f32[256,128]{1,0:T(8,128)} %get-tuple-element.12.lead_ref) | copy-start | bytes 393220

commit v7 on v5

--- a/solution.py
+++ b/solution.py
@@ -16,7 +16,7 @@
 LANES = 128
 OWNERS = 64
 STEP = 4
-PIECES = 4
+PIECES = 8
 OWN_HEADS = HEADS // OWNERS
 COLS = OWN_HEADS * HEAD_DIM
 GROUP_COLS = HEADS // GROUPS * HEAD_DIM
@@ -381,11 +381,11 @@
             held = jnp.concatenate(
                 [held_ref[g * GROUP_OWNERS + i] for i in range(GROUP_OWNERS)], axis=1
             )
-            far_buf[g % 2] = dot(readout_ref[:, g * STATE : (g + 1) * STATE], held)
+            far_buf[g % 2] = dot(readout_ref[:, g * STATE : (g + 1) * STATE], held).astype(bf16)
         if g > 0:
             at = (g - 1) * GROUP_COLS
-            far = far_buf[(g - 1) % 2] * spread(lead_ref[...], at, GROUP_COLS)
-            out_buf[g - 1] = (far + local_buf[g - 1].astype(f32)).astype(bf16)
+            lead = spread(lead_ref[...], at, GROUP_COLS).astype(bf16)
+            out_buf[g - 1] = far_buf[(g - 1) % 2] * lead + local_buf[g - 1]
             sent += copies(
                 (out_buf.at[g - 1], out_hbm.at[:, pl.ds(at, GROUP_COLS)], out_sem.at[g - 1])
             )
@@ -402,7 +402,7 @@
         in_specs=[vmem, vmem, vmem, hbm],
         out_specs=hbm,
         scratch_shapes=[
-            pltpu.VMEM((2, TOK, GROUP_COLS), f32),
+            pltpu.VMEM((2, TOK, GROUP_COLS), bf16),
             pltpu.VMEM((GROUPS, TOK, GROUP_COLS), bf16),
             pltpu.VMEM((GROUPS, TOK, GROUP_COLS), bf16),
             pltpu.SemaphoreType.DMA((GROUPS,)),

time: 98.1 us -> 97.3 us (level)
  no operation moved by 1% of the time
where the time goes in v7:
time: 97.3 us; the launch traced here: 97 us
  waiting for transfers between devices  44.5 us (46%)
  starting transfers between devices  26.9 us (28%)
  Pallas kernels  25.4 us (26%)
    all_to_all x2, waiting for transfers between devices, exchange(): lax.all_to_all(v, ('seq', 'head'), split_axis=0, concat_axis=0, tiled=Tru...  41.8 us
    all_to_all x2, starting transfers between devices, exchange(): lax.all_to_all(v, ('seq', 'head'), split_axis=0, concat_axis=0, tiled=Tru...  19.2 us
    pallas_call x2, Pallas kernels, local_of(): pl.pallas_call(functools.partial(local_kernel, part), out_shape=[jax.Shap...  14.1 us
    ppermute x2, starting transfers between devices, swap_runs(): return lax.ppermute(v, 'seq', [(i, i ^ bits * STEP) for i in range(ways)])  7.67 us
    pallas_call x1, Pallas kernels, states_of(): pl.pallas_call(state_kernel, out_shape=jax.ShapeDtypeStruct((OWNERS, ROWS...  5.15 us
    pallas_call x1, Pallas kernels, outputs_of(): pl.pallas_call(out_kernel, out_shape=jax.ShapeDtypeStruct((TOK, HEADS * H...  4.18 us
    ppermute x2, waiting for transfers between devices, swap_runs(): return lax.ppermute(v, 'seq', [(i, i ^ bits * STEP) for i in range(ways)])  2.65 us
  transfers between devices with their start and end apart: 4, of which 4 were waited for; matrix products, arithmetic and copies ran while one was open for 0% of the time, Pallas kernels for 14%

profile of v7, /device:TPU:1, one launch (start us, length us, event | category | flops | bytes accessed | tf_op | source)
XLA Modules:
  0.0 97.0 jit_solution(4633902514000609264)
XLA Ops:
  0.0 5.2 %states.1 = bf16[64,136,128]{2,1,0:T(8,128)(2,1)} custom-call(bf16[256,8192]{1,0:T(8,128)(2,1)} %x_hbm.5, f32[256,128]{1,0:T(8,128)} %step_hbm.5, f32[256,128]{1,0:T(8,128)} %decay_hbm.5, bf16[256,1024]{1,0:T(8,128)(2,1)} %inject_hbm.5), custom_call_target="tpu_custom_call" | custom-call | flops 2000000000 | bytes 8000000 | tf_op jit(solution)/shard_map/states/pallas_call | solution.py:134
  5.2 10.4 %all-to-all-start = ((bf16[64,136,128]{2,1,0:T(8,128)(2,1)}), bf16[64,136,128]{2,1,0:T(8,128)(2,1)S(1)}, u32[]{:S(2)}, u32[]{:S(2)}) async-start(bf16[64,136,128]{2,1,0:T(8,128)(2,1)} %states.1), calls=%async_computation | async-start | bytes 4456448 | tf_op jit(solution)/shard_map/all_to_all | solution.py:424
  15.5 7.3 %local0.1 = (bf16[256,8192]{1,0:T(8,128)(2,1)}, f32[256,128]{1,0:T(8,128)}) custom-call(bf16[256,8192]{1,0:T(8,128)(2,1)} %x_hbm.5, f32[256,128]{1,0:T(8,128)} %step_hbm.5, f32[256,128]{1,0:T(8,128)} %decay_hbm.5, bf16[256,1024]{1,0:T(8,128)(2,1)} %inject_hbm.5, bf16[256,1024]{1,0:T(8,128)(2,1)} %readout_ref.1, f32[1,128]{1,0:T(1,128)} %bitcast.2), custom_call_target="tpu_custom_call" | custom-call | flops 2000000000 | bytes 6000000 | tf_op jit(solution)/shard_map/local0/pallas_call | solution.py:340
  22.8 21.4 %all-to-all-done.in_ref = bf16[64,136,128]{2,1,0:T(8,128)(2,1)S(1)} async-done(((bf16[64,136,128]{2,1,0:T(8,128)(2,1)}), bf16[64,136,128]{2,1,0:T(8,128)(2,1)S(1)}, u32[]{:S(2)}, u32[]{:S(2)}) %all-to-all-start) | async-done | bytes 2228256 | tf_op jit(solution)/shard_map/all_to_all | solution.py:424
  44.2 0.5 total.1.own_ref
  44.7 3.1 %collective-permute-start = (bf16[136,128]{1,0:T(8,128)(2,1)S(1)}, bf16[136,128]{1,0:T(8,128)(2,1)S(1)}, u32[]{:S(2)}, u32[]{:S(2)}) collective-permute-start(bf16[136,128]{1,0:T(8,128)(2,1)S(1)} %total.1.own_ref), channel_id=1, source_target_pairs={{0,64},{16,80},{32,96},{48,112},{64,0},{80,16},{96,32},{112,48},{1... | collective-permute-start | bytes 104456 | tf_op jit(solution)/shard_map/ppermute | solution.py:420
  47.8 1.3 %collective-permute-done.other_ref = bf16[136,128]{1,0:T(8,128)(2,1)S(1)} collective-permute-done((bf16[136,128]{1,0:T(8,128)(2,1)S(1)}, bf16[136,128]{1,0:T(8,128)(2,1)S(1)}, u32[]{:S(2)}, u32[]{:S(2)}) %collective-permute-start) | collective-permute-done | bytes 34848 | tf_op jit(solution)/shard_map/ppermute | solution.py:420
  49.2 4.6 %collective-permute-start.1 = (bf16[136,128]{1,0:T(8,128)(2,1)S(1)}, bf16[136,128]{1,0:T(8,128)(2,1)S(1)}, u32[]{:S(2)}, u32[]{:S(2)}) collective-permute-start(bf16[136,128]{1,0:T(8,128)(2,1)S(1)} %pair.1), channel_id=1, source_target_pairs={{0,192},{16,208},{32,224},{48,240},{64,128},{80,144},{96,160},{112... | collective-permute-start | bytes 104456 | tf_op jit(solution)/shard_map/ppermute | solution.py:420
  53.8 1.3 %collective-permute-done.1.pair_ref = bf16[136,128]{1,0:T(8,128)(2,1)S(1)} collective-permute-done((bf16[136,128]{1,0:T(8,128)(2,1)S(1)}, bf16[136,128]{1,0:T(8,128)(2,1)S(1)}, u32[]{:S(2)}, u32[]{:S(2)}) %collective-permute-start.1) | collective-permute-done | bytes 34848 | tf_op jit(solution)/shard_map/ppermute | solution.py:420
  55.1 1.4 %held.1 = bf16[64,128,128]{2,1,0:T(8,128)(2,1)} custom-call(s32[1]{0:T(128)} %bitcast.1.place_ref, bf16[136,128]{1,0:T(8,128)(2,1)S(1)} %collective-permute-done.other_ref, bf16[136,128]{1,0:T(8,128)(2,1)S(1)} %collective-permute-done.1.pair_ref, bf16[64,136,128]{2,1,0:T(8,128)(2,1)S(1)} %all-to-all-done.in_ref), custom_call_target="tpu_custom_call" | custom-call | flops 4000000 | bytes 4000000 | tf_op jit(solution)/shard_map/held/pallas_call | solution.py:232
  56.6 8.9 %all-to-all-start.1 = ((bf16[64,128,128]{2,1,0:T(8,128)(2,1)}), bf16[64,128,128]{2,1,0:T(8,128)(2,1)S(1)}, u32[]{:S(2)}, u32[]{:S(2)}) async-start(bf16[64,128,128]{2,1,0:T(8,128)(2,1)} %held.1), calls=%async_computation.1 | async-start | bytes 4194304 | tf_op jit(solution)/shard_map/all_to_all | solution.py:424
  65.4 0.0 copy-start
  65.4 0.0 copy-start.1
  65.5 6.8 %local1.1.local_hbm = bf16[256,8192]{1,0:T(8,128)(2,1)} custom-call(bf16[256,8192]{1,0:T(8,128)(2,1)} %x_hbm.5, f32[256,128]{1,0:T(8,128)} %step_hbm.5, f32[256,128]{1,0:T(8,128)} %decay_hbm.5, bf16[256,1024]{1,0:T(8,128)(2,1)} %inject_hbm.5, bf16[256,1024]{1,0:T(8,128)(2,1)} %readout_ref.1, f32[1,128]{1,0:T(1,128)} %bitcast.3, ...), custom_call_target="tpu_custom_call", output_to_operand_aliasing={{}: (6, {})} | custom-call | flops 2000000000 | bytes 6000000 | tf_op jit(solution)/shard_map/local1/pallas_call | solution.py:340
  72.2 20.4 %all-to-all-done.1.held_ref = bf16[64,128,128]{2,1,0:T(8,128)(2,1)S(1)} async-done(((bf16[64,128,128]{2,1,0:T(8,128)(2,1)}), bf16[64,128,128]{2,1,0:T(8,128)(2,1)S(1)}, u32[]{:S(2)}, u32[]{:S(2)}) %all-to-all-start.1) | async-done | bytes 2097184 | tf_op jit(solution)/shard_map/all_to_all | solution.py:424
  92.6 0.0 copy-done
  92.6 0.0 copy-done.1
  92.6 4.2 %outputs.1 = bf16[256,8192]{1,0:T(8,128)(2,1)} custom-call(f32[256,128]{1,0:T(8,128)S(1)} %copy-done.1, bf16[256,1024]{1,0:T(8,128)(2,1)S(1)} %copy-done, bf16[64,128,128]{2,1,0:T(8,128)(2,1)S(1)} %all-to-all-done.1.held_ref, bf16[256,8192]{1,0:T(8,128)(2,1)} %local1.1.local_hbm), custom_call_target="tpu_custom_call" | custom-call | flops 2000000000 | bytes 12000000 | tf_op jit(solution)/shard_map/outputs/pallas_call | solution.py:399
  (1 shorter events, 0.0 us)
Async XLA Ops:
  5.2 39.1 %all-to-all-start = ((bf16[64,136,128]{2,1,0:T(8,128)(2,1)}), bf16[64,136,128]{2,1,0:T(8,128)(2,1)S(1)}, u32[]{:S(2)}, u32[]{:S(2)}) async-start(bf16[64,136,128]{2,1,0:T(8,128)(2,1)} %states.1), calls=%async_computation | async-start | bytes 4456448 | tf_op jit(solution)/shard_map/all_to_all | solution.py:424
  44.7 4.4 %collective-permute-start = (bf16[136,128]{1,0:T(8,128)(2,1)S(1)}, bf16[136,128]{1,0:T(8,128)(2,1)S(1)}, u32[]{:S(2)}, u32[]{:S(2)}) collective-permute-start(bf16[136,128]{1,0:T(8,128)(2,1)S(1)} %total.1.own_ref), channel_id=1, source_target_pairs={{0,64},{16,80},{32,96},{48,112},{64,0},{80,16},{96,32},{112,48},{1... | collective-permute-start | bytes 104456 | tf_op jit(solution)/shard_map/ppermute | solution.py:420
  49.2 5.9 %collective-permute-start.1 = (bf16[136,128]{1,0:T(8,128)(2,1)S(1)}, bf16[136,128]{1,0:T(8,128)(2,1)S(1)}, u32[]{:S(2)}, u32[]{:S(2)}) collective-permute-start(bf16[136,128]{1,0:T(8,128)(2,1)S(1)} %pair.1), channel_id=1, source_target_pairs={{0,192},{16,208},{32,224},{48,240},{64,128},{80,144},{96,160},{112... | collective-permute-start | bytes 104456 | tf_op jit(solution)/shard_map/ppermute | solution.py:420
  56.6 36.1 %all-to-all-start.1 = ((bf16[64,128,128]{2,1,0:T(8,128)(2,1)}), bf16[64,128,128]{2,1,0:T(8,128)(2,1)S(1)}, u32[]{:S(2)}, u32[]{:S(2)}) async-start(bf16[64,128,128]{2,1,0:T(8,128)(2,1)} %held.1), calls=%async_computation.1 | async-start | bytes 4194304 | tf_op jit(solution)/shard_map/all_to_all | solution.py:424
  65.4 27.2 %copy-start = (bf16[256,1024]{1,0:T(8,128)(2,1)S(1)}, bf16[256,1024]{1,0:T(8,128)(2,1)}, u32[]{:S(2)}) copy-start(bf16[256,1024]{1,0:T(8,128)(2,1)} %readout_ref.1) | copy-start | bytes 1572868
  65.4 27.2 %copy-start.1 = (f32[256,128]{1,0:T(8,128)S(1)}, f32[256,128]{1,0:T(8,128)}, u32[]{:S(2)}) copy-start(f32[256,128]{1,0:T(8,128)} %get-tuple-element.12.lead_ref) | copy-start | bytes 393220

commit v8 on v7

--- a/solution.py
+++ b/solution.py
@@ -439,6 +439,7 @@
     args = (features, step_size, log_decay, inject, readout, skip_gain[None, :])
     arrived = exchange(states_of(features, step_size, log_decay, inject), devices)
     local, lead = local_of(0, (), *args)
+    (local,) = local_of(1, (local,), *args)
     arrived, local, lead = lax.optimization_barrier((arrived, local, lead))
     place = (lax.axis_index("seq") // STEP).astype(jnp.int32)[None]
     total = total_of(arrived)
@@ -446,7 +447,6 @@
     pair = swap_runs(pair_of(place, total, other), 3, ways)
     held = held_of(place, other, pair, arrived)
     held = exchange(held, devices)
-    (local,) = local_of(1, (local,), *args)
     return outputs_of(lead, readout, held, local)
 
 

time: 97.3 us -> 97.4 us (level)
  blocking collectives: 0 us -> 36.1 us
  waiting for transfers between devices: 44.5 us -> 17.4 us
  starting transfers between devices: 26.9 us -> 18 us
    all_to_all x0 -> x1, blocking collectives: none -> 36.1 us  [exchange(): lax.all_to_all(v, ('seq', 'head'), split_axis=0, concat_axis=0, tiled=Tru...]
    all_to_all x2 -> x1, waiting for transfers between devices: 41.8 us -> 14.7 us  [exchange(): lax.all_to_all(v, ('seq', 'head'), split_axis=0, concat_axis=0, tiled=Tru...]
    all_to_all x2 -> x1, starting transfers between devices: 19.2 us -> 10.4 us  [exchange(): lax.all_to_all(v, ('seq', 'head'), split_axis=0, concat_axis=0, tiled=Tru...]
  transfers between devices with their start and end apart: 4 -> 3, of which waited for: 4 -> 3; matrix products, arithmetic and copies ran while one was open for 0% -> 0% of each run, Pallas kernels for 14% -> 14%
where the time goes in v8:
time: 97.4 us; the launch traced here: 97 us
  blocking collectives  36.1 us (37%)
  Pallas kernels  25.3 us (26%)
  starting transfers between devices  18 us (18%)
  waiting for transfers between devices  17.4 us (18%)
    all_to_all x1, blocking collectives, exchange(): lax.all_to_all(v, ('seq', 'head'), split_axis=0, concat_axis=0, tiled=Tru...  36.1 us
    all_to_all x1, waiting for transfers between devices, exchange(): lax.all_to_all(v, ('seq', 'head'), split_axis=0, concat_axis=0, tiled=Tru...  14.7 us
    pallas_call x2, Pallas kernels, local_of(): pl.pallas_call(functools.partial(local_kernel, part), out_shape=[jax.Shap...  14 us
    all_to_all x1, starting transfers between devices, exchange(): lax.all_to_all(v, ('seq', 'head'), split_axis=0, concat_axis=0, tiled=Tru...  10.4 us
    ppermute x2, starting transfers between devices, swap_runs(): return lax.ppermute(v, 'seq', [(i, i ^ bits * STEP) for i in range(ways)])  7.67 us
    pallas_call x1, Pallas kernels, states_of(): pl.pallas_call(state_kernel, out_shape=jax.ShapeDtypeStruct((OWNERS, ROWS...  5.15 us
    pallas_call x1, Pallas kernels, outputs_of(): pl.pallas_call(out_kernel, out_shape=jax.ShapeDtypeStruct((TOK, HEADS * H...  4.18 us
    ppermute x2, waiting for transfers between devices, swap_runs(): return lax.ppermute(v, 'seq', [(i, i ^ bits * STEP) for i in range(ways)])  2.65 us
  transfers between devices with their start and end apart: 3, of which 3 were waited for; matrix products, arithmetic and copies ran while one was open for 0% of the time, Pallas kernels for 14%

profile of v8, /device:TPU:1, one launch (start us, length us, event | category | flops | bytes accessed | tf_op | source)
XLA Modules:
  0.0 97.0 jit_solution(12937543219859673845)
XLA Ops:
  0.0 5.2 %states.1 = bf16[64,136,128]{2,1,0:T(8,128)(2,1)} custom-call(bf16[256,8192]{1,0:T(8,128)(2,1)} %x_hbm.5, f32[256,128]{1,0:T(8,128)} %step_hbm.5, f32[256,128]{1,0:T(8,128)} %decay_hbm.5, bf16[256,1024]{1,0:T(8,128)(2,1)} %inject_hbm.5), custom_call_target="tpu_custom_call" | custom-call | flops 2000000000 | bytes 8000000 | tf_op jit(solution)/shard_map/states/pallas_call | solution.py:134
  5.2 10.4 %all-to-all-start = ((bf16[64,136,128]{2,1,0:T(8,128)(2,1)}), bf16[64,136,128]{2,1,0:T(8,128)(2,1)S(1)}, u32[]{:S(2)}, u32[]{:S(2)}) async-start(bf16[64,136,128]{2,1,0:T(8,128)(2,1)} %states.1), calls=%async_computation | async-start | bytes 4456448 | tf_op jit(solution)/shard_map/all_to_all | solution.py:424
  15.5 7.3 %local0.1 = (bf16[256,8192]{1,0:T(8,128)(2,1)}, f32[256,128]{1,0:T(8,128)}) custom-call(bf16[256,8192]{1,0:T(8,128)(2,1)} %x_hbm.5, f32[256,128]{1,0:T(8,128)} %step_hbm.5, f32[256,128]{1,0:T(8,128)} %decay_hbm.5, bf16[256,1024]{1,0:T(8,128)(2,1)} %inject_hbm.5, bf16[256,1024]{1,0:T(8,128)(2,1)} %readout_ref.1, f32[1,128]{1,0:T(1,128)} %bitcast.2), custom_call_target="tpu_custom_call" | custom-call | flops 2000000000 | bytes 6000000 | tf_op jit(solution)/shard_map/local0/pallas_call | solution.py:340
  22.8 6.7 %local1.1.local_hbm = bf16[256,8192]{1,0:T(8,128)(2,1)} custom-call(bf16[256,8192]{1,0:T(8,128)(2,1)} %x_hbm.5, f32[256,128]{1,0:T(8,128)} %step_hbm.5, f32[256,128]{1,0:T(8,128)} %decay_hbm.5, bf16[256,1024]{1,0:T(8,128)(2,1)} %inject_hbm.5, bf16[256,1024]{1,0:T(8,128)(2,1)} %readout_ref.1, f32[1,128]{1,0:T(1,128)} %bitcast.3, ...), custom_call_target="tpu_custom_call", output_to_operand_aliasing={{}: (6, {})} | custom-call | flops 2000000000 | bytes 6000000 | tf_op jit(solution)/shard_map/local1/pallas_call | solution.py:340
  29.5 14.7 %all-to-all-done.in_ref = bf16[64,136,128]{2,1,0:T(8,128)(2,1)S(1)} async-done(((bf16[64,136,128]{2,1,0:T(8,128)(2,1)}), bf16[64,136,128]{2,1,0:T(8,128)(2,1)S(1)}, u32[]{:S(2)}, u32[]{:S(2)}) %all-to-all-start) | async-done | bytes 2228256 | tf_op jit(solution)/shard_map/all_to_all | solution.py:424
  44.2 0.5 total.1.own_ref
  44.7 3.1 %collective-permute-start = (bf16[136,128]{1,0:T(8,128)(2,1)S(1)}, bf16[136,128]{1,0:T(8,128)(2,1)S(1)}, u32[]{:S(2)}, u32[]{:S(2)}) collective-permute-start(bf16[136,128]{1,0:T(8,128)(2,1)S(1)} %total.1.own_ref), channel_id=1, source_target_pairs={{0,64},{16,80},{32,96},{48,112},{64,0},{80,16},{96,32},{112,48},{1... | collective-permute-start | bytes 104456 | tf_op jit(solution)/shard_map/ppermute | solution.py:420
  47.8 1.3 %collective-permute-done.other_ref = bf16[136,128]{1,0:T(8,128)(2,1)S(1)} collective-permute-done((bf16[136,128]{1,0:T(8,128)(2,1)S(1)}, bf16[136,128]{1,0:T(8,128)(2,1)S(1)}, u32[]{:S(2)}, u32[]{:S(2)}) %collective-permute-start) | collective-permute-done | bytes 34848 | tf_op jit(solution)/shard_map/ppermute | solution.py:420
  49.2 0.0 copy-start
  49.2 0.0 copy-start.1
  49.2 4.6 %collective-permute-start.1 = (bf16[136,128]{1,0:T(8,128)(2,1)S(1)}, bf16[136,128]{1,0:T(8,128)(2,1)S(1)}, u32[]{:S(2)}, u32[]{:S(2)}) collective-permute-start(bf16[136,128]{1,0:T(8,128)(2,1)S(1)} %pair.1), channel_id=1, source_target_pairs={{0,192},{16,208},{32,224},{48,240},{64,128},{80,144},{96,160},{112... | collective-permute-start | bytes 104456 | tf_op jit(solution)/shard_map/ppermute | solution.py:420
  53.8 1.3 %collective-permute-done.1.pair_ref = bf16[136,128]{1,0:T(8,128)(2,1)S(1)} collective-permute-done((bf16[136,128]{1,0:T(8,128)(2,1)S(1)}, bf16[136,128]{1,0:T(8,128)(2,1)S(1)}, u32[]{:S(2)}, u32[]{:S(2)}) %collective-permute-start.1) | collective-permute-done | bytes 34848 | tf_op jit(solution)/shard_map/ppermute | solution.py:420
  55.1 1.4 %held.1 = bf16[64,128,128]{2,1,0:T(8,128)(2,1)} custom-call(s32[1]{0:T(128)} %bitcast.1.place_ref, bf16[136,128]{1,0:T(8,128)(2,1)S(1)} %collective-permute-done.other_ref, bf16[136,128]{1,0:T(8,128)(2,1)S(1)} %collective-permute-done.1.pair_ref, bf16[64,136,128]{2,1,0:T(8,128)(2,1)S(1)} %all-to-all-done.in_ref), custom_call_target="tpu_custom_call" | custom-call | flops 4000000 | bytes 4000000 | tf_op jit(solution)/shard_map/held/pallas_call | solution.py:232
  56.6 36.1 %all_to_all.10.held_ref = bf16[64,128,128]{2,1,0:T(8,128)(2,1)S(1)} all-to-all(bf16[64,128,128]{2,1,0:T(8,128)(2,1)} %held.1), channel_id=1, replica_groups={{0,1,2,3,4,5,6,7,8,9,10,11,12,13,14,15,16,17,18,19,20,21,22,23,24,25,26..., dimensions={0} | all-to-all | bytes 4194304 | tf_op jit(solution)/shard_map/all_to_all | solution.py:424
  92.7 0.0 copy-done
  92.7 0.0 copy-done.1
  92.7 4.2 %outputs.1 = bf16[256,8192]{1,0:T(8,128)(2,1)} custom-call(f32[256,128]{1,0:T(8,128)S(1)} %copy-done.1, bf16[256,1024]{1,0:T(8,128)(2,1)S(1)} %copy-done, bf16[64,128,128]{2,1,0:T(8,128)(2,1)S(1)} %all_to_all.10.held_ref, bf16[256,8192]{1,0:T(8,128)(2,1)} %local1.1.local_hbm), custom_call_target="tpu_custom_call" | custom-call | flops 2000000000 | bytes 12000000 | tf_op jit(solution)/shard_map/outputs/pallas_call | solution.py:399
  (1 shorter events, 0.0 us)
Async XLA Ops:
  5.2 39.1 %all-to-all-start = ((bf16[64,136,128]{2,1,0:T(8,128)(2,1)}), bf16[64,136,128]{2,1,0:T(8,128)(2,1)S(1)}, u32[]{:S(2)}, u32[]{:S(2)}) async-start(bf16[64,136,128]{2,1,0:T(8,128)(2,1)} %states.1), calls=%async_computation | async-start | bytes 4456448 | tf_op jit(solution)/shard_map/all_to_all | solution.py:424
  44.7 4.4 %collective-permute-start = (bf16[136,128]{1,0:T(8,128)(2,1)S(1)}, bf16[136,128]{1,0:T(8,128)(2,1)S(1)}, u32[]{:S(2)}, u32[]{:S(2)}) collective-permute-start(bf16[136,128]{1,0:T(8,128)(2,1)S(1)} %total.1.own_ref), channel_id=1, source_target_pairs={{0,64},{16,80},{32,96},{48,112},{64,0},{80,16},{96,32},{112,48},{1... | collective-permute-start | bytes 104456 | tf_op jit(solution)/shard_map/ppermute | solution.py:420
  49.2 43.5 %copy-start = (bf16[256,1024]{1,0:T(8,128)(2,1)S(1)}, bf16[256,1024]{1,0:T(8,128)(2,1)}, u32[]{:S(2)}) copy-start(bf16[256,1024]{1,0:T(8,128)(2,1)} %readout_ref.1) | copy-start | bytes 1572868
  49.2 43.5 %copy-start.1 = (f32[256,128]{1,0:T(8,128)S(1)}, f32[256,128]{1,0:T(8,128)}, u32[]{:S(2)}) copy-start(f32[256,128]{1,0:T(8,128)} %get-tuple-element.12.lead_ref) | copy-start | bytes 393220
  49.2 5.9 %collective-permute-start.1 = (bf16[136,128]{1,0:T(8,128)(2,1)S(1)}, bf16[136,128]{1,0:T(8,128)(2,1)S(1)}, u32[]{:S(2)}, u32[]{:S(2)}) collective-permute-start(bf16[136,128]{1,0:T(8,128)(2,1)S(1)} %pair.1), channel_id=1, source_target_pairs={{0,192},{16,208},{32,224},{48,240},{64,128},{80,144},{96,160},{112... | collective-permute-start | bytes 104456 | tf_op jit(solution)/shard_map/ppermute | solution.py:420

commit v9 on v7

--- a/solution.py
+++ b/solution.py
@@ -383,12 +383,19 @@
             )
             far_buf[g % 2] = dot(readout_ref[:, g * STATE : (g + 1) * STATE], held).astype(bf16)
         if g > 0:
-            at = (g - 1) * GROUP_COLS
-            lead = spread(lead_ref[...], at, GROUP_COLS).astype(bf16)
-            out_buf[g - 1] = far_buf[(g - 1) % 2] * lead + local_buf[g - 1]
-            sent += copies(
-                (out_buf.at[g - 1], out_hbm.at[:, pl.ds(at, GROUP_COLS)], out_sem.at[g - 1])
-            )
+            for w in range(GROUP_COLS // WIDE):
+                part = pl.ds(w * WIDE, WIDE)
+                at = (g - 1) * GROUP_COLS + w * WIDE
+                lead = spread(lead_ref[...], at, WIDE).astype(bf16)
+                far = far_buf[(g - 1) % 2, :, part]
+                out_buf[g - 1, :, part] = far * lead + local_buf[g - 1, :, part]
+                sent += copies(
+                    (
+                        out_buf.at[g - 1, :, part],
+                        out_hbm.at[:, pl.ds(at, WIDE)],
+                        out_sem.at[g - 1, w],
+                    )
+                )
     for c in sent:
         c.wait()
 
@@ -406,7 +413,7 @@
             pltpu.VMEM((GROUPS, TOK, GROUP_COLS), bf16),
             pltpu.VMEM((GROUPS, TOK, GROUP_COLS), bf16),
             pltpu.SemaphoreType.DMA((GROUPS,)),
-            pltpu.SemaphoreType.DMA((GROUPS,)),
+            pltpu.SemaphoreType.DMA((GROUPS, GROUP_COLS // WIDE)),
         ],
         compiler_params=pltpu.CompilerParams(vmem_limit_bytes=OUT_VMEM_LIMIT),
         cost_estimate=pl.CostEstimate(

time: 97.3 us -> 97.3 us (level)
  no operation moved by 1% of the time
where the time goes in v9:
time: 97.3 us; the launch traced here: 97 us
  waiting for transfers between devices  44.5 us (46%)
  starting transfers between devices  26.9 us (28%)
  Pallas kernels  25.4 us (26%)
    all_to_all x2, waiting for transfers between devices, exchange(): lax.all_to_all(v, ('seq', 'head'), split_axis=0, concat_axis=0, tiled=Tru...  41.8 us
    all_to_all x2, starting transfers between devices, exchange(): lax.all_to_all(v, ('seq', 'head'), split_axis=0, concat_axis=0, tiled=Tru...  19.2 us
    pallas_call x2, Pallas kernels, local_of(): pl.pallas_call(functools.partial(local_kernel, part), out_shape=[jax.Shap...  14.1 us
    ppermute x2, starting transfers between devices, swap_runs(): return lax.ppermute(v, 'seq', [(i, i ^ bits * STEP) for i in range(ways)])  7.67 us
    pallas_call x1, Pallas kernels, states_of(): pl.pallas_call(state_kernel, out_shape=jax.ShapeDtypeStruct((OWNERS, ROWS...  5.15 us
    pallas_call x1, Pallas kernels, outputs_of(): pl.pallas_call(out_kernel, out_shape=jax.ShapeDtypeStruct((TOK, HEADS * H...  4.15 us
    ppermute x2, waiting for transfers between devices, swap_runs(): return lax.ppermute(v, 'seq', [(i, i ^ bits * STEP) for i in range(ways)])  2.65 us
  transfers between devices with their start and end apart: 4, of which 4 were waited for; matrix products, arithmetic and copies ran while one was open for 0% of the time, Pallas kernels for 14%

profile of v9, /device:TPU:1, one launch (start us, length us, event | category | flops | bytes accessed | tf_op | source)
XLA Modules:
  0.0 97.0 jit_solution(15925136428122977017)
XLA Ops:
  0.0 5.2 %states.1 = bf16[64,136,128]{2,1,0:T(8,128)(2,1)} custom-call(bf16[256,8192]{1,0:T(8,128)(2,1)} %x_hbm.5, f32[256,128]{1,0:T(8,128)} %step_hbm.5, f32[256,128]{1,0:T(8,128)} %decay_hbm.5, bf16[256,1024]{1,0:T(8,128)(2,1)} %inject_hbm.5), custom_call_target="tpu_custom_call" | custom-call | flops 2000000000 | bytes 8000000 | tf_op jit(solution)/shard_map/states/pallas_call | solution.py:134
  5.2 10.4 %all-to-all-start = ((bf16[64,136,128]{2,1,0:T(8,128)(2,1)}), bf16[64,136,128]{2,1,0:T(8,128)(2,1)S(1)}, u32[]{:S(2)}, u32[]{:S(2)}) async-start(bf16[64,136,128]{2,1,0:T(8,128)(2,1)} %states.1), calls=%async_computation | async-start | bytes 4456448 | tf_op jit(solution)/shard_map/all_to_all | solution.py:431
  15.5 7.3 %local0.1 = (bf16[256,8192]{1,0:T(8,128)(2,1)}, f32[256,128]{1,0:T(8,128)}) custom-call(bf16[256,8192]{1,0:T(8,128)(2,1)} %x_hbm.5, f32[256,128]{1,0:T(8,128)} %step_hbm.5, f32[256,128]{1,0:T(8,128)} %decay_hbm.5, bf16[256,1024]{1,0:T(8,128)(2,1)} %inject_hbm.5, bf16[256,1024]{1,0:T(8,128)(2,1)} %readout_ref.1, f32[1,128]{1,0:T(1,128)} %bitcast.2), custom_call_target="tpu_custom_call" | custom-call | flops 2000000000 | bytes 6000000 | tf_op jit(solution)/shard_map/local0/pallas_call | solution.py:340
  22.8 21.4 %all-to-all-done.in_ref = bf16[64,136,128]{2,1,0:T(8,128)(2,1)S(1)} async-done(((bf16[64,136,128]{2,1,0:T(8,128)(2,1)}), bf16[64,136,128]{2,1,0:T(8,128)(2,1)S(1)}, u32[]{:S(2)}, u32[]{:S(2)}) %all-to-all-start) | async-done | bytes 2228256 | tf_op jit(solution)/shard_map/all_to_all | solution.py:431
  44.2 0.5 total.1.own_ref
  44.7 3.1 %collective-permute-start = (bf16[136,128]{1,0:T(8,128)(2,1)S(1)}, bf16[136,128]{1,0:T(8,128)(2,1)S(1)}, u32[]{:S(2)}, u32[]{:S(2)}) collective-permute-start(bf16[136,128]{1,0:T(8,128)(2,1)S(1)} %total.1.own_ref), channel_id=1, source_target_pairs={{0,64},{16,80},{32,96},{48,112},{64,0},{80,16},{96,32},{112,48},{1... | collective-permute-start | bytes 104456 | tf_op jit(solution)/shard_map/ppermute | solution.py:427
  47.8 1.3 %collective-permute-done.other_ref = bf16[136,128]{1,0:T(8,128)(2,1)S(1)} collective-permute-done((bf16[136,128]{1,0:T(8,128)(2,1)S(1)}, bf16[136,128]{1,0:T(8,128)(2,1)S(1)}, u32[]{:S(2)}, u32[]{:S(2)}) %collective-permute-start) | collective-permute-done | bytes 34848 | tf_op jit(solution)/shard_map/ppermute | solution.py:427
  49.2 4.6 %collective-permute-start.1 = (bf16[136,128]{1,0:T(8,128)(2,1)S(1)}, bf16[136,128]{1,0:T(8,128)(2,1)S(1)}, u32[]{:S(2)}, u32[]{:S(2)}) collective-permute-start(bf16[136,128]{1,0:T(8,128)(2,1)S(1)} %pair.1), channel_id=1, source_target_pairs={{0,192},{16,208},{32,224},{48,240},{64,128},{80,144},{96,160},{112... | collective-permute-start | bytes 104456 | tf_op jit(solution)/shard_map/ppermute | solution.py:427
  53.8 1.3 %collective-permute-done.1.pair_ref = bf16[136,128]{1,0:T(8,128)(2,1)S(1)} collective-permute-done((bf16[136,128]{1,0:T(8,128)(2,1)S(1)}, bf16[136,128]{1,0:T(8,128)(2,1)S(1)}, u32[]{:S(2)}, u32[]{:S(2)}) %collective-permute-start.1) | collective-permute-done | bytes 34848 | tf_op jit(solution)/shard_map/ppermute | solution.py:427
  55.1 1.4 %held.1 = bf16[64,128,128]{2,1,0:T(8,128)(2,1)} custom-call(s32[1]{0:T(128)} %bitcast.1.place_ref, bf16[136,128]{1,0:T(8,128)(2,1)S(1)} %collective-permute-done.other_ref, bf16[136,128]{1,0:T(8,128)(2,1)S(1)} %collective-permute-done.1.pair_ref, bf16[64,136,128]{2,1,0:T(8,128)(2,1)S(1)} %all-to-all-done.in_ref), custom_call_target="tpu_custom_call" | custom-call | flops 4000000 | bytes 4000000 | tf_op jit(solution)/shard_map/held/pallas_call | solution.py:232
  56.6 8.9 %all-to-all-start.1 = ((bf16[64,128,128]{2,1,0:T(8,128)(2,1)}), bf16[64,128,128]{2,1,0:T(8,128)(2,1)S(1)}, u32[]{:S(2)}, u32[]{:S(2)}) async-start(bf16[64,128,128]{2,1,0:T(8,128)(2,1)} %held.1), calls=%async_computation.1 | async-start | bytes 4194304 | tf_op jit(solution)/shard_map/all_to_all | solution.py:431
  65.4 0.0 copy-start
  65.4 0.0 copy-start.1
  65.5 6.8 %local1.1.local_hbm = bf16[256,8192]{1,0:T(8,128)(2,1)} custom-call(bf16[256,8192]{1,0:T(8,128)(2,1)} %x_hbm.5, f32[256,128]{1,0:T(8,128)} %step_hbm.5, f32[256,128]{1,0:T(8,128)} %decay_hbm.5, bf16[256,1024]{1,0:T(8,128)(2,1)} %inject_hbm.5, bf16[256,1024]{1,0:T(8,128)(2,1)} %readout_ref.1, f32[1,128]{1,0:T(1,128)} %bitcast.3, ...), custom_call_target="tpu_custom_call", output_to_operand_aliasing={{}: (6, {})} | custom-call | flops 2000000000 | bytes 6000000 | tf_op jit(solution)/shard_map/local1/pallas_call | solution.py:340
  72.2 20.4 %all-to-all-done.1.held_ref = bf16[64,128,128]{2,1,0:T(8,128)(2,1)S(1)} async-done(((bf16[64,128,128]{2,1,0:T(8,128)(2,1)}), bf16[64,128,128]{2,1,0:T(8,128)(2,1)S(1)}, u32[]{:S(2)}, u32[]{:S(2)}) %all-to-all-start.1) | async-done | bytes 2097184 | tf_op jit(solution)/shard_map/all_to_all | solution.py:431
  92.6 0.0 copy-done
  92.6 0.0 copy-done.1
  92.6 4.1 %outputs.1 = bf16[256,8192]{1,0:T(8,128)(2,1)} custom-call(f32[256,128]{1,0:T(8,128)S(1)} %copy-done.1, bf16[256,1024]{1,0:T(8,128)(2,1)S(1)} %copy-done, bf16[64,128,128]{2,1,0:T(8,128)(2,1)S(1)} %all-to-all-done.1.held_ref, bf16[256,8192]{1,0:T(8,128)(2,1)} %local1.1.local_hbm), custom_call_target="tpu_custom_call" | custom-call | flops 2000000000 | bytes 12000000 | tf_op jit(solution)/shard_map/outputs/pallas_call | solution.py:406
  (1 shorter events, 0.0 us)
Async XLA Ops:
  5.2 39.1 %all-to-all-start = ((bf16[64,136,128]{2,1,0:T(8,128)(2,1)}), bf16[64,136,128]{2,1,0:T(8,128)(2,1)S(1)}, u32[]{:S(2)}, u32[]{:S(2)}) async-start(bf16[64,136,128]{2,1,0:T(8,128)(2,1)} %states.1), calls=%async_computation | async-start | bytes 4456448 | tf_op jit(solution)/shard_map/all_to_all | solution.py:431
  44.7 4.4 %collective-permute-start = (bf16[136,128]{1,0:T(8,128)(2,1)S(1)}, bf16[136,128]{1,0:T(8,128)(2,1)S(1)}, u32[]{:S(2)}, u32[]{:S(2)}) collective-permute-start(bf16[136,128]{1,0:T(8,128)(2,1)S(1)} %total.1.own_ref), channel_id=1, source_target_pairs={{0,64},{16,80},{32,96},{48,112},{64,0},{80,16},{96,32},{112,48},{1... | collective-permute-start | bytes 104456 | tf_op jit(solution)/shard_map/ppermute | solution.py:427
  49.2 5.9 %collective-permute-start.1 = (bf16[136,128]{1,0:T(8,128)(2,1)S(1)}, bf16[136,128]{1,0:T(8,128)(2,1)S(1)}, u32[]{:S(2)}, u32[]{:S(2)}) collective-permute-start(bf16[136,128]{1,0:T(8,128)(2,1)S(1)} %pair.1), channel_id=1, source_target_pairs={{0,192},{16,208},{32,224},{48,240},{64,128},{80,144},{96,160},{112... | collective-permute-start | bytes 104456 | tf_op jit(solution)/shard_map/ppermute | solution.py:427
  56.6 36.1 %all-to-all-start.1 = ((bf16[64,128,128]{2,1,0:T(8,128)(2,1)}), bf16[64,128,128]{2,1,0:T(8,128)(2,1)S(1)}, u32[]{:S(2)}, u32[]{:S(2)}) async-start(bf16[64,128,128]{2,1,0:T(8,128)(2,1)} %held.1), calls=%async_computation.1 | async-start | bytes 4194304 | tf_op jit(solution)/shard_map/all_to_all | solution.py:431
  65.4 27.2 %copy-start = (bf16[256,1024]{1,0:T(8,128)(2,1)S(1)}, bf16[256,1024]{1,0:T(8,128)(2,1)}, u32[]{:S(2)}) copy-start(bf16[256,1024]{1,0:T(8,128)(2,1)} %readout_ref.1) | copy-start | bytes 1572868
  65.4 27.2 %copy-start.1 = (f32[256,128]{1,0:T(8,128)S(1)}, f32[256,128]{1,0:T(8,128)}, u32[]{:S(2)}) copy-start(f32[256,128]{1,0:T(8,128)} %get-tuple-element.12.lead_ref) | copy-start | bytes 393220
